TPU v7x, 32 devices: a whole 2x2x4 slice. The times are simulated.
32 devices in a mesh: ha: 4 (over y, core), wa: 2 (over x), ta: 4 (over z).
Axes of the slice: x: 2, y: 2, z: 4, core: 2. Of those that a mesh axis runs over, the one named last changes fastest.
Arguments:
- video: bfloat16 [16, 96, 64, 256], P('ta', 'ha', 'wa'), may hold values from -210 to 210
- norm_gain: float32 [256], replicated, may hold values from 0.1 to 1.9
- norm_bias: float32 [256], replicated, may hold values from -3 to 3
- spatial_weight: bfloat16 [3, 3, 256, 256], replicated, may hold values from -0.125 to 0.125
- spatial_bias: float32 [256], replicated, may hold values from -3 to 3
- temporal_weight: bfloat16 [3, 256, 256], replicated, may hold values from -0.21875 to 0.21875
- temporal_bias: float32 [256], replicated, may hold values from -3 to 3
Outputs:
- encoded: bfloat16 [16, 96, 64, 256], P('ta', 'ha', 'wa')
All inputs are finite; a program needn't handle non-finite values.
Results may differ from a plain program's by a relative error of at most 0.0054.
Values may be sent and summed in bfloat16 or wider, within the bound.
No kernel may reach another device: no remote copies, remote signals or barrier semaphores. Data moves between devices by JAX's collectives and lax.ppermute only.
A program may use at most 64 MiB of HBM per device.

v0:
```python
import jax
import jax.numpy as jnp
from jax import lax
from jax.sharding import PartitionSpec as P

G = 32


def with_halo(cells, sides, width):
    for axis, dim in sides:
        count = lax.axis_size(axis)
        ends = count - 1
        head = lax.slice_in_dim(cells, 0, width, axis=dim)
        tail = lax.slice_in_dim(cells, cells.shape[dim] - width, cells.shape[dim], axis=dim)
        cells = jnp.concatenate(
            [
                lax.ppermute(tail, axis, [(i, (i + 1) % count) for i in range(ends)]),
                cells,
                lax.ppermute(head, axis, [((i + 1) % count, i) for i in range(ends)]),
            ],
            axis=dim,
        )
    return cells


def shifted(value, axis, steps):
    count = lax.axis_size(axis)
    leading, last = (max(0, -steps), min(count, count - steps))
    return lax.ppermute(value, axis, [(source, source + steps) for source in range(leading, last)])


def convolve(block, spatial_weight, spatial_bias, rows, cols):
    total = jnp.zeros((block.shape[0], rows, cols, spatial_weight.shape[3]), jnp.float32)
    for dy in range(3):
        for dx in range(3):
            total = total + jnp.einsum(
                "fhwc,cd->fhwd",
                block[:, dy : dy + rows, dx : dx + cols],
                spatial_weight[dy, dx],
                preferred_element_type=jnp.float32,
            )
    return (total + spatial_bias).astype(jnp.bfloat16)


def local(
    video, norm_gain, norm_bias, spatial_weight, spatial_bias, temporal_weight, temporal_bias
):
    frames, rows, cols, chans = video.shape
    width = chans // G
    x_values = video.astype(jnp.float32).reshape(frames, rows, cols, G, width)
    count = float(rows * cols * width * lax.axis_size("ha") * lax.axis_size("wa"))
    totals = lax.psum(jnp.sum(x_values, axis=(1, 2, 4)), ("ha", "wa"))
    mean = totals / count
    centered = x_values - mean[:, None, None, :, None]
    spread = lax.psum(jnp.sum(centered * centered, axis=(1, 2, 4)), ("ha", "wa"))
    var = spread / count
    scaled = centered * lax.rsqrt(var + 1e-06)[:, None, None, :, None]
    scaled = scaled.reshape(frames, rows, cols, chans) * norm_gain + norm_bias
    act = jax.nn.silu(scaled).astype(jnp.bfloat16)
    padded = with_halo(act, (("ha", 1), ("wa", 2)), 1)
    spatial = convolve(padded, spatial_weight, spatial_bias, rows, cols)
    earlier = shifted(spatial[frames - 2 :], "ta", 1)
    leading = jnp.concatenate([spatial[:1], spatial[:1]], axis=0)
    earlier = jnp.where(lax.axis_index("ta") == 0, leading, earlier)
    extended = jnp.concatenate([earlier, spatial], axis=0)
    total = jnp.zeros((frames, rows, cols, temporal_weight.shape[2]), jnp.float32)
    for tap in range(3):
        total = total + jnp.einsum(
            "fhwc,cd->fhwd",
            extended[2 - tap : 2 - tap + frames],
            temporal_weight[tap],
            preferred_element_type=jnp.float32,
        )
    return (total + temporal_bias).astype(jnp.bfloat16)


def solution(mesh):
    placed = (P("ta", "ha", "wa", None), P(), P(), P(), P(), P(), P())
    return jax.shard_map(
        local, mesh=mesh, in_specs=placed, out_specs=P("ta", "ha", "wa", None), check_vma=False
    )
```

profile of v0, /device:TPU:16, one launch (start us, length us, event | category | flops | bytes accessed | tf_op | source)
XLA Modules:
  0.0 82.5 jit_solution(10046666974749645342)
XLA Ops:
  0.0 1.8 %convert_reduce_fusion = f32[4,256]{1,0:T(4,128)S(1)} fusion(bf16[4,24,32,256]{3,2,1,0:T(8,128)(2,1)} %param.7), kind=kLoop, calls=%fused_computation.1 | loop fusion | flops 1571840 | bytes 1576960 | tf_op jit(solution)/shard_map/reduce_sum | solution.py:52
  1.9 0.1 reduce_sum.25
  2.0 13.8 %psum.14 = f32[4,32]{1,0:T(4,128)S(1)} all-reduce(f32[4,32]{1,0:T(4,128)S(1)} %reduce_sum.25), channel_id=1, replica_groups=mesh['ha'=4,'wa'=2,'ta'=4] {'ha','wa'}, use_global_device_ids=true, to_apply=%region_2.0 | all-reduce | flops 128 | bytes 1024 | tf_op jit(solution)/shard_map/psum | solution.py:52
  15.9 0.1 sub.15
  16.0 0.4 fusion.2
  16.5 0.1 reduce_sum.37
  16.6 12.3 %psum.15 = f32[4,32]{1,0:T(4,128)S(1)} all-reduce(f32[4,32]{1,0:T(4,128)S(1)} %reduce_sum.37), channel_id=1, replica_groups=mesh['ha'=4,'wa'=2,'ta'=4] {'ha','wa'}, use_global_device_ids=true, to_apply=%region_5.6 | all-reduce | flops 128 | bytes 1024 | tf_op jit(solution)/shard_map/psum | solution.py:55
  29.0 0.1 mul.31
  29.1 1.1 %fusion.10 = bf16[4,24,32,256]{3,2,1,0:T(8,128)(2,1)S(1)} fusion(bf16[4,24,32,256]{3,2,1,0:T(8,128)(2,1)S(1)} %copy-done, f32[256]{0:T(256)S(1)} %copy-done.3, f32[256]{0:T(256)S(1)} %copy-done.4, f32[4,256]{1,0:T(4,128)S(1)} %mul.31, f32[4,256]{1,0:T(4,128)S(1)} %sub.15), kind=kLoop, calls=%fused_computation.12 | loop fusion | flops 7864320 | bytes 3155968 | tf_op jit(solution)/shard_map/convert_element_type | solution.py:59
  30.2 1.9 %collective-permute-start = (bf16[4,1,32,256]{3,2,1,0:T(8,128)(2,1)S(1)}, bf16[4,1,32,256]{3,2,1,0:T(8,128)(2,1)S(1)}, u32[]{:S(2)}, u32[]{:S(2)}) collective-permute-start(bf16[4,1,32,256]{3,2,1,0:T(8,128)(2,1)S(1)} %get-tuple-element.9), channel_id=1, source_target_pairs={{0,8},{8,16},{16,24},{1,9},{9,17},{17,25},{2,10},{10,18},{18,26},{... | collective-permute-start | bytes 196616 | tf_op jit(solution)/shard_map/ppermute | solution.py:17
  32.2 1.3 %collective-permute-start.1 = (bf16[4,1,32,256]{3,2,1,0:T(8,128)(2,1)S(1)}, bf16[4,1,32,256]{3,2,1,0:T(8,128)(2,1)S(1)}, u32[]{:S(2)}, u32[]{:S(2)}) collective-permute-start(bf16[4,1,32,256]{3,2,1,0:T(8,128)(2,1)S(1)} %get-tuple-element.10), channel_id=1, source_target_pairs={{8,0},{16,8},{24,16},{9,1},{17,9},{25,17},{10,2},{18,10},{26,18},{... | collective-permute-start | bytes 196616 | tf_op jit(solution)/shard_map/ppermute | solution.py:19
  33.5 0.6 fusion.42
  34.1 2.4 %collective-permute-done.1 = bf16[4,1,32,256]{3,2,1,0:T(8,128)(2,1)S(1)} collective-permute-done((bf16[4,1,32,256]{3,2,1,0:T(8,128)(2,1)S(1)}, bf16[4,1,32,256]{3,2,1,0:T(8,128)(2,1)S(1)}, u32[]{:S(2)}, u32[]{:S(2)}) %collective-permute-start.1) | collective-permute-done | bytes 65568 | tf_op jit(solution)/shard_map/ppermute | solution.py:19
  36.4 0.2 pad_maximum_fusion.4
  36.6 3.4 %collective-permute-start.2 = (bf16[4,26,1,256]{3,2,1,0:T(2,128)(2,1)S(1)}, bf16[4,26,1,256]{3,2,1,0:T(2,128)(2,1)S(1)}, u32[]{:S(2)}, u32[]{:S(2)}) collective-permute-start(bf16[4,26,1,256]{3,2,1,0:T(2,128)(2,1)S(1)} %get-tuple-element.8), channel_id=1, source_target_pairs={{0,4},{1,5},{2,6},{3,7},{8,12},{9,13},{10,14},{11,15},{16,20},{17,... | collective-permute-start | bytes 159752 | tf_op jit(solution)/shard_map/ppermute | solution.py:17
  40.1 1.3 %collective-permute-start.3 = (bf16[4,26,1,256]{3,2,1,0:T(2,128)(2,1)S(1)}, bf16[4,26,1,256]{3,2,1,0:T(2,128)(2,1)S(1)}, u32[]{:S(2)}, u32[]{:S(2)}) collective-permute-start(bf16[4,26,1,256]{3,2,1,0:T(2,128)(2,1)S(1)} %get-tuple-element.7), channel_id=1, source_target_pairs={{4,0},{5,1},{6,2},{7,3},{12,8},{13,9},{14,10},{15,11},{20,16},{21,... | collective-permute-start | bytes 159752 | tf_op jit(solution)/shard_map/ppermute | solution.py:19
  41.4 2.3 %fusion.11 = f32[4,24,32,256]{3,2,1,0:T(8,128)} fusion(bf16[4,24,32,256]{3,2,1,0:T(8,128)(2,1)S(1)} %fusion.10, bf16[4,1,32,256]{3,2,1,0:T(8,128)(2,1)S(1)} %collective-permute-done, bf16[3,3,256,256]{3,2,1,0:T(8,128)(2,1)S(1)} %copy-done.1), kind=kOutput, calls=%fused_computation.18 | convolution fusion | flops 405929984 | bytes 4915200 | tf_op jit(solution)/shard_map/fhwc,cd->fhwd/dot_general | solution.py:36
  43.6 2.2 %fusion.15 = f32[4,24,32,256]{3,2,1,0:T(8,128)} fusion(bf16[4,1,32,256]{3,2,1,0:T(8,128)(2,1)S(1)} %collective-permute-done.1, bf16[4,24,32,256]{3,2,1,0:T(8,128)(2,1)S(1)} %fusion.10, bf16[3,3,256,256]{3,2,1,0:T(8,128)(2,1)S(1)} %copy-done.1), kind=kOutput, calls=%fused_computation.22 | convolution fusion | flops 405929984 | bytes 4915200 | tf_op jit(solution)/shard_map/fhwc,cd->fhwd/dot_general | solution.py:36
  45.9 0.8 collective-permute-done.3
  46.7 1.3 %pad_maximum_fusion.1 = (bf16[4,26,33,256]{3,2,1,0:T(8,128)(2,1)S(1)}, bf16[4,26,33,256]{3,2,1,0:T(8,128)(2,1)S(1)}) fusion(bf16[4,26,1,256]{3,2,1,0:T(2,128)(2,1)S(1)} %collective-permute-done.3, bf16[4,1,32,256]{3,2,1,0:T(8,128)(2,1)S(1)} %collective-permute-done.1, bf16[4,24,32,256]{3,2,1,0:T(8,128)(2,1)S(1)} %fusion.10, ...), kind=kLoop, calls=%fused_computation.17 | loop fusion | flops 14057472 | bytes 5324800 | tf_op jit(solution)/shard_map/concatenate | solution.py:15
  48.0 0.6 fusion.23
  48.5 0.6 fusion.27
  49.1 0.6 fusion.25
  49.7 0.6 fusion.29
  50.3 2.3 %fusion.31 = f32[4,24,32,256]{3,2,1,0:T(8,128)} fusion(bf16[4,26,33,256]{3,2,1,0:T(8,128)(2,1)S(1)} %get-tuple-element.6, bf16[3,3,256,256]{3,2,1,0:T(8,128)(2,1)S(1)} %copy-done.1), kind=kOutput, calls=%fused_computation.36 | convolution fusion | flops 402653184 | bytes 4849664 | tf_op jit(solution)/shard_map/fhwc,cd->fhwd/dot_general | solution.py:36
  52.6 5.7 %add_convert_fusion.1 = bf16[4,24,32,256]{3,2,1,0:T(8,128)(2,1)S(1)} fusion(f32[4,24,32,256]{3,2,1,0:T(8,128)} %fusion.15, f32[4,24,32,256]{3,2,1,0:T(8,128)S(1)} %fusion.23, f32[4,24,32,256]{3,2,1,0:T(8,128)S(1)} %fusion.25, f32[4,24,32,256]{3,2,1,0:T(8,128)S(1)} %fusion.42, f32[4,24,32,256]{3,2,1,0:T(8,128)S(1)} %fusion.27, ...), kind=kOutput, calls=%fused_computation.14 | convolution fusion | flops 410517504 | bytes 28443648 | tf_op jit(solution)/shard_map/fhwc,cd->fhwd/dot_general | solution.py:36
  58.4 3.6 %collective-permute-start.4 = (bf16[2,24,32,256]{3,2,1,0:T(8,128)(2,1)S(1)}, bf16[2,24,32,256]{3,2,1,0:T(8,128)(2,1)S(1)}, u32[]{:S(2)}, u32[]{:S(2)}) collective-permute-start(bf16[2,24,32,256]{3,2,1,0:T(8,128)(2,1)S(1)} %slice.130), channel_id=1, source_target_pairs={{0,1},{1,2},{2,3},{4,5},{5,6},{6,7},{8,9},{9,10},{10,11},{12,13},{... | collective-permute-start | bytes 2359304 | tf_op jit(solution)/shard_map/ppermute | solution.py:29
  62.1 0.6 fusion.36
  62.7 17.3 %collective-permute-done.4 = bf16[2,24,32,256]{3,2,1,0:T(8,128)(2,1)S(1)} collective-permute-done((bf16[2,24,32,256]{3,2,1,0:T(8,128)(2,1)S(1)}, bf16[2,24,32,256]{3,2,1,0:T(8,128)(2,1)S(1)}, u32[]{:S(2)}, u32[]{:S(2)}) %collective-permute-start.4) | collective-permute-done | bytes 786464 | tf_op jit(solution)/shard_map/ppermute | solution.py:29
  79.9 0.1 maximum_select_fusion
  80.0 0.6 fusion.33
  80.7 1.8 %add_convert_fusion = bf16[4,24,32,256]{3,2,1,0:T(8,128)(2,1)} fusion(f32[4,24,32,256]{3,2,1,0:T(8,128)S(1)} %fusion.36, f32[4,24,32,256]{3,2,1,0:T(8,128)S(1)} %fusion.33, f32[256]{0:T(256)S(1)} %copy-done.6, bf16[4,24,32,256]{3,2,1,0:T(8,128)(2,1)S(1)} %add_convert_fusion.1, bf16[2,24,32,256]{3,2,1,0:T(8,128)(2,1)S(1)} %maximum_select_fusion, ...), kind=kOutput, calls=%fused_computation.13 | convolution fusion | flops 410517504 | bytes 10355712 | tf_op jit(solution)/shard_map/fhwc,cd->fhwd/dot_general | solution.py:68
  (25 shorter events, 0.6 us)
Async XLA Ops:
  0.0 16.0 %copy-start = (bf16[4,24,32,256]{3,2,1,0:T(8,128)(2,1)S(1)}, bf16[4,24,32,256]{3,2,1,0:T(8,128)(2,1)}, u32[]{:S(2)}) copy-start(bf16[4,24,32,256]{3,2,1,0:T(8,128)(2,1)} %param.7) | copy-start | bytes 4718596
  0.0 29.1 %copy-start.4 = (f32[256]{0:T(256)S(1)}, f32[256]{0:T(256)}, u32[]{:S(2)}) copy-start(f32[256]{0:T(256)} %param.8) | copy-start | bytes 3076
  0.0 29.1 %copy-start.3 = (f32[256]{0:T(256)S(1)}, f32[256]{0:T(256)}, u32[]{:S(2)}) copy-start(f32[256]{0:T(256)} %param.9) | copy-start | bytes 3076
  16.0 17.5 %copy-start.1 = (bf16[3,3,256,256]{3,2,1,0:T(8,128)(2,1)S(1)}, bf16[3,3,256,256]{3,2,1,0:T(8,128)(2,1)}, u32[]{:S(2)}) copy-start(bf16[3,3,256,256]{3,2,1,0:T(8,128)(2,1)} %param.10) | copy-start | bytes 3538948
  30.2 3.8 %collective-permute-start = (bf16[4,1,32,256]{3,2,1,0:T(8,128)(2,1)S(1)}, bf16[4,1,32,256]{3,2,1,0:T(8,128)(2,1)S(1)}, u32[]{:S(2)}, u32[]{:S(2)}) collective-permute-start(bf16[4,1,32,256]{3,2,1,0:T(8,128)(2,1)S(1)} %get-tuple-element.9), channel_id=1, source_target_pairs={{0,8},{8,16},{16,24},{1,9},{9,17},{17,25},{2,10},{10,18},{18,26},{... | collective-permute-start | bytes 196616 | tf_op jit(solution)/shard_map/ppermute | solution.py:17
  32.2 4.3 %collective-permute-start.1 = (bf16[4,1,32,256]{3,2,1,0:T(8,128)(2,1)S(1)}, bf16[4,1,32,256]{3,2,1,0:T(8,128)(2,1)S(1)}, u32[]{:S(2)}, u32[]{:S(2)}) collective-permute-start(bf16[4,1,32,256]{3,2,1,0:T(8,128)(2,1)S(1)} %get-tuple-element.10), channel_id=1, source_target_pairs={{8,0},{16,8},{24,16},{9,1},{17,9},{25,17},{10,2},{18,10},{26,18},{... | collective-permute-start | bytes 196616 | tf_op jit(solution)/shard_map/ppermute | solution.py:19
  36.6 9.3 %collective-permute-start.2 = (bf16[4,26,1,256]{3,2,1,0:T(2,128)(2,1)S(1)}, bf16[4,26,1,256]{3,2,1,0:T(2,128)(2,1)S(1)}, u32[]{:S(2)}, u32[]{:S(2)}) collective-permute-start(bf16[4,26,1,256]{3,2,1,0:T(2,128)(2,1)S(1)} %get-tuple-element.8), channel_id=1, source_target_pairs={{0,4},{1,5},{2,6},{3,7},{8,12},{9,13},{10,14},{11,15},{16,20},{17,... | collective-permute-start | bytes 159752 | tf_op jit(solution)/shard_map/ppermute | solution.py:17
  40.1 6.6 %collective-permute-start.3 = (bf16[4,26,1,256]{3,2,1,0:T(2,128)(2,1)S(1)}, bf16[4,26,1,256]{3,2,1,0:T(2,128)(2,1)S(1)}, u32[]{:S(2)}, u32[]{:S(2)}) collective-permute-start(bf16[4,26,1,256]{3,2,1,0:T(2,128)(2,1)S(1)} %get-tuple-element.7), channel_id=1, source_target_pairs={{4,0},{5,1},{6,2},{7,3},{12,8},{13,9},{14,10},{15,11},{20,16},{21,... | collective-permute-start | bytes 159752 | tf_op jit(solution)/shard_map/ppermute | solution.py:19
  50.3 2.3 %copy-start.5 = (f32[256]{0:T(256)S(1)}, f32[256]{0:T(256)}, u32[]{:S(2)}) copy-start(f32[256]{0:T(256)} %param.11) | copy-start | bytes 3076
  58.3 3.8 %copy-start.2 = (bf16[3,256,256]{2,1,0:T(8,128)(2,1)S(1)}, bf16[3,256,256]{2,1,0:T(8,128)(2,1)}, u32[]{:S(2)}) copy-start(bf16[3,256,256]{2,1,0:T(8,128)(2,1)} %param.12) | copy-start | bytes 1179652
  58.4 21.5 %collective-permute-start.4 = (bf16[2,24,32,256]{3,2,1,0:T(8,128)(2,1)S(1)}, bf16[2,24,32,256]{3,2,1,0:T(8,128)(2,1)S(1)}, u32[]{:S(2)}, u32[]{:S(2)}) collective-permute-start(bf16[2,24,32,256]{3,2,1,0:T(8,128)(2,1)S(1)} %slice.130), channel_id=1, source_target_pairs={{0,1},{1,2},{2,3},{4,5},{5,6},{6,7},{8,9},{9,10},{10,11},{12,13},{... | collective-permute-start | bytes 2359304 | tf_op jit(solution)/shard_map/ppermute | solution.py:29
  80.0 0.7 copy-start.6
where the time goes:
time: 84 us; the launch traced here: 82.5 us
  blocking collectives  26.1 us (31%)
  waiting for transfers between devices  20.4 us (24%)
  matrix products  18.3 us (22%)
  starting transfers between devices  11.6 us (14%)
  other arithmetic  5.07 us (6%)
    ppermute x1, waiting for transfers between devices, shifted(): lax.ppermute(value, axis, [(source, source + steps) for source in range(l...  17.3 us
    dot_general x9, matrix products, convolve(): jnp.einsum('fhwc,cd->fhwd', block[:, dy:dy + rows, dx:dx + cols], spatial...  15.4 us
    psum x1, blocking collectives, local(): totals = lax.psum(jnp.sum(x_values, axis=(1, 2, 4)), ('ha', 'wa'))  13.8 us
    psum x1, blocking collectives, local(): lax.psum(jnp.sum(centered * centered, axis=(1, 2, 4)), ('ha', 'wa'))  12.3 us
    ppermute x2, starting transfers between devices, with_halo(): lax.ppermute(tail, axis, [(i, (i + 1) % count) for i in range(ends)])  5.39 us
    ppermute x1, starting transfers between devices, shifted(): lax.ppermute(value, axis, [(source, source + steps) for source in range(l...  3.63 us
    ppermute x2, waiting for transfers between devices, with_halo(): lax.ppermute(head, axis, [((i + 1) % count, i) for i in range(ends)])  3.15 us
    dot_general x3, matrix products, local(): jnp.einsum('fhwc,cd->fhwd', extended[2 - tap:2 - tap + frames], temporal_...  2.91 us
  transfers between devices with their start and end apart: 5, of which 3 were waited for; matrix products, arithmetic and copies ran while one was open for 7% of the time, Pallas kernels for 0%

commit v1 on v0

v1 whole, which is shorter than its diff:
```python
import functools

import jax
import jax.numpy as jnp
from jax import lax
from jax.experimental import pallas as pl
from jax.experimental.pallas import tpu as pltpu
from jax.sharding import PartitionSpec as P

G = 32
EPS = 1e-06
PREV = 2
F32 = jnp.float32
BF16 = jnp.bfloat16
VMEM = pl.BlockSpec(memory_space=pltpu.VMEM)
ANY = pl.BlockSpec(memory_space=pl.ANY)


def call(kernel, outs, out_specs=None, scratch=(), flops=0, name=None, **kw):
    nbytes = sum(o.size * o.dtype.itemsize for o in outs)
    return pl.pallas_call(
        kernel,
        out_shape=outs,
        out_specs=out_specs or [VMEM] * len(outs),
        scratch_shapes=list(scratch),
        compiler_params=pltpu.CompilerParams(vmem_limit_bytes=40 << 20),
        cost_estimate=pl.CostEstimate(flops=flops, bytes_accessed=nbytes, transcendentals=0),
        name=name,
        **kw,
    )


def pad_to(n, k):
    return (n + k - 1) // k * k


def split3(x):
    hi = x.astype(BF16)
    rest = x - hi.astype(F32)
    mid = rest.astype(BF16)
    low = (rest - mid.astype(F32)).astype(BF16)
    return hi, mid, low


def as_terms(x, rows):
    parts = jnp.concatenate([t.astype(F32) for t in split3(x)], axis=0)
    fill = rows - parts.shape[0]
    if fill:
        parts = jnp.concatenate([parts, jnp.zeros((fill, x.shape[1]), F32)], axis=0)
    return parts.astype(BF16)


def from_terms(t, rows):
    t = t.astype(F32)
    return t[:rows] + t[rows : 2 * rows] + t[2 * rows : 3 * rows]


class Sizes:
    def __init__(self, video, ha, wa):
        self.frames, self.rows, self.cols, self.chans = video.shape
        self.ha, self.wa = ha, wa
        self.ncol = 1 if wa == 2 else 2
        self.colrow = pad_to(self.rows + 2, 16)
        self.all = self.frames + PREV
        self.strip = 2 * self.cols + self.ncol * self.colrow
        self.local_stats = pad_to(3 * 2 * PREV, 16)
        self.stats = pad_to(3 * 2 * self.all, 16)


def local_kernel(s, video, stats, strips, zstrip, bulk):
    wa = lax.axis_index("wa")
    first = s.frames - PREV
    tail_m, tail_q = [], []
    for f in range(s.frames):
        total = jnp.zeros((s.cols, s.chans), F32)
        for r in range(s.rows):
            total = total + video[f, r].astype(F32)
        mean = jnp.sum(total, axis=0, keepdims=True) * (1.0 / (s.rows * s.cols))
        spread = jnp.zeros((s.cols, s.chans), F32)
        left, right = [], []
        for r in range(s.rows):
            x = video[f, r].astype(F32)
            left.append(x[:1])
            right.append(x[s.cols - 1 :])
            x = x - mean
            spread = spread + x * x
        square = jnp.sum(spread, axis=0, keepdims=True)
        stats[f : f + 1] = mean
        stats[s.frames + f : s.frames + f + 1] = square
        fill = [jnp.zeros((s.colrow - s.rows, s.chans), F32)]
        left = jnp.concatenate(left + fill, axis=0)
        right = jnp.concatenate(right + fill, axis=0)
        if s.ncol == 1:
            edges = [jnp.where(wa == 0, right, left).astype(BF16)]
        else:
            edges = [left.astype(BF16), right.astype(BF16)]
        for ref, at, use in ((strips, f, True), (zstrip, f - first, f >= first)):
            if not use:
                continue
            o = at * s.strip
            ref[o : o + s.cols] = video[f, 0]
            ref[o + s.cols : o + 2 * s.cols] = video[f, s.rows - 1]
            for k, e in enumerate(edges):
                o2 = o + 2 * s.cols + k * s.colrow
                ref[o2 : o2 + s.colrow] = e
        if f >= first:
            bulk[f - first] = video[f, 1 : s.rows - 1]
            tail_m.append(mean)
            tail_q.append(square)
    o = PREV * s.strip
    zstrip[o : o + s.local_stats] = as_terms(jnp.concatenate(tail_m + tail_q, axis=0), s.local_stats)


def strip_of(s, strips, zrecv, f):
    if f < s.frames:
        return strips, f * s.strip
    return zrecv, (f - s.frames) * s.strip


def rows_kernel(s, stats, strips, zrecv, pay1, pay2, payt):
    ha = lax.axis_index("ha")
    even = lax.rem(ha, 2) == 0
    for f in range(s.all):
        ref, o = strip_of(s, strips, zrecv, f)
        top = ref[o : o + s.cols].astype(F32)
        bottom = ref[o + s.cols : o + 2 * s.cols].astype(F32)
        pay1[f * s.cols : (f + 1) * s.cols] = jnp.where(even, bottom, top).astype(BF16)
        pay2[f * s.cols : (f + 1) * s.cols] = jnp.where(even, top, bottom).astype(BF16)
    o = PREV * s.strip
    prev = from_terms(zrecv[o : o + s.local_stats], 2 * PREV)
    own = stats[...]
    both = jnp.concatenate([own[: s.frames], prev[:PREV], own[s.frames :], prev[PREV:]], axis=0)
    terms = as_terms(both, s.stats)
    o = s.all * s.cols
    pay1[o : o + s.stats] = terms
    pay2[o : o + s.stats] = terms
    payt[...] = terms


def merge(n, parts):
    half = parts[0].shape[0] // 2
    mean = sum(p[:half] for p in parts) * (1.0 / len(parts))
    square = sum(p[half:] + n * (p[:half] - mean) * (p[:half] - mean) for p in parts)
    return jnp.concatenate([mean, square], axis=0)


def cols_kernel(s, strips, zrecv, terms, got1, got2, gott, halo, payc, part):
    ha, wa = lax.axis_index("ha"), lax.axis_index("wa")
    even = lax.rem(ha, 2) == 0
    at = lax.broadcasted_iota(jnp.int32, (s.colrow, s.chans), 0)
    for f in range(s.all):
        one = got1[f * s.cols : (f + 1) * s.cols].astype(F32)
        two = got2[f * s.cols : (f + 1) * s.cols].astype(F32)
        top = jnp.where(even, two, one)
        bottom = jnp.where(even, one, two)
        halo[f, 0] = top.astype(BF16)
        halo[f, 1] = bottom.astype(BF16)
        ref, o = strip_of(s, strips, zrecv, f)
        for k in range(s.ncol):
            o2 = o + 2 * s.cols + k * s.colrow
            edge = ref[o2 : o2 + s.colrow].astype(F32)
            right = wa == 0 if s.ncol == 1 else k == 1
            tcell = jnp.where(right, top[s.cols - 1 :], top[:1])
            bcell = jnp.where(right, bottom[s.cols - 1 :], bottom[:1])
            edge = jnp.where(at == s.rows, tcell, edge)
            edge = jnp.where(at == s.rows + 1, bcell, edge)
            o3 = (f * s.ncol + k) * s.colrow
            payc[o3 : o3 + s.colrow] = edge.astype(BF16)
    if gott is not None:
        o = s.all * s.cols
        rows = 2 * s.all
        parts = [from_terms(terms[...], rows)]
        parts += [from_terms(g[o : o + s.stats], rows) for g in (got1, got2)]
        parts += [from_terms(gott[...], rows)]
        merged = merge(float(s.rows * s.cols), parts)
        part[...] = merged
        o = s.all * s.ncol * s.colrow
        payc[o : o + s.stats] = as_terms(merged, s.stats)


def activation(x, mean, scale, shift):
    h = (x - mean) * scale + shift
    return h + h * jnp.tanh(h)


def fill_taps(s, taps, raw_row, edges, mean, scale, shift):
    ha, wa = lax.axis_index("ha"), lax.axis_index("wa")
    top_in = jnp.where(ha > 0, 1.0, 0.0).astype(F32)
    bottom_in = jnp.where(ha < s.ha - 1, 1.0, 0.0).astype(F32)
    left_in = jnp.where(wa > 0, 1.0, 0.0).astype(F32)
    right_in = jnp.where(wa < s.wa - 1, 1.0, 0.0).astype(F32)
    acts = [activation(e.astype(F32), mean, scale, shift) for e in edges]
    left, right = acts[0] * left_in, acts[-1] * right_in
    at = lax.broadcasted_iota(jnp.int32, (s.cols, s.chans), 0)
    for i in range(s.rows + 2):
        act = activation(raw_row(i).astype(F32), mean, scale, shift)
        j = s.rows if i == 0 else s.rows + 1 if i == s.rows + 1 else i - 1
        lcell, rcell = left[j : j + 1], right[j : j + 1]
        west = jnp.where(at == 0, lcell, pltpu.roll(act, 1, 0))
        east = jnp.where(at == s.cols - 1, rcell, pltpu.roll(act, s.cols - 1, 0))
        if i in (0, s.rows + 1):
            inside = top_in if i == 0 else bottom_in
            west, act, east = west * inside, act * inside, east * inside
        taps[0, i] = west.astype(BF16)
        taps[1, i] = act.astype(BF16)
        taps[2, i] = east.astype(BF16)


def spatial_dot(s, taps, weight, bias):
    lhs = jnp.concatenate(
        [
            taps[dx, dy : dy + s.rows].reshape(s.rows * s.cols, s.chans)
            for dy in range(3)
            for dx in range(3)
        ],
        axis=1,
    )
    return (jnp.dot(lhs, weight[...], preferred_element_type=F32) + bias[...]).astype(BF16)


def temporal_dot(s, frames, weight, bias):
    lhs = jnp.concatenate(frames, axis=1)
    out = jnp.dot(lhs, weight[...], preferred_element_type=F32) + bias[...]
    return out.astype(BF16).reshape(s.rows, s.cols, s.chans)


def edges_of(s, got, f):
    edges = []
    for k in range(s.ncol):
        o = (f * s.ncol + k) * s.colrow
        edges.append(got[k][pl.ds(f * s.colrow, s.colrow)] if s.ncol > 1 else got[0][pl.ds(o, s.colrow)])
    return edges


def own_kernel(s, nstat, video, halo, *refs):
    gotc = refs[: s.ncol]
    (part, gain, nbias, sw, sb, tw, tb, enc, lead, aff, taps, spatial, out, sem) = refs[s.ncol :]
    rows = 2 * s.all
    count = float(s.rows * s.cols * s.ha * s.wa)
    stat = part[...]
    if nstat == 2:
        o = s.all * s.colrow
        stat = merge(count / 2, [stat, from_terms(gotc[0][o : o + s.stats], rows)])
    width = s.chans // G
    a = lax.broadcasted_iota(jnp.int32, (s.chans, s.chans), 0) // width
    b = lax.broadcasted_iota(jnp.int32, (s.chans, s.chans), 1) // width
    group = jnp.where(a == b, 1.0, 0.0).astype(F32)
    tot = functools.partial(jnp.dot, precision=lax.Precision.HIGHEST, preferred_element_type=F32)
    m, q = stat[: s.all], stat[s.all :]
    mean = tot(m, group) * (1.0 / width)
    var = tot(q + count * (m - mean) * (m - mean), group) * (1.0 / (count * width))
    scale = lax.rsqrt(var + EPS) * gain[...] * 0.5
    shift = nbias[...] * 0.5
    aff[: s.all] = mean
    aff[s.all :] = scale
    ta = lax.axis_index("ta")

    def put(f):
        return pltpu.make_async_copy(out.at[f], enc.at[f], sem.at[f])

    def frame(f, _):
        def raw_row(i):
            if i == 0:
                return halo[f, 0]
            if i == s.rows + 1:
                return halo[f, 1]
            return video[f, i - 1]

        fill_taps(s, taps, raw_row, edges_of(s, gotc, f), aff[pl.ds(f, 1)], aff[pl.ds(s.all + f, 1)], shift)
        spatial[f] = spatial_dot(s, taps, sw, sb)
        return _

    lax.fori_loop(0, s.frames, frame, 0)
    for f in range(PREV, s.frames):
        out[f] = temporal_dot(s, [spatial[f - k] for k in range(3)], tw, tb)
        put(f).start()

    @pl.when(ta == 0)
    def _():
        for f in range(PREV):
            out[f] = temporal_dot(s, [spatial[max(f - k, 0)] for k in range(3)], tw, tb)
            put(f).start()
            put(f).wait()

    for f in range(PREV):
        lead[f] = spatial[f]
    for f in range(PREV, s.frames):
        put(f).wait()


def prev_kernel(s, bulk, zrecv, halo, *refs):
    gotc = refs[: s.ncol]
    (aff, nbias, sw, sb, tw, tb, lead, enc_in, enc, taps, spatial, out, sem) = refs[s.ncol :]
    ta = lax.axis_index("ta")
    shift = nbias[...] * 0.5

    @pl.when(ta > 0)
    def _():
        def frame(p, _):
            f = s.frames + p
            o = p * s.strip

            def raw_row(i):
                if i == 0:
                    return halo[f, 0]
                if i == s.rows + 1:
                    return halo[f, 1]
                if i == 1:
                    return zrecv[pl.ds(o, s.cols)]
                if i == s.rows:
                    return zrecv[pl.ds(o + s.cols, s.cols)]
                return bulk[p, i - 2]

            fill_taps(s, taps, raw_row, edges_of(s, gotc, f), aff[pl.ds(f, 1)], aff[pl.ds(s.all + f, 1)], shift)
            spatial[p] = spatial_dot(s, taps, sw, sb)
            return _

        lax.fori_loop(0, PREV, frame, 0)
        seq = [spatial[0], spatial[1], lead[0], lead[1]]
        copies = []
        for f in range(PREV):
            out[f] = temporal_dot(s, [seq[PREV + f - k] for k in range(3)], tw, tb)
            copies.append(pltpu.make_async_copy(out.at[f], enc.at[f], sem.at[f]))
            copies[-1].start()
        for c in copies:
            c.wait()


def mates(n, phase):
    pairs = [(i, i ^ 1) for i in range(n)]
    if phase == 0:
        return pairs
    return [(i, (((i + 1) % n) ^ 1) - 1 if ((i + 1) % n) ^ 1 else n - 1) for i in range(n)]


def local(video, norm_gain, norm_bias, spatial_weight, spatial_bias, temporal_weight, temporal_bias):
    nta, nha, nwa = (lax.axis_size(a) for a in ("ta", "ha", "wa"))
    s = Sizes(video, nha, nwa)
    c = s.chans
    sd = jax.ShapeDtypeStruct
    ring = [(i, (i + 1) % nta) for i in range(nta)]
    sw = spatial_weight.reshape(9 * c, c)
    tw = temporal_weight.reshape(3 * c, c)
    gain, nbias, sb, tb = (v.reshape(1, c) for v in (norm_gain, norm_bias, spatial_bias, temporal_bias))

    stats, strips, zstrip, bulk = call(
        functools.partial(local_kernel, s),
        [
            sd((2 * s.frames, c), F32),
            sd((s.frames * s.strip, c), BF16),
            sd((PREV * s.strip + s.local_stats, c), BF16),
            sd((PREV, s.rows - 2, s.cols, c), BF16),
        ],
        name="local",
        in_specs=[VMEM],
    )(video)
    zrecv = lax.ppermute(zstrip, "ta", ring)
    bulk = lax.ppermute(bulk, "ta", ring)

    fused = nha == 4 and nwa == 2
    rowpay = sd((s.all * s.cols + s.stats, c), BF16)
    pay1, pay2, terms = call(
        functools.partial(rows_kernel, s),
        [rowpay, rowpay, sd((s.stats, c), BF16)],
        name="rows",
        in_specs=[VMEM] * 3,
    )(stats, strips, zrecv)
    got1 = lax.ppermute(pay1, "ha", mates(nha, 0))
    got2 = lax.ppermute(pay2, "ha", mates(nha, 1))
    colrows = s.all * s.ncol * s.colrow + (s.stats if fused else 0)
    outs = [sd((s.all, 2, s.cols, c), BF16), sd((colrows, c), BF16)]
    if fused:
        gott = lax.ppermute(terms, "ha", [(i, i ^ 2) for i in range(nha)])
        halo, payc, part = call(
            functools.partial(cols_kernel, s),
            outs + [sd((2 * s.all, c), F32)],
            name="cols",
            in_specs=[VMEM] * 6,
        )(strips, zrecv, terms, got1, got2, gott)
        gotc = [lax.ppermute(payc, "wa", [(0, 1), (1, 0)])]
    else:
        def kernel(strips, zrecv, got1, got2, halo, payc):
            cols_kernel(s, strips, zrecv, None, got1, got2, None, halo, payc, None)

        halo, payc = call(kernel, outs, name="cols", in_specs=[VMEM] * 4)(strips, zrecv, got1, got2)
        rows = 2 * s.all
        both = from_terms(terms, rows)
        every = lax.all_gather(both, ("ha", "wa"))
        part = merge(float(s.rows * s.cols), [every[i] for i in range(nha * nwa)])
        if s.ncol == 1:
            gotc = [lax.ppermute(payc, "wa", [(0, 1), (1, 0)])]
        else:
            sides = payc.reshape(s.all, 2, s.colrow, c)
            up = [(i, (i + 1) % nwa) for i in range(nwa)]
            down = [((i + 1) % nwa, i) for i in range(nwa)]
            gotc = [
                lax.ppermute(sides[:, 1].reshape(-1, c), "wa", up),
                lax.ppermute(sides[:, 0].reshape(-1, c), "wa", down),
            ]
    flops = 2 * s.rows * s.cols * c * c
    frame = (s.rows * s.cols, c)
    taps = pltpu.VMEM((3, s.rows + 2, s.cols, c), BF16)
    enc, lead, aff = call(
        functools.partial(own_kernel, s, 2 if fused else 1),
        [sd(video.shape, BF16), sd((PREV,) + frame, BF16), sd((2 * s.all, c), F32)],
        out_specs=[ANY, VMEM, VMEM],
        scratch=[
            taps,
            pltpu.VMEM((s.frames,) + frame, BF16),
            pltpu.VMEM((s.frames, s.rows, s.cols, c), BF16),
            pltpu.SemaphoreType.DMA((s.frames,)),
        ],
        flops=flops * (9 * s.frames + 3 * (s.frames - PREV)),
        name="own",
        in_specs=[VMEM] * (9 + s.ncol),
    )(video, halo, *gotc, part, gain, nbias, sw, sb, tw, tb)
    (enc,) = call(
        functools.partial(prev_kernel, s),
        [sd(video.shape, BF16)],
        out_specs=[ANY],
        scratch=[
            taps,
            pltpu.VMEM((PREV,) + frame, BF16),
            pltpu.VMEM((PREV, s.rows, s.cols, c), BF16),
            pltpu.SemaphoreType.DMA((PREV,)),
        ],
        flops=flops * 12 * PREV,
        name="prev",
        in_specs=[VMEM] * (10 + s.ncol) + [ANY],
        input_output_aliases={10 + s.ncol: 0},
    )(bulk, zrecv, halo, *gotc, aff, nbias, sw, sb, tw, tb, lead, enc)
    return enc


def solution(mesh):
    placed = (P("ta", "ha", "wa", None), P(), P(), P(), P(), P(), P())
    return jax.shard_map(
        local, mesh=mesh, in_specs=placed, out_specs=P("ta", "ha", "wa", None), check_vma=False
    )
```

time: 84 us -> 33.7 us (0.40)
  the two profiles are of different devices: /device:TPU:16 before, /device:TPU:0 now
where the time goes in v1:
time: 33.7 us; the launch traced here: 33.5 us
  waiting for transfers between devices  11.7 us (35%)
  Pallas kernels  10.3 us (31%)
  starting transfers between devices  8.61 us (26%)
  local copies, waits for them, and re-layouts  2.7 us (8%)
    pallas_call x1, Pallas kernels, local(): call(functools.partial(own_kernel, s, 2 if fused else 1), [sd(video.shape...  9.31 us
    ppermute x1, waiting for transfers between devices, local(): zrecv = lax.ppermute(zstrip, 'ta', ring)  4.25 us
    ppermute x1, waiting for transfers between devices, local(): gott = lax.ppermute(terms, 'ha', [(i, i ^ 2) for i in range(nha)])  4.1 us
    ppermute x1, waiting for transfers between devices, local(): gotc = [lax.ppermute(payc, 'wa', [(0, 1), (1, 0)])]  3.39 us
    ppermute x1, starting transfers between devices, local(): zrecv = lax.ppermute(zstrip, 'ta', ring)  3.08 us
    unnamed x18, local copies, waits for them, and re-layouts  2.7 us
    ppermute x1, starting transfers between devices, local(): got2 = lax.ppermute(pay2, 'ha', mates(nha, 1))  1.85 us
    ppermute x1, starting transfers between devices, local(): gotc = [lax.ppermute(payc, 'wa', [(0, 1), (1, 0)])]  1.74 us
  transfers between devices with their start and end apart: 6, of which 3 were waited for; matrix products, arithmetic and copies ran while one was open for 0% of the time, Pallas kernels for 28%

profile of v1, /device:TPU:0, one launch (start us, length us, event | category | flops | bytes accessed | tf_op | source)
XLA Modules:
  0.0 33.5 jit_solution(8338093657627400980)
XLA Ops:
  0.0 0.0 copy-start
  0.0 1.4 %copy-done = bf16[4,24,32,256]{3,2,1,0:T(8,128)(2,1)S(1)} copy-done((bf16[4,24,32,256]{3,2,1,0:T(8,128)(2,1)S(1)}, bf16[4,24,32,256]{3,2,1,0:T(8,128)(2,1)}, u32[]{:S(2)}) %copy-start) | copy-done | bytes 1572888
  1.4 0.0 copy-start.1
  1.4 0.0 copy-start.4
  1.4 0.0 copy-start.5
  1.4 0.0 copy-start.7
  1.4 0.0 copy-start.8
  1.4 0.8 %local.1 = (f32[8,256]{1,0:T(8,128)S(1)}, bf16[384,256]{1,0:T(8,128)(2,1)S(1)}, bf16[208,256]{1,0:T(8,128)(2,1)S(1)}, bf16[2,22,32,256]{3,2,1,0:T(8,128)(2,1)S(1)}) custom-call(bf16[4,24,32,256]{3,2,1,0:T(8,128)(2,1)S(1)} %copy-done), custom_call_target="tpu_custom_call" | custom-call | bytes 1032192 | tf_op jit(solution)/shard_map/local/pallas_call | solution.py:346
  2.2 3.1 %collective-permute-start.1 = (bf16[208,256]{1,0:T(8,128)(2,1)S(1)}, bf16[208,256]{1,0:T(8,128)(2,1)S(1)}, u32[]{:S(2)}, u32[]{:S(2)}) collective-permute-start(bf16[208,256]{1,0:T(8,128)(2,1)S(1)} %get-tuple-element.19), channel_id=1, source_target_pairs={{0,1},{1,2},{2,3},{3,0},{4,5},{5,6},{6,7},{7,4},{8,9},{9,10},{10,1... | collective-permute-start | bytes 319496 | tf_op jit(solution)/shard_map/ppermute | solution.py:357
  5.3 1.6 %collective-permute-start = (bf16[2,22,32,256]{3,2,1,0:T(8,128)(2,1)S(1)}, bf16[2,22,32,256]{3,2,1,0:T(8,128)(2,1)S(1)}, u32[]{:S(2)}, u32[]{:S(2)}) collective-permute-start(bf16[2,22,32,256]{3,2,1,0:T(8,128)(2,1)S(1)} %get-tuple-element.18), channel_id=1, source_target_pairs={{0,1},{1,2},{2,3},{3,0},{4,5},{5,6},{6,7},{7,4},{8,9},{9,10},{10,1... | collective-permute-start | bytes 2162696 | tf_op jit(solution)/shard_map/ppermute | solution.py:358
  6.9 4.2 %collective-permute-done.1.zrecv = bf16[208,256]{1,0:T(8,128)(2,1)S(1)} collective-permute-done((bf16[208,256]{1,0:T(8,128)(2,1)S(1)}, bf16[208,256]{1,0:T(8,128)(2,1)S(1)}, u32[]{:S(2)}, u32[]{:S(2)}) %collective-permute-start.1) | collective-permute-done | bytes 106528 | tf_op jit(solution)/shard_map/ppermute | solution.py:357
  11.1 0.1 rows.1
  11.2 0.1 collective-permute-start.2
  11.3 1.9 %collective-permute-start.3 = (bf16[240,256]{1,0:T(8,128)(2,1)S(1)}, bf16[240,256]{1,0:T(8,128)(2,1)S(1)}, u32[]{:S(2)}, u32[]{:S(2)}) collective-permute-start(bf16[240,256]{1,0:T(8,128)(2,1)S(1)} %get-tuple-element.24), channel_id=1, source_target_pairs={{0,24},{8,16},{16,8},{24,0},{1,25},{9,17},{17,9},{25,1},{2,26},{10... | collective-permute-start | bytes 368648 | tf_op jit(solution)/shard_map/ppermute | solution.py:369
  13.1 0.3 collective-permute-start.4
  13.4 4.1 %collective-permute-done.4.gott = bf16[48,256]{1,0:T(8,128)(2,1)S(1)} collective-permute-done((bf16[48,256]{1,0:T(8,128)(2,1)S(1)}, bf16[48,256]{1,0:T(8,128)(2,1)S(1)}, u32[]{:S(2)}, u32[]{:S(2)}) %collective-permute-start.4) | collective-permute-done | bytes 24608 | tf_op jit(solution)/shard_map/ppermute | solution.py:373
  17.5 0.0 collective-permute-done.2.got1
  17.5 0.0 collective-permute-done.3.got2
  17.5 0.1 cols.1
  17.7 1.7 %collective-permute-start.5 = (bf16[240,256]{1,0:T(8,128)(2,1)S(1)}, bf16[240,256]{1,0:T(8,128)(2,1)S(1)}, u32[]{:S(2)}, u32[]{:S(2)}) collective-permute-start(bf16[240,256]{1,0:T(8,128)(2,1)S(1)} %get-tuple-element.26), channel_id=1, source_target_pairs={{0,4},{4,0},{1,5},{5,1},{2,6},{6,2},{3,7},{7,3},{8,12},{12,8},{9,1... | collective-permute-start | bytes 368648 | tf_op jit(solution)/shard_map/ppermute | solution.py:380
  19.4 3.4 %collective-permute-done.5.refs_0_ = bf16[240,256]{1,0:T(8,128)(2,1)S(1)} collective-permute-done((bf16[240,256]{1,0:T(8,128)(2,1)S(1)}, bf16[240,256]{1,0:T(8,128)(2,1)S(1)}, u32[]{:S(2)}, u32[]{:S(2)}) %collective-permute-start.5) | collective-permute-done | bytes 122912 | tf_op jit(solution)/shard_map/ppermute | solution.py:380
  22.8 0.0 copy-done.1
  22.8 0.0 copy-done.4
  22.8 0.0 copy-done.5
  22.8 0.0 copy-done.6
  22.8 0.0 copy-done.7
  22.8 0.0 copy-done.8
  22.8 0.0 copy-start.2
  22.8 1.3 %copy-done.2 = bf16[3,3,256,256]{3,2,1,0:T(8,128)(2,1)S(1)} copy-done((bf16[3,3,256,256]{3,2,1,0:T(8,128)(2,1)S(1)}, bf16[3,3,256,256]{3,2,1,0:T(8,128)(2,1)}, u32[]{:S(2)}) %copy-start.2) | copy-done | bytes 1179672
  24.1 9.3 %own.1 = (bf16[4,24,32,256]{3,2,1,0:T(8,128)(2,1)}, bf16[2,768,256]{2,1,0:T(8,128)(2,1)S(1)}, f32[12,256]{1,0:T(8,128)S(1)}) custom-call(bf16[4,24,32,256]{3,2,1,0:T(8,128)(2,1)S(1)} %copy-done.1, bf16[6,2,32,256]{3,2,1,0:T(8,128)(2,1)S(1)} %get-tuple-element.25.halo, bf16[240,256]{1,0:T(8,128)(2,1)S(1)} %collective-permute-done.5.refs_0_, ...), custom_call_target="tpu_custom_call" | custom-call | flops 4227858432 | bytes 2371584 | tf_op jit(solution)/shard_map/own/pallas_call | solution.py:403
  33.4 0.0 collective-permute-done.bulk
  33.4 0.0 copy-done.3
  (3 shorter events, 0.0 us)
Async XLA Ops:
  0.0 1.4 %copy-start = (bf16[4,24,32,256]{3,2,1,0:T(8,128)(2,1)S(1)}, bf16[4,24,32,256]{3,2,1,0:T(8,128)(2,1)}, u32[]{:S(2)}) copy-start(bf16[4,24,32,256]{3,2,1,0:T(8,128)(2,1)} %video.3) | copy-start | bytes 4718596
  1.4 21.4 %copy-start.1 = (bf16[4,24,32,256]{3,2,1,0:T(8,128)(2,1)S(1)}, bf16[4,24,32,256]{3,2,1,0:T(8,128)(2,1)}, u32[]{:S(2)}) copy-start(bf16[4,24,32,256]{3,2,1,0:T(8,128)(2,1)} %video.3) | copy-start | bytes 4718596
  1.4 21.4 %copy-start.4 = (bf16[3,256,256]{2,1,0:T(8,128)(2,1)S(1)}, bf16[3,256,256]{2,1,0:T(8,128)(2,1)}, u32[]{:S(2)}) copy-start(bf16[3,256,256]{2,1,0:T(8,128)(2,1)} %param.12) | copy-start | bytes 1179652
  1.4 21.4 %copy-start.5 = (f32[256]{0:T(256)S(1)}, f32[256]{0:T(256)}, u32[]{:S(2)}) copy-start(f32[256]{0:T(256)} %param.8) | copy-start | bytes 3076
  1.4 21.4 %copy-start.6 = (f32[256]{0:T(256)S(1)}, f32[256]{0:T(256)}, u32[]{:S(2)}) copy-start(f32[256]{0:T(256)} %param.9) | copy-start | bytes 3076
  1.4 21.4 %copy-start.7 = (f32[256]{0:T(256)S(1)}, f32[256]{0:T(256)}, u32[]{:S(2)}) copy-start(f32[256]{0:T(256)} %param.11) | copy-start | bytes 3076
  1.4 21.4 %copy-start.8 = (f32[256]{0:T(256)S(1)}, f32[256]{0:T(256)}, u32[]{:S(2)}) copy-start(f32[256]{0:T(256)} %param.13) | copy-start | bytes 3076
  2.2 8.9 %collective-permute-start.1 = (bf16[208,256]{1,0:T(8,128)(2,1)S(1)}, bf16[208,256]{1,0:T(8,128)(2,1)S(1)}, u32[]{:S(2)}, u32[]{:S(2)}) collective-permute-start(bf16[208,256]{1,0:T(8,128)(2,1)S(1)} %get-tuple-element.19), channel_id=1, source_target_pairs={{0,1},{1,2},{2,3},{3,0},{4,5},{5,6},{6,7},{7,4},{8,9},{9,10},{10,1... | collective-permute-start | bytes 319496 | tf_op jit(solution)/shard_map/ppermute | solution.py:357
  5.3 28.1 %collective-permute-start = (bf16[2,22,32,256]{3,2,1,0:T(8,128)(2,1)S(1)}, bf16[2,22,32,256]{3,2,1,0:T(8,128)(2,1)S(1)}, u32[]{:S(2)}, u32[]{:S(2)}) collective-permute-start(bf16[2,22,32,256]{3,2,1,0:T(8,128)(2,1)S(1)} %get-tuple-element.18), channel_id=1, source_target_pairs={{0,1},{1,2},{2,3},{3,0},{4,5},{5,6},{6,7},{7,4},{8,9},{9,10},{10,1... | collective-permute-start | bytes 2162696 | tf_op jit(solution)/shard_map/ppermute | solution.py:358
  11.2 6.3 %collective-permute-start.2 = (bf16[240,256]{1,0:T(8,128)(2,1)S(1)}, bf16[240,256]{1,0:T(8,128)(2,1)S(1)}, u32[]{:S(2)}, u32[]{:S(2)}) collective-permute-start(bf16[240,256]{1,0:T(8,128)(2,1)S(1)} %get-tuple-element.23), channel_id=1, source_target_pairs={{0,8},{8,0},{16,24},{24,16},{1,9},{9,1},{17,25},{25,17},{2,10},{10... | collective-permute-start | bytes 368648 | tf_op jit(solution)/shard_map/ppermute | solution.py:368
  11.3 6.3 %collective-permute-start.3 = (bf16[240,256]{1,0:T(8,128)(2,1)S(1)}, bf16[240,256]{1,0:T(8,128)(2,1)S(1)}, u32[]{:S(2)}, u32[]{:S(2)}) collective-permute-start(bf16[240,256]{1,0:T(8,128)(2,1)S(1)} %get-tuple-element.24), channel_id=1, source_target_pairs={{0,24},{8,16},{16,8},{24,0},{1,25},{9,17},{17,9},{25,1},{2,26},{10... | collective-permute-start | bytes 368648 | tf_op jit(solution)/shard_map/ppermute | solution.py:369
  13.1 4.4 %collective-permute-start.4 = (bf16[48,256]{1,0:T(8,128)(2,1)S(1)}, bf16[48,256]{1,0:T(8,128)(2,1)S(1)}, u32[]{:S(2)}, u32[]{:S(2)}) collective-permute-start(bf16[48,256]{1,0:T(8,128)(2,1)S(1)} %get-tuple-element.22.terms), channel_id=1, source_target_pairs={{0,16},{8,24},{16,0},{24,8},{1,17},{9,25},{17,1},{25,9},{2,18},{10... | collective-permute-start | bytes 73736 | tf_op jit(solution)/shard_map/ppermute | solution.py:373
  17.7 5.1 %collective-permute-start.5 = (bf16[240,256]{1,0:T(8,128)(2,1)S(1)}, bf16[240,256]{1,0:T(8,128)(2,1)S(1)}, u32[]{:S(2)}, u32[]{:S(2)}) collective-permute-start(bf16[240,256]{1,0:T(8,128)(2,1)S(1)} %get-tuple-element.26), channel_id=1, source_target_pairs={{0,4},{4,0},{1,5},{5,1},{2,6},{6,2},{3,7},{7,3},{8,12},{12,8},{9,1... | collective-permute-start | bytes 368648 | tf_op jit(solution)/shard_map/ppermute | solution.py:380
  22.8 1.3 %copy-start.2 = (bf16[3,3,256,256]{3,2,1,0:T(8,128)(2,1)S(1)}, bf16[3,3,256,256]{3,2,1,0:T(8,128)(2,1)}, u32[]{:S(2)}) copy-start(bf16[3,3,256,256]{3,2,1,0:T(8,128)(2,1)} %param.10) | copy-start | bytes 3538948
  24.1 9.3 %copy-start.3 = (bf16[3,3,256,256]{3,2,1,0:T(8,128)(2,1)S(1)}, bf16[3,3,256,256]{3,2,1,0:T(8,128)(2,1)}, u32[]{:S(2)}) copy-start(bf16[3,3,256,256]{3,2,1,0:T(8,128)(2,1)} %param.10) | copy-start | bytes 3538948

commit v2 on v0

v2 whole, which is shorter than its diff:
```python
import functools

import jax
import jax.numpy as jnp
from jax import lax
from jax.experimental import pallas as pl
from jax.experimental.pallas import tpu as pltpu
from jax.sharding import PartitionSpec as P

G = 32
EPS = 1e-06
QUARTERS = 4
DOTS = 6
PREV = 2
F32 = jnp.float32
BF16 = jnp.bfloat16
VMEM = pl.BlockSpec(memory_space=pltpu.VMEM)
ANY = pl.BlockSpec(memory_space=pl.ANY)


def call(kernel, outs, out_specs=None, scratch=(), name=None, **kw):
    return pl.pallas_call(
        kernel,
        out_shape=outs,
        out_specs=out_specs or [VMEM] * len(outs),
        scratch_shapes=list(scratch),
        compiler_params=pltpu.CompilerParams(vmem_limit_bytes=24 << 20),
        cost_estimate=pl.CostEstimate(flops=1024, bytes_accessed=1024, transcendentals=0),
        name=name,
        **kw,
    )


def pad_to(n, k):
    return (n + k - 1) // k * k


def split3(x):
    hi = x.astype(BF16)
    rest = x - hi.astype(F32)
    mid = rest.astype(BF16)
    low = (rest - mid.astype(F32)).astype(BF16)
    return hi, mid, low


def as_terms(x, rows):
    parts = jnp.concatenate([t.astype(F32) for t in split3(x)], axis=0)
    fill = rows - parts.shape[0]
    if fill:
        parts = jnp.concatenate([parts, jnp.zeros((fill, x.shape[1]), F32)], axis=0)
    return parts.astype(BF16)


def from_terms(t, rows):
    t = t.astype(F32)
    return t[:rows] + t[rows : 2 * rows] + t[2 * rows : 3 * rows]


class Sizes:
    def __init__(self, video, ha, wa):
        self.frames, self.rows, self.cols, self.chans = video.shape
        self.ha, self.wa = ha, wa
        self.ncol = 1 if wa == 2 else 2
        self.fused = ha == 4 and wa == 2
        self.colrow = pad_to(self.rows + 2, 16)
        self.strip = 2 * self.cols + self.ncol * self.colrow
        self.stats = pad_to(3 * 2 * self.frames, 16)
        self.last = pad_to(3 * 2 * PREV, 16)
        self.corner = pad_to(self.frames, 16)


def head_kernel(s, video, bulk):
    for p in range(PREV):
        bulk[p] = video[s.frames - PREV + p]


def local_kernel(s, video, bulk, pay, stats, *cols):
    ha, wa = lax.axis_index("ha"), lax.axis_index("wa")
    even = lax.rem(ha, 2) == 0
    means, squares = [], []
    for f in range(s.frames):
        total = jnp.zeros((s.cols, s.chans), F32)
        for r in range(s.rows):
            total = total + video[f, r].astype(F32)
        mean = jnp.sum(total, axis=0, keepdims=True) * (1.0 / (s.rows * s.cols))
        spread = jnp.zeros((s.cols, s.chans), F32)
        left, right = [], []
        for r in range(s.rows):
            x = video[f, r].astype(F32)
            left.append(x[:1])
            right.append(x[s.cols - 1 :])
            x = x - mean
            spread = spread + x * x
        means.append(mean)
        squares.append(jnp.sum(spread, axis=0, keepdims=True))
        fill = [jnp.zeros((s.colrow - s.rows, s.chans), F32)]
        left = jnp.concatenate(left + fill, axis=0)
        right = jnp.concatenate(right + fill, axis=0)
        if s.ncol == 1:
            edges = [jnp.where(wa == 0, right, left)]
        else:
            edges = [right, left]
        for ref, e in zip(cols, edges):
            ref[f * s.colrow : (f + 1) * s.colrow] = e.astype(BF16)
        top = video[f, 0].astype(F32)
        bottom = video[f, s.rows - 1].astype(F32)
        pay[f * s.cols : (f + 1) * s.cols] = jnp.where(even, bottom, top).astype(BF16)
    stat = jnp.concatenate(means + squares, axis=0)
    stats[...] = stat
    o = s.frames * s.cols
    pay[o : o + s.stats] = as_terms(stat, s.stats)


def merge(n, parts):
    half = parts[0].shape[0] // 2
    mean = sum(p[:half] for p in parts) * (1.0 / len(parts))
    square = sum(p[half:] + n * (p[:half] - mean) * (p[:half] - mean) for p in parts)
    return jnp.concatenate([mean, square], axis=0)


def pair_kernel(s, video, stats, got, *refs):
    cols, refs = refs[: s.ncol], refs[s.ncol :]
    payy, part = refs[:2]
    payx, payd = refs[2 : 2 + s.ncol], refs[2 + s.ncol :]
    ha, wa = lax.axis_index("ha"), lax.axis_index("wa")
    even = lax.rem(ha, 2) == 0
    o = s.frames * s.cols
    stat = merge(float(s.rows * s.cols), [stats[...], from_terms(got[o : o + s.stats], 2 * s.frames)])
    part[...] = stat
    terms = as_terms(stat, s.stats)
    at = lax.broadcasted_iota(jnp.int32, (s.colrow, s.chans), 0)
    cells = [[] for _ in range(s.ncol)]
    for f in range(s.frames):
        top = video[f, 0].astype(F32)
        bottom = video[f, s.rows - 1].astype(F32)
        outer = jnp.where(even, top, bottom)
        payy[f * s.cols : (f + 1) * s.cols] = outer.astype(BF16)
        inner = got[f * s.cols : (f + 1) * s.cols].astype(F32)
        for k in range(s.ncol):
            right = wa == 0 if s.ncol == 1 else k == 0
            cell = jnp.where(right, inner[s.cols - 1 :], inner[:1])
            cells[k].append(jnp.where(right, outer[s.cols - 1 :], outer[:1]))
            edge = cols[k][f * s.colrow : (f + 1) * s.colrow].astype(F32)
            edge = jnp.where(at >= s.rows, cell, edge)
            payx[k][f * s.colrow : (f + 1) * s.colrow] = edge.astype(BF16)
    for k in range(s.ncol):
        fill = s.corner - s.frames
        rows = cells[k] + ([jnp.zeros((fill, s.chans), F32)] if fill else [])
        payd[k][: s.corner] = jnp.concatenate(rows, axis=0).astype(BF16)
    payy[o : o + s.stats] = terms
    if s.fused:
        o = s.frames * s.colrow
        payx[0][o : o + s.stats] = terms
        payd[0][s.corner : s.corner + s.stats] = terms


def edge_kernel(s, part, gain, got, goty, *refs):
    gotx, gotd = refs[: s.ncol], refs[s.ncol : 2 * s.ncol]
    aff, hand, halo, *cols = refs[2 * s.ncol :]
    even = lax.rem(lax.axis_index("ha"), 2) == 0
    rows = 2 * s.frames
    count = float(s.rows * s.cols * s.ha * s.wa)
    stat = part[...]
    if s.fused:
        offsets = ((goty, s.frames * s.cols), (gotx[0], s.frames * s.colrow), (gotd[0], s.corner))
        stat = merge(count / 4, [stat] + [from_terms(ref[o : o + s.stats], rows) for ref, o in offsets])
    width = s.chans // G
    a = lax.broadcasted_iota(jnp.int32, (s.chans, s.chans), 0) // width
    b = lax.broadcasted_iota(jnp.int32, (s.chans, s.chans), 1) // width
    group = jnp.where(a == b, 1.0, 0.0).astype(BF16)

    def tot(x):
        terms = jnp.concatenate(split3(x), axis=0)
        y = jnp.dot(terms, group, preferred_element_type=F32)
        n = s.frames
        return y[:n] + y[n : 2 * n] + y[2 * n :]

    m, q = stat[: s.frames], stat[s.frames :]
    mean = tot(m) * (1.0 / width)
    var = tot(q + count * (m - mean) * (m - mean)) * (1.0 / (count * width))
    scale = lax.rsqrt(var + EPS) * gain[...] * 0.5
    aff[: s.frames] = mean
    aff[s.frames :] = scale
    first = s.frames - PREV
    at = lax.broadcasted_iota(jnp.int32, (s.colrow, s.chans), 0)
    for f in range(s.frames):
        p = (f - first) * s.strip
        one = got[f * s.cols : (f + 1) * s.cols].astype(F32)
        two = goty[f * s.cols : (f + 1) * s.cols].astype(F32)
        top = jnp.where(even, two, one).astype(BF16)
        bottom = jnp.where(even, one, two).astype(BF16)
        halo[f, 0] = top
        halo[f, 1] = bottom
        if f >= first:
            hand[p : p + s.cols] = top
            hand[p + s.cols : p + 2 * s.cols] = bottom
        for k in range(s.ncol):
            cell = gotd[k][: s.corner].astype(F32)[f : f + 1]
            edge = gotx[k][f * s.colrow : (f + 1) * s.colrow].astype(F32)
            outer = jnp.where(even, s.rows, s.rows + 1)
            edge = jnp.where(at == outer, cell, edge).astype(BF16)
            cols[k][f * s.colrow : (f + 1) * s.colrow] = edge
            if f >= first:
                o = p + 2 * s.cols + k * s.colrow
                hand[o : o + s.colrow] = edge
    o = PREV * s.strip
    hand[o : o + s.last] = as_terms(jnp.concatenate([mean[first:], scale[first:]], axis=0), s.last)


def activation(x, mean, scale, shift):
    h = (x - mean) * scale + shift
    return h + h * jnp.tanh(h)


def fill_taps(s, taps, raw_row, edges, mean, scale, shift):
    ha, wa = lax.axis_index("ha"), lax.axis_index("wa")
    top_in = jnp.where(ha > 0, 1.0, 0.0).astype(F32)
    bottom_in = jnp.where(ha < s.ha - 1, 1.0, 0.0).astype(F32)
    left_in = jnp.where(wa > 0, 1.0, 0.0).astype(F32)
    right_in = jnp.where(wa < s.wa - 1, 1.0, 0.0).astype(F32)
    acts = [activation(e.astype(F32), mean, scale, shift) for e in edges]
    left, right = acts[0] * left_in, acts[-1] * right_in
    at = lax.broadcasted_iota(jnp.int32, (s.cols, s.chans), 0)
    for i in range(s.rows + 2):
        act = activation(raw_row(i).astype(F32), mean, scale, shift)
        j = s.rows if i == 0 else s.rows + 1 if i == s.rows + 1 else i - 1
        lcell, rcell = left[j : j + 1], right[j : j + 1]
        west = jnp.where(at == 0, lcell, pltpu.roll(act, 1, 0))
        east = jnp.where(at == s.cols - 1, rcell, pltpu.roll(act, s.cols - 1, 0))
        if i in (0, s.rows + 1):
            inside = top_in if i == 0 else bottom_in
            west, act, east = west * inside, act * inside, east * inside
        taps[0, i] = west.astype(BF16)
        taps[1, i] = act.astype(BF16)
        taps[2, i] = east.astype(BF16)


def spatial_dot(s, taps, weight, bias):
    step = s.rows // DOTS
    done = []
    for r in range(0, s.rows, step):
        lhs = jnp.concatenate(
            [
                taps[dx, r + dy : r + dy + step].reshape(step * s.cols, s.chans)
                for dy in range(3)
                for dx in range(3)
            ],
            axis=1,
        )
        done.append((jnp.dot(lhs, weight[...], preferred_element_type=F32) + bias[...]).astype(BF16))
    return jnp.concatenate(done, axis=0)


def temporal_dot(s, frames, weight, bias):
    lhs = jnp.concatenate(frames, axis=1)
    out = jnp.dot(lhs, weight[...], preferred_element_type=F32) + bias[...]
    return out.astype(BF16).reshape(s.rows, s.cols, s.chans)


def put(s, ref, enc, sem, f, skip=0):
    step = s.rows // QUARTERS
    parts = [pl.ds(k * step, step) for k in range(QUARTERS)]
    return [
        pltpu.make_async_copy(ref.at[f - skip, part], enc.at[f, part], sem.at[f, k])
        for k, part in enumerate(parts)
    ]


def start(copies):
    for c in copies:
        c.start()


def wait(copies):
    for c in copies:
        c.wait()


def own_kernel(s, video, halo, aff, nbias, sw, sb, tw, tb, *refs):
    cols = refs[: s.ncol]
    enc, last, lead, taps, spatial, out, sem = refs[s.ncol :]
    shift = nbias[...] * 0.5
    first = lax.axis_index("ta") == 0

    def conv(f):
        def raw_row(i):
            if i == 0:
                return halo[f, 0]
            if i == s.rows + 1:
                return halo[f, 1]
            return video[f, i - 1]

        edges = [c[pl.ds(f * s.colrow, s.colrow)] for c in cols]
        fill_taps(s, taps, raw_row, edges, aff[pl.ds(f, 1)], aff[pl.ds(s.frames + f, 1)], shift)
        spatial[f] = spatial_dot(s, taps, sw, sb)

    def encode(f):
        out[f] = temporal_dot(s, [spatial[max(f - k, 0)] for k in range(3)], tw, tb)
        start(put(s, out, enc, sem, f))

    def frame(f, _):
        conv(f)
        return _

    lax.fori_loop(0, s.frames, frame, 0)

    @pl.when(first)
    def _():
        for f in range(PREV):
            encode(f)

    for f in range(PREV, s.frames):
        last[f - PREV] = temporal_dot(s, [spatial[f - k] for k in range(3)], tw, tb)
    for f in range(PREV):
        lead[f] = spatial[f]

    @pl.when(first)
    def _():
        for f in range(PREV):
            wait(put(s, out, enc, sem, f))


def prev_kernel(s, bulk, got, nbias, sw, sb, tw, tb, lead, last, _, enc, taps, spatial, out, sem):
    shift = nbias[...] * 0.5
    for f in range(PREV, s.frames):
        start(put(s, last, enc, sem, f, PREV))

    @pl.when(lax.axis_index("ta") > 0)
    def _():
        o = PREV * s.strip
        stat = from_terms(got[o : o + s.last], 2 * PREV)
        for p in range(PREV):
            o = p * s.strip

            def raw_row(i):
                if i == 0:
                    return got[o : o + s.cols]
                if i == s.rows + 1:
                    return got[o + s.cols : o + 2 * s.cols]
                return bulk[p, i - 1]

            o2 = o + 2 * s.cols
            edges = [got[o2 + k * s.colrow : o2 + (k + 1) * s.colrow] for k in range(s.ncol)]
            fill_taps(s, taps.at[p], raw_row, edges, stat[p : p + 1], stat[PREV + p : PREV + p + 1], shift)
            spatial[p] = spatial_dot(s, taps.at[p], sw, sb)
        seq = [spatial[0], spatial[1], lead[0], lead[1]]
        for f in range(PREV):
            out[f] = temporal_dot(s, [seq[PREV + f - k] for k in range(3)], tw, tb)
            start(put(s, out, enc, sem, f))
        for f in range(PREV):
            wait(put(s, out, enc, sem, f))

    for f in range(PREV, s.frames):
        wait(put(s, last, enc, sem, f, PREV))


def mates(n, phase):
    if phase == 0:
        return [(i, i ^ 1) for i in range(n)]
    return [(i, (i - 1) % n if i % 2 == 0 else (i + 1) % n) for i in range(n)]


def local(video, norm_gain, norm_bias, spatial_weight, spatial_bias, temporal_weight, temporal_bias):
    nta, nha, nwa = (lax.axis_size(a) for a in ("ta", "ha", "wa"))
    s = Sizes(video, nha, nwa)
    c = s.chans
    sd = jax.ShapeDtypeStruct
    ring = [(i, (i + 1) % nta) for i in range(nta)]
    if nwa == 2:
        sides = [[(0, 1), (1, 0)]]
    else:
        sides = [[(i, (i + d) % nwa) for i in range(nwa)] for d in (1, -1)]
    sw = spatial_weight.reshape(9 * c, c)
    tw = temporal_weight.reshape(3 * c, c)
    gain, nbias, sb, tb = (v.reshape(1, c) for v in (norm_gain, norm_bias, spatial_bias, temporal_bias))

    (bulk,) = call(
        functools.partial(head_kernel, s),
        [sd((PREV,) + video.shape[1:], BF16)],
        name="head",
        in_specs=[VMEM],
    )(video)
    rowpay = sd((s.frames * s.cols + s.stats, c), BF16)
    stat = sd((2 * s.frames, c), F32)
    colout = [sd((s.frames * s.colrow, c), BF16)] * s.ncol
    riding = s.stats if s.fused else 0
    pay, stats, *cols = call(
        functools.partial(local_kernel, s),
        [rowpay, stat] + colout,
        name="local",
        in_specs=[VMEM, ANY],
    )(video, bulk)
    bulk = lax.ppermute(bulk, "ta", ring)
    got1 = lax.ppermute(pay, "ha", mates(nha, 0))
    payy, part, *pays = call(
        functools.partial(pair_kernel, s),
        [rowpay, stat]
        + [sd((s.frames * s.colrow + riding, c), BF16)] * s.ncol
        + [sd((s.corner + riding, c), BF16)] * s.ncol,
        name="pair",
        in_specs=[VMEM] * (3 + s.ncol),
    )(video, stats, got1, *cols)
    outer = mates(nha, 1)
    diagonal = [[(h * nwa + w, g * nwa + v) for h, g in outer for w, v in p] for p in sides]
    goty = lax.ppermute(payy, "ha", outer)
    gotx = [lax.ppermute(x, "wa", p) for x, p in zip(pays[: s.ncol], sides)]
    gotd = [lax.ppermute(x, ("ha", "wa"), p) for x, p in zip(pays[s.ncol :], diagonal)]
    if not s.fused:
        every = lax.all_gather(stats, ("ha", "wa"))
        part = merge(float(s.rows * s.cols), [every[i] for i in range(nha * nwa)])
    aff, hand, halo, *cols = call(
        functools.partial(edge_kernel, s),
        [stat, sd((PREV * s.strip + s.last, c), BF16), sd((s.frames, 2, s.cols, c), BF16)] + colout,
        name="edge",
        in_specs=[VMEM] * (4 + 2 * s.ncol),
    )(part, gain, got1, goty, *gotx, *gotd)
    got = lax.ppermute(hand, "ta", ring)
    frame = (s.rows * s.cols, c)
    taps = (3, s.rows + 2, s.cols, c)
    one = video.shape[1:]
    enc, last, lead = call(
        functools.partial(own_kernel, s),
        [sd(video.shape, BF16), sd((s.frames - PREV,) + one, BF16), sd((PREV,) + frame, BF16)],
        out_specs=[ANY, VMEM, VMEM],
        scratch=[
            pltpu.VMEM(taps, BF16),
            pltpu.VMEM((s.frames,) + frame, BF16),
            pltpu.VMEM((PREV,) + one, BF16),
            pltpu.SemaphoreType.DMA((PREV, QUARTERS)),
        ],
        name="own",
        in_specs=[VMEM] * (8 + s.ncol),
    )(video, halo, aff, nbias, sw, sb, tw, tb, *cols)
    (enc,) = call(
        functools.partial(prev_kernel, s),
        [sd(video.shape, BF16)],
        out_specs=[ANY],
        scratch=[
            pltpu.VMEM((PREV,) + taps, BF16),
            pltpu.VMEM((PREV,) + frame, BF16),
            pltpu.VMEM((PREV,) + one, BF16),
            pltpu.SemaphoreType.DMA((s.frames, QUARTERS)),
        ],
        name="prev",
        in_specs=[VMEM] * 9 + [ANY],
        input_output_aliases={9: 0},
    )(bulk, got, nbias, sw, sb, tw, tb, lead, last, enc)
    return enc


def solution(mesh):
    placed = (P("ta", "ha", "wa", None), P(), P(), P(), P(), P(), P())
    return jax.shard_map(
        local, mesh=mesh, in_specs=placed, out_specs=P("ta", "ha", "wa", None), check_vma=False
    )
```

time: 84 us -> 27.6 us (0.33)
  the two profiles are of different devices: /device:TPU:16 before, /device:TPU:0 now
where the time goes in v2:
time: 27.6 us; the launch traced here: 27.4 us
  waiting for transfers between devices  9.55 us (35%)
  Pallas kernels  8.54 us (31%)
  starting transfers between devices  7.77 us (28%)
  local copies, waits for them, and re-layouts  1.45 us (5%)
    pallas_call x1, Pallas kernels, local(): call(functools.partial(own_kernel, s), [sd(video.shape, BF16), sd((s.fram...  6.34 us
    ppermute x1, waiting for transfers between devices, local(): got = lax.ppermute(hand, 'ta', ring)  4.28 us
    ppermute x1, waiting for transfers between devices, local(): lax.ppermute(x, ('ha', 'wa'), p)  4 us
    ppermute x1, starting transfers between devices, local(): bulk = lax.ppermute(bulk, 'ta', ring)  3.08 us
    ppermute x1, starting transfers between devices, local(): got = lax.ppermute(hand, 'ta', ring)  1.63 us
    ppermute x1, starting transfers between devices, local(): gotx = [lax.ppermute(x, 'wa', p) for x, p in zip(pays[:s.ncol], sides)]  1.49 us
    unnamed x16, local copies, waits for them, and re-layouts  1.45 us
    ppermute x1, starting transfers between devices, local(): goty = lax.ppermute(payy, 'ha', outer)  1.34 us
  transfers between devices with their start and end apart: 6, of which 3 were waited for; matrix products, arithmetic and copies ran while one was open for 0% of the time, Pallas kernels for 27%

profile of v2, /device:TPU:0, one launch (start us, length us, event | category | flops | bytes accessed | tf_op | source)
XLA Modules:
  0.0 27.4 jit_solution(14551450225242577475)
XLA Ops:
  0.0 0.0 copy-start
  0.0 1.4 %copy-done = bf16[4,24,32,256]{3,2,1,0:T(8,128)(2,1)S(1)} copy-done((bf16[4,24,32,256]{3,2,1,0:T(8,128)(2,1)S(1)}, bf16[4,24,32,256]{3,2,1,0:T(8,128)(2,1)}, u32[]{:S(2)}) %copy-start) | copy-done | bytes 1572888
  1.4 0.1 head.1.bulk
  1.5 0.0 copy-start.7
  1.5 3.1 %collective-permute-start = (bf16[2,24,32,256]{3,2,1,0:T(8,128)(2,1)S(1)}, bf16[2,24,32,256]{3,2,1,0:T(8,128)(2,1)S(1)}, u32[]{:S(2)}, u32[]{:S(2)}) collective-permute-start(bf16[2,24,32,256]{3,2,1,0:T(8,128)(2,1)S(1)} %head.1.bulk), channel_id=1, source_target_pairs={{0,1},{1,2},{2,3},{3,0},{4,5},{5,6},{6,7},{7,4},{8,9},{9,10},{10,1... | collective-permute-start | bytes 2359304 | tf_op jit(solution)/shard_map/ppermute | solution.py:393
  4.6 0.0 copy-start.2
  4.6 0.7 %local.1 = (bf16[160,256]{1,0:T(8,128)(2,1)S(1)}, f32[8,256]{1,0:T(8,128)S(1)}, bf16[128,256]{1,0:T(8,128)(2,1)S(1)}) custom-call(bf16[4,24,32,256]{3,2,1,0:T(8,128)(2,1)S(1)} %copy-done, bf16[2,24,32,256]{3,2,1,0:T(8,128)(2,1)S(1)} %head.1.bulk), custom_call_target="tpu_custom_call" | custom-call | flops 1024 | bytes 1024 | tf_op jit(solution)/shard_map/local/pallas_call | solution.py:387
  5.3 0.0 copy-start.3
  5.3 0.0 copy-start.4
  5.3 0.0 copy-start.5
  5.3 0.0 copy-start.6
  5.4 0.1 collective-permute-start.1
  5.4 1.3 %collective-permute-done.1.got = bf16[160,256]{1,0:T(8,128)(2,1)S(1)} collective-permute-done((bf16[160,256]{1,0:T(8,128)(2,1)S(1)}, bf16[160,256]{1,0:T(8,128)(2,1)S(1)}, u32[]{:S(2)}, u32[]{:S(2)}) %collective-permute-start.1) | collective-permute-done | bytes 81952 | tf_op jit(solution)/shard_map/ppermute | solution.py:394
  6.8 1.3 %collective-permute-start.2 = (bf16[160,256]{1,0:T(8,128)(2,1)S(1)}, bf16[160,256]{1,0:T(8,128)(2,1)S(1)}, u32[]{:S(2)}, u32[]{:S(2)}) collective-permute-start(bf16[160,256]{1,0:T(8,128)(2,1)S(1)} %get-tuple-element.23), channel_id=1, source_target_pairs={{0,24},{8,16},{16,8},{24,0},{1,25},{9,17},{17,9},{25,1},{2,26},{10... | collective-permute-start | bytes 245768 | tf_op jit(solution)/shard_map/ppermute | solution.py:405
  8.1 1.5 %collective-permute-start.3 = (bf16[160,256]{1,0:T(8,128)(2,1)S(1)}, bf16[160,256]{1,0:T(8,128)(2,1)S(1)}, u32[]{:S(2)}, u32[]{:S(2)}) collective-permute-start(bf16[160,256]{1,0:T(8,128)(2,1)S(1)} %get-tuple-element.24), channel_id=1, source_target_pairs={{0,4},{4,0},{1,5},{5,1},{2,6},{6,2},{3,7},{7,3},{8,12},{12,8},{9,1... | collective-permute-start | bytes 245768 | tf_op jit(solution)/shard_map/ppermute | solution.py:406
  9.6 0.2 collective-permute-start.4
  9.7 4.0 %collective-permute-done.4.refs_1_ = bf16[48,256]{1,0:T(8,128)(2,1)S(1)} collective-permute-done((bf16[48,256]{1,0:T(8,128)(2,1)S(1)}, bf16[48,256]{1,0:T(8,128)(2,1)S(1)}, u32[]{:S(2)}, u32[]{:S(2)}) %collective-permute-start.4) | collective-permute-done | bytes 24608 | tf_op jit(solution)/shard_map/ppermute | solution.py:407
  13.7 0.0 collective-permute-done.2.goty
  13.7 0.0 collective-permute-done.3.refs_0_
  13.8 0.0 copy-done.7
  13.8 0.4 %edge.1 = (f32[8,256]{1,0:T(8,128)S(1)}, bf16[208,256]{1,0:T(8,128)(2,1)S(1)}, bf16[4,2,32,256]{3,2,1,0:T(8,128)(2,1)S(1)}, bf16[128,256]{1,0:T(8,128)(2,1)S(1)}) custom-call(f32[8,256]{1,0:T(8,128)S(1)} %get-tuple-element.22.part, f32[1,256]{1,0:T(1,128)S(1)} %bitcast.16, bf16[160,256]{1,0:T(8,128)(2,1)S(1)} %collective-permute-done.1.got, ...), custom_call_target="tpu_custom_call" | custom-call | flops 1024 | bytes 1024 | tf_op jit(solution)/shard_map/edge/pallas_call | solution.py:411
  14.1 1.6 %collective-permute-start.5 = (bf16[208,256]{1,0:T(8,128)(2,1)S(1)}, bf16[208,256]{1,0:T(8,128)(2,1)S(1)}, u32[]{:S(2)}, u32[]{:S(2)}) collective-permute-start(bf16[208,256]{1,0:T(8,128)(2,1)S(1)} %get-tuple-element.26), channel_id=1, source_target_pairs={{0,1},{1,2},{2,3},{3,0},{4,5},{5,6},{6,7},{7,4},{8,9},{9,10},{10,1... | collective-permute-start | bytes 319496 | tf_op jit(solution)/shard_map/ppermute | solution.py:417
  15.7 0.0 copy-done.2
  15.7 0.0 copy-done.1
  15.8 0.0 copy-done.3
  15.8 0.0 copy-done.4
  15.8 0.0 copy-done.5
  15.8 0.0 copy-done.6
  15.8 6.3 %own.1 = (bf16[4,24,32,256]{3,2,1,0:T(8,128)(2,1)}, bf16[2,24,32,256]{3,2,1,0:T(8,128)(2,1)S(1)}, bf16[2,768,256]{2,1,0:T(8,128)(2,1)S(1)}) custom-call(bf16[4,24,32,256]{3,2,1,0:T(8,128)(2,1)S(1)} %copy-done.1, bf16[4,2,32,256]{3,2,1,0:T(8,128)(2,1)S(1)} %get-tuple-element.27.halo, f32[8,256]{1,0:T(8,128)S(1)} %get-tuple-element.28.aff, ...), custom_call_target="tpu_custom_call" | custom-call | flops 1024 | bytes 1024 | tf_op jit(solution)/shard_map/own/pallas_call | solution.py:421
  22.1 4.3 %collective-permute-done.5.got = bf16[208,256]{1,0:T(8,128)(2,1)S(1)} collective-permute-done((bf16[208,256]{1,0:T(8,128)(2,1)S(1)}, bf16[208,256]{1,0:T(8,128)(2,1)S(1)}, u32[]{:S(2)}, u32[]{:S(2)}) %collective-permute-start.5) | collective-permute-done | bytes 106528 | tf_op jit(solution)/shard_map/ppermute | solution.py:417
  26.4 0.0 collective-permute-done.bulk
  26.4 1.0 %prev.1 = bf16[4,24,32,256]{3,2,1,0:T(8,128)(2,1)} custom-call(bf16[2,24,32,256]{3,2,1,0:T(8,128)(2,1)S(1)} %collective-permute-done.bulk, bf16[208,256]{1,0:T(8,128)(2,1)S(1)} %collective-permute-done.5.got, f32[1,256]{1,0:T(1,128)S(1)} %bitcast.11, bf16[2304,256]{1,0:T(8,128)(2,1)S(1)} %bitcast.7, ...), custom_call_target="tpu_custom_call", output_to_operand_aliasing={{}: (9, {})} | custom-call | flops 1024 | bytes 1024 | tf_op jit(solution)/shard_map/prev/pallas_call | solution.py:434
  (2 shorter events, 0.0 us)
Async XLA Ops:
  0.0 1.4 %copy-start = (bf16[4,24,32,256]{3,2,1,0:T(8,128)(2,1)S(1)}, bf16[4,24,32,256]{3,2,1,0:T(8,128)(2,1)}, u32[]{:S(2)}) copy-start(bf16[4,24,32,256]{3,2,1,0:T(8,128)(2,1)} %video.7) | copy-start | bytes 4718596
  1.5 12.3 %copy-start.7 = (f32[256]{0:T(256)S(1)}, f32[256]{0:T(256)}, u32[]{:S(2)}) copy-start(f32[256]{0:T(256)} %param.8) | copy-start | bytes 3076
  1.5 24.9 %collective-permute-start = (bf16[2,24,32,256]{3,2,1,0:T(8,128)(2,1)S(1)}, bf16[2,24,32,256]{3,2,1,0:T(8,128)(2,1)S(1)}, u32[]{:S(2)}, u32[]{:S(2)}) collective-permute-start(bf16[2,24,32,256]{3,2,1,0:T(8,128)(2,1)S(1)} %head.1.bulk), channel_id=1, source_target_pairs={{0,1},{1,2},{2,3},{3,0},{4,5},{5,6},{6,7},{7,4},{8,9},{9,10},{10,1... | collective-permute-start | bytes 2359304 | tf_op jit(solution)/shard_map/ppermute | solution.py:393
  4.6 11.2 %copy-start.2 = (bf16[3,3,256,256]{3,2,1,0:T(8,128)(2,1)S(1)}, bf16[3,3,256,256]{3,2,1,0:T(8,128)(2,1)}, u32[]{:S(2)}) copy-start(bf16[3,3,256,256]{3,2,1,0:T(8,128)(2,1)} %param.10) | copy-start | bytes 3538948
  5.3 10.4 %copy-start.1 = (bf16[4,24,32,256]{3,2,1,0:T(8,128)(2,1)S(1)}, bf16[4,24,32,256]{3,2,1,0:T(8,128)(2,1)}, u32[]{:S(2)}) copy-start(bf16[4,24,32,256]{3,2,1,0:T(8,128)(2,1)} %video.7) | copy-start | bytes 4718596
  5.3 10.4 %copy-start.3 = (bf16[3,256,256]{2,1,0:T(8,128)(2,1)S(1)}, bf16[3,256,256]{2,1,0:T(8,128)(2,1)}, u32[]{:S(2)}) copy-start(bf16[3,256,256]{2,1,0:T(8,128)(2,1)} %param.12) | copy-start | bytes 1179652
  5.3 10.4 %copy-start.4 = (f32[256]{0:T(256)S(1)}, f32[256]{0:T(256)}, u32[]{:S(2)}) copy-start(f32[256]{0:T(256)} %param.9) | copy-start | bytes 3076
  5.3 10.4 %copy-start.5 = (f32[256]{0:T(256)S(1)}, f32[256]{0:T(256)}, u32[]{:S(2)}) copy-start(f32[256]{0:T(256)} %param.11) | copy-start | bytes 3076
  5.3 10.4 %copy-start.6 = (f32[256]{0:T(256)S(1)}, f32[256]{0:T(256)}, u32[]{:S(2)}) copy-start(f32[256]{0:T(256)} %param.13) | copy-start | bytes 3076
  5.4 1.3 %collective-permute-start.1 = (bf16[160,256]{1,0:T(8,128)(2,1)S(1)}, bf16[160,256]{1,0:T(8,128)(2,1)S(1)}, u32[]{:S(2)}, u32[]{:S(2)}) collective-permute-start(bf16[160,256]{1,0:T(8,128)(2,1)S(1)} %get-tuple-element.20), channel_id=1, source_target_pairs={{0,8},{8,0},{16,24},{24,16},{1,9},{9,1},{17,25},{25,17},{2,10},{10... | collective-permute-start | bytes 245768 | tf_op jit(solution)/shard_map/ppermute | solution.py:394
  6.8 7.0 %collective-permute-start.2 = (bf16[160,256]{1,0:T(8,128)(2,1)S(1)}, bf16[160,256]{1,0:T(8,128)(2,1)S(1)}, u32[]{:S(2)}, u32[]{:S(2)}) collective-permute-start(bf16[160,256]{1,0:T(8,128)(2,1)S(1)} %get-tuple-element.23), channel_id=1, source_target_pairs={{0,24},{8,16},{16,8},{24,0},{1,25},{9,17},{17,9},{25,1},{2,26},{10... | collective-permute-start | bytes 245768 | tf_op jit(solution)/shard_map/ppermute | solution.py:405
  8.1 5.7 %collective-permute-start.3 = (bf16[160,256]{1,0:T(8,128)(2,1)S(1)}, bf16[160,256]{1,0:T(8,128)(2,1)S(1)}, u32[]{:S(2)}, u32[]{:S(2)}) collective-permute-start(bf16[160,256]{1,0:T(8,128)(2,1)S(1)} %get-tuple-element.24), channel_id=1, source_target_pairs={{0,4},{4,0},{1,5},{5,1},{2,6},{6,2},{3,7},{7,3},{8,12},{12,8},{9,1... | collective-permute-start | bytes 245768 | tf_op jit(solution)/shard_map/ppermute | solution.py:406
  9.6 4.2 %collective-permute-start.4 = (bf16[48,256]{1,0:T(8,128)(2,1)S(1)}, bf16[48,256]{1,0:T(8,128)(2,1)S(1)}, u32[]{:S(2)}, u32[]{:S(2)}) collective-permute-start(bf16[48,256]{1,0:T(8,128)(2,1)S(1)} %get-tuple-element.25), channel_id=1, source_target_pairs={{0,28},{4,24},{8,20},{12,16},{16,12},{20,8},{24,4},{28,0},{1,29},{... | collective-permute-start | bytes 73736 | tf_op jit(solution)/shard_map/ppermute | solution.py:407
  14.1 12.3 %collective-permute-start.5 = (bf16[208,256]{1,0:T(8,128)(2,1)S(1)}, bf16[208,256]{1,0:T(8,128)(2,1)S(1)}, u32[]{:S(2)}, u32[]{:S(2)}) collective-permute-start(bf16[208,256]{1,0:T(8,128)(2,1)S(1)} %get-tuple-element.26), channel_id=1, source_target_pairs={{0,1},{1,2},{2,3},{3,0},{4,5},{5,6},{6,7},{7,4},{8,9},{9,10},{10,1... | collective-permute-start | bytes 319496 | tf_op jit(solution)/shard_map/ppermute | solution.py:417

commit v3 on v2

--- a/solution.py
+++ b/solution.py
@@ -18,14 +18,14 @@
 ANY = pl.BlockSpec(memory_space=pl.ANY)
 
 
-def call(kernel, outs, out_specs=None, scratch=(), name=None, **kw):
+def call(kernel, outs, out_specs=None, scratch=(), flops=1024, name=None, **kw):
     return pl.pallas_call(
         kernel,
         out_shape=outs,
         out_specs=out_specs or [VMEM] * len(outs),
         scratch_shapes=list(scratch),
         compiler_params=pltpu.CompilerParams(vmem_limit_bytes=24 << 20),
-        cost_estimate=pl.CostEstimate(flops=1024, bytes_accessed=1024, transcendentals=0),
+        cost_estimate=pl.CostEstimate(flops=flops, bytes_accessed=1024, transcendentals=0),
         name=name,
         **kw,
     )
@@ -65,16 +65,18 @@
         self.colrow = pad_to(self.rows + 2, 16)
         self.strip = 2 * self.cols + self.ncol * self.colrow
         self.stats = pad_to(3 * 2 * self.frames, 16)
-        self.last = pad_to(3 * 2 * PREV, 16)
+        self.early = (PREV - 1) * self.rows + self.rows // 12
         self.corner = pad_to(self.frames, 16)
 
 
-def head_kernel(s, video, bulk):
-    for p in range(PREV):
-        bulk[p] = video[s.frames - PREV + p]
-
-
-def local_kernel(s, video, bulk, pay, stats, *cols):
+def head_kernel(s, video, early, late):
+    flat = (PREV * s.rows, s.cols, s.chans)
+    sent = video[s.frames - PREV :].reshape(flat)
+    early[...] = sent[: s.early]
+    late[...] = sent[s.early :]
+
+
+def local_kernel(s, video, early, pay, stats, *cols):
     ha, wa = lax.axis_index("ha"), lax.axis_index("wa")
     even = lax.rem(ha, 2) == 0
     means, squares = [], []
@@ -119,9 +121,9 @@
 
 
 def pair_kernel(s, video, stats, got, *refs):
-    cols, refs = refs[: s.ncol], refs[s.ncol :]
-    payy, part = refs[:2]
-    payx, payd = refs[2 : 2 + s.ncol], refs[2 + s.ncol :]
+    cols, refs = refs[: s.ncol], refs[s.ncol + 1 :]
+    _, payy, part = refs[:3]
+    payx, payd = refs[3 : 3 + s.ncol], refs[3 + s.ncol :]
     ha, wa = lax.axis_index("ha"), lax.axis_index("wa")
     even = lax.rem(ha, 2) == 0
     o = s.frames * s.cols
@@ -154,10 +156,9 @@
         payd[0][s.corner : s.corner + s.stats] = terms
 
 
-def edge_kernel(s, part, gain, got, goty, *refs):
+def group_kernel(s, part, gain, goty, *refs):
     gotx, gotd = refs[: s.ncol], refs[s.ncol : 2 * s.ncol]
-    aff, hand, halo, *cols = refs[2 * s.ncol :]
-    even = lax.rem(lax.axis_index("ha"), 2) == 0
+    aff, moved = refs[2 * s.ncol :]
     rows = 2 * s.frames
     count = float(s.rows * s.cols * s.ha * s.wa)
     stat = part[...]
@@ -181,6 +182,15 @@
     scale = lax.rsqrt(var + EPS) * gain[...] * 0.5
     aff[: s.frames] = mean
     aff[s.frames :] = scale
+    first = s.frames - PREV
+    moved[:PREV] = mean[first:]
+    moved[PREV:] = scale[first:]
+
+
+def edge_kernel(s, aff, got, goty, *refs):
+    gotx, gotd = refs[: s.ncol], refs[s.ncol : 2 * s.ncol]
+    hand, halo, *cols = refs[2 * s.ncol :]
+    even = lax.rem(lax.axis_index("ha"), 2) == 0
     first = s.frames - PREV
     at = lax.broadcasted_iota(jnp.int32, (s.colrow, s.chans), 0)
     for f in range(s.frames):
@@ -203,8 +213,6 @@
             if f >= first:
                 o = p + 2 * s.cols + k * s.colrow
                 hand[o : o + s.colrow] = edge
-    o = PREV * s.strip
-    hand[o : o + s.last] = as_terms(jnp.concatenate([mean[first:], scale[first:]], axis=0), s.last)
 
 
 def activation(x, mean, scale, shift):
@@ -218,13 +226,19 @@
     bottom_in = jnp.where(ha < s.ha - 1, 1.0, 0.0).astype(F32)
     left_in = jnp.where(wa > 0, 1.0, 0.0).astype(F32)
     right_in = jnp.where(wa < s.wa - 1, 1.0, 0.0).astype(F32)
-    acts = [activation(e.astype(F32), mean, scale, shift) for e in edges]
-    left, right = acts[0] * left_in, acts[-1] * right_in
+    if edges is not None:
+        acts = [activation(e.astype(F32), mean, scale, shift) for e in edges]
+        left, right = acts[0] * left_in, acts[-1] * right_in
     at = lax.broadcasted_iota(jnp.int32, (s.cols, s.chans), 0)
     for i in range(s.rows + 2):
-        act = activation(raw_row(i).astype(F32), mean, scale, shift)
+        raw = raw_row(i)
+        if raw is None:
+            for dx in range(3):
+                taps[dx, i] = jnp.zeros((s.cols, s.chans), BF16)
+            continue
+        act = activation(raw.astype(F32), mean, scale, shift)
         j = s.rows if i == 0 else s.rows + 1 if i == s.rows + 1 else i - 1
-        lcell, rcell = left[j : j + 1], right[j : j + 1]
+        lcell, rcell = (0.0, 0.0) if edges is None else (left[j : j + 1], right[j : j + 1])
         west = jnp.where(at == 0, lcell, pltpu.roll(act, 1, 0))
         east = jnp.where(at == s.cols - 1, rcell, pltpu.roll(act, s.cols - 1, 0))
         if i in (0, s.rows + 1):
@@ -257,12 +271,13 @@
     return out.astype(BF16).reshape(s.rows, s.cols, s.chans)
 
 
-def put(s, ref, enc, sem, f, skip=0):
+def put(s, ref, enc, sem, f, quarters=range(QUARTERS)):
     step = s.rows // QUARTERS
-    parts = [pl.ds(k * step, step) for k in range(QUARTERS)]
     return [
-        pltpu.make_async_copy(ref.at[f - skip, part], enc.at[f, part], sem.at[f, k])
-        for k, part in enumerate(parts)
+        pltpu.make_async_copy(
+            ref.at[f, pl.ds(k * step, step)], enc.at[f, pl.ds(k * step, step)], sem.at[f, k]
+        )
+        for k in quarters
     ]
 
 
@@ -278,11 +293,11 @@
 
 def own_kernel(s, video, halo, aff, nbias, sw, sb, tw, tb, *refs):
     cols = refs[: s.ncol]
-    enc, last, lead, taps, spatial, out, sem = refs[s.ncol :]
+    enc, base, taps, spatial, out, sem = refs[s.ncol + 1 :]
     shift = nbias[...] * 0.5
     first = lax.axis_index("ta") == 0
 
-    def conv(f):
+    def frame(f, _):
         def raw_row(i):
             if i == 0:
                 return halo[f, 0]
@@ -293,65 +308,160 @@
         edges = [c[pl.ds(f * s.colrow, s.colrow)] for c in cols]
         fill_taps(s, taps, raw_row, edges, aff[pl.ds(f, 1)], aff[pl.ds(s.frames + f, 1)], shift)
         spatial[f] = spatial_dot(s, taps, sw, sb)
+        return _
+
+    lax.fori_loop(0, s.frames, frame, 0)
 
     def encode(f):
         out[f] = temporal_dot(s, [spatial[max(f - k, 0)] for k in range(3)], tw, tb)
         start(put(s, out, enc, sem, f))
 
-    def frame(f, _):
-        conv(f)
-        return _
-
-    lax.fori_loop(0, s.frames, frame, 0)
+    for f in range(PREV, s.frames):
+        encode(f)
 
     @pl.when(first)
     def _():
         for f in range(PREV):
             encode(f)
-
-    for f in range(PREV, s.frames):
-        last[f - PREV] = temporal_dot(s, [spatial[f - k] for k in range(3)], tw, tb)
-    for f in range(PREV):
-        lead[f] = spatial[f]
-
-    @pl.when(first)
+        for f in range(PREV):
+            wait(put(s, out, enc, sem, f))
+
+    @pl.when(jnp.logical_not(first))
     def _():
         for f in range(PREV):
-            wait(put(s, out, enc, sem, f))
-
-
-def prev_kernel(s, bulk, got, nbias, sw, sb, tw, tb, lead, last, _, enc, taps, spatial, out, sem):
+            lhs = jnp.concatenate([spatial[f - k] for k in range(f + 1)], axis=1)
+            weight = tw[: (f + 1) * s.chans]
+            base[f] = jnp.dot(lhs, weight, preferred_element_type=F32) + tb[...]
+
+    for f in range(PREV, s.frames):
+        wait(put(s, out, enc, sem, f))
+
+
+def inner_kernel(s, early, late, moved, nbias, sw, sb, taps, spatial):
     shift = nbias[...] * 0.5
-    for f in range(PREV, s.frames):
-        start(put(s, last, enc, sem, f, PREV))
 
     @pl.when(lax.axis_index("ta") > 0)
     def _():
-        o = PREV * s.strip
-        stat = from_terms(got[o : o + s.last], 2 * PREV)
         for p in range(PREV):
+
+            def raw_row(i):
+                if i == 0 or i == s.rows + 1:
+                    return None
+                r = p * s.rows + i - 1
+                return early[r] if r < s.early else late[r - s.early]
+
+            fill_taps(s, taps.at[p], raw_row, None, moved[p : p + 1], moved[PREV + p : PREV + p + 1], shift)
+            spatial[p] = spatial_dot(s, taps.at[p], sw, sb)
+
+
+def outer_kernel(s, got, moved, taps, spatial, nbias, sw, sb, tw, base, _, enc, grid, out, sem):
+    ha, wa = lax.axis_index("ha"), lax.axis_index("wa")
+    shift = nbias[...] * 0.5
+    inside = [jnp.where(ha > 0, 1.0, 0.0).astype(F32), jnp.where(ha < s.ha - 1, 1.0, 0.0).astype(F32)]
+    at = lax.broadcasted_iota(jnp.int32, (s.cols, s.chans), 0)
+    down = lax.broadcasted_iota(jnp.int32, (s.colrow, s.chans), 0)
+    if s.ncol == 1:
+        sides = [wa == 0]
+        present = [jnp.ones((), F32)]
+    else:
+        sides = [False, True]
+        present = [jnp.where(wa > 0, 1.0, 0.0).astype(F32), jnp.where(wa < s.wa - 1, 1.0, 0.0).astype(F32)]
+
+    @pl.when(lax.axis_index("ta") > 0)
+    def _():
+        lhs = []
+        for p in range(PREV):
+            mean, scale = moved[p : p + 1], moved[PREV + p : PREV + p + 1]
             o = p * s.strip
-
-            def raw_row(i):
-                if i == 0:
-                    return got[o : o + s.cols]
-                if i == s.rows + 1:
-                    return got[o + s.cols : o + 2 * s.cols]
-                return bulk[p, i - 1]
-
-            o2 = o + 2 * s.cols
-            edges = [got[o2 + k * s.colrow : o2 + (k + 1) * s.colrow] for k in range(s.ncol)]
-            fill_taps(s, taps.at[p], raw_row, edges, stat[p : p + 1], stat[PREV + p : PREV + p + 1], shift)
-            spatial[p] = spatial_dot(s, taps.at[p], sw, sb)
-        seq = [spatial[0], spatial[1], lead[0], lead[1]]
+            acts = []
+            for k in range(2):
+                raw = got[o + k * s.cols : o + (k + 1) * s.cols].astype(F32)
+                act = activation(raw, mean, scale, shift) * inside[k]
+                west = jnp.where(at == 0, 0.0, pltpu.roll(act, 1, 0))
+                east = jnp.where(at == s.cols - 1, 0.0, pltpu.roll(act, s.cols - 1, 0))
+                acts.append((west, act, east))
+            top = [a.astype(BF16) for a in acts[0]]
+            bottom = [a.astype(BF16) for a in acts[1]]
+            lhs.append(
+                jnp.concatenate(top + [taps[p, dx, i] for i in (1, 2) for dx in range(3)], axis=1)
+            )
+            n = s.rows
+            lhs.append(
+                jnp.concatenate([taps[p, dx, i] for i in (n - 1, n) for dx in range(3)] + bottom, axis=1)
+            )
+            for k in range(s.ncol):
+                o2 = o + 2 * s.cols + k * s.colrow
+                cell = activation(got[o2 : o2 + s.colrow].astype(F32), mean, scale, shift) * present[k]
+                upper = cell[n : n + 1] * inside[0]
+                lower = cell[n + 1 : n + 2] * inside[1]
+                right = sides[k]
+
+                def end(x):
+                    return jnp.where(right, x[-1:], x[:1])
+
+                def column(d):
+                    rows = []
+                    for i in range(1, n + 1):
+                        tile = taps[p, 1, i].astype(F32)
+                        if d == 0:
+                            rows.append(jnp.where(right, tile[s.cols - 1 :], tile[:1]))
+                        else:
+                            rows.append(jnp.where(right, tile[s.cols - 2 : s.cols - 1], tile[1:2]))
+                    fill = jnp.zeros((s.colrow - n, s.chans), F32)
+                    return jnp.concatenate(rows + [fill], axis=0)
+
+                here, inner = column(0), column(1)
+                far = jnp.where(down < n, cell, 0.0)
+                ends = [
+                    (end(acts[0][1]), end(acts[1][1])),
+                    (
+                        jnp.where(right, acts[0][1][s.cols - 2 : s.cols - 1], acts[0][1][1:2]),
+                        jnp.where(right, acts[1][1][s.cols - 2 : s.cols - 1], acts[1][1][1:2]),
+                    ),
+                    (upper, lower),
+                ]
+                steps = []
+                for dy in range(3):
+                    group = []
+                    for x, (first, final) in zip((here, inner, far), ends):
+                        if dy == 0:
+                            x = jnp.where(down == 0, first, pltpu.roll(x, 1, 0))
+                        elif dy == 2:
+                            x = jnp.where(down == n - 1, final, pltpu.roll(x, s.colrow - 1, 0))
+                        group.append(x)
+                    mid, inn, out_ = group
+                    steps += [jnp.where(right, inn, out_), mid, jnp.where(right, out_, inn)]
+                lhs.append(jnp.concatenate([x.astype(BF16) for x in steps], axis=1))
+        border = jnp.dot(jnp.concatenate(lhs, axis=0), sw[...], preferred_element_type=F32) + sb[...]
+        size = 2 * s.cols + s.ncol * s.colrow
+        tile = 16
+        cells = lax.broadcasted_iota(jnp.int32, (tile, s.chans), 0)
+        for p in range(PREV):
+            o = p * size
+            n = (s.rows - 1) * s.cols
+            grid[p, : s.cols] = border[o : o + s.cols].astype(BF16)
+            grid[p, s.cols : n] = spatial[p, s.cols : n]
+            grid[p, n:] = border[o + s.cols : o + 2 * s.cols].astype(BF16)
+            for k in range(s.ncol):
+                place = jnp.where(sides[k], tile - 1, 0)
+                mask = cells == place
+                for h in range(s.rows):
+                    o2 = o + 2 * s.cols + k * s.colrow + h
+                    at0 = h * s.cols + jnp.where(sides[k], s.cols - tile, 0)
+                    part = pl.ds(pl.multiple_of(at0, tile), tile)
+                    row = jnp.where(mask, border[o2 : o2 + 1], grid[p, part].astype(F32))
+                    grid[p, part] = row.astype(BF16)
+        half = s.rows * s.cols // 2
         for f in range(PREV):
-            out[f] = temporal_dot(s, [seq[PREV + f - k] for k in range(3)], tw, tb)
-            start(put(s, out, enc, sem, f))
+            for k in range(2):
+                part = slice(k * half, (k + 1) * half)
+                lhs = jnp.concatenate([grid[q, part] for q in range(PREV - 1, f - 1, -1)], axis=1)
+                y = jnp.dot(lhs, tw[(f + 1) * s.chans :], preferred_element_type=F32) + base[f, part]
+                block = (s.rows // 2, s.cols, s.chans)
+                out[f, k * block[0] : (k + 1) * block[0]] = y.astype(BF16).reshape(block)
+                start(put(s, out, enc, sem, f, range(k * QUARTERS // 2, (k + 1) * QUARTERS // 2)))
         for f in range(PREV):
             wait(put(s, out, enc, sem, f))
-
-    for f in range(PREV, s.frames):
-        wait(put(s, last, enc, sem, f, PREV))
 
 
 def mates(n, phase):
@@ -374,9 +484,11 @@
     tw = temporal_weight.reshape(3 * c, c)
     gain, nbias, sb, tb = (v.reshape(1, c) for v in (norm_gain, norm_bias, spatial_bias, temporal_bias))
 
-    (bulk,) = call(
+    one = video.shape[1:]
+    late_shape = sd((PREV * s.rows - s.early,) + one[1:], BF16)
+    early, late = call(
         functools.partial(head_kernel, s),
-        [sd((PREV,) + video.shape[1:], BF16)],
+        [sd((s.early,) + one[1:], BF16), late_shape],
         name="head",
         in_specs=[VMEM],
     )(video)
@@ -389,62 +501,77 @@
         [rowpay, stat] + colout,
         name="local",
         in_specs=[VMEM, ANY],
-    )(video, bulk)
-    bulk = lax.ppermute(bulk, "ta", ring)
+    )(video, early)
+    early = lax.ppermute(early, "ta", ring)
     got1 = lax.ppermute(pay, "ha", mates(nha, 0))
-    payy, part, *pays = call(
+    late, payy, part, *pays = call(
         functools.partial(pair_kernel, s),
-        [rowpay, stat]
+        [late_shape, rowpay, stat]
         + [sd((s.frames * s.colrow + riding, c), BF16)] * s.ncol
         + [sd((s.corner + riding, c), BF16)] * s.ncol,
+        out_specs=[ANY] + [VMEM] * (2 + 2 * s.ncol),
         name="pair",
-        in_specs=[VMEM] * (3 + s.ncol),
-    )(video, stats, got1, *cols)
+        in_specs=[VMEM] * (3 + s.ncol) + [ANY],
+        input_output_aliases={3 + s.ncol: 0},
+    )(video, stats, got1, *cols, late)
     outer = mates(nha, 1)
     diagonal = [[(h * nwa + w, g * nwa + v) for h, g in outer for w, v in p] for p in sides]
     goty = lax.ppermute(payy, "ha", outer)
     gotx = [lax.ppermute(x, "wa", p) for x, p in zip(pays[: s.ncol], sides)]
     gotd = [lax.ppermute(x, ("ha", "wa"), p) for x, p in zip(pays[s.ncol :], diagonal)]
+    late = lax.ppermute(late, "ta", ring[:-1])
     if not s.fused:
         every = lax.all_gather(stats, ("ha", "wa"))
         part = merge(float(s.rows * s.cols), [every[i] for i in range(nha * nwa)])
-    aff, hand, halo, *cols = call(
+    aff, moved = call(
+        functools.partial(group_kernel, s),
+        [stat, sd((2 * PREV, c), F32)],
+        name="group",
+        in_specs=[VMEM] * (3 + 2 * s.ncol),
+    )(part, gain, goty, *gotx, *gotd)
+    moved = lax.ppermute(moved, "ta", ring)
+    hand, halo, *cols = call(
         functools.partial(edge_kernel, s),
-        [stat, sd((PREV * s.strip + s.last, c), BF16), sd((s.frames, 2, s.cols, c), BF16)] + colout,
+        [sd((PREV * s.strip, c), BF16), sd((s.frames, 2, s.cols, c), BF16)] + colout,
         name="edge",
-        in_specs=[VMEM] * (4 + 2 * s.ncol),
-    )(part, gain, got1, goty, *gotx, *gotd)
+        in_specs=[VMEM] * (3 + 2 * s.ncol),
+    )(aff, got1, goty, *gotx, *gotd)
     got = lax.ppermute(hand, "ta", ring)
     frame = (s.rows * s.cols, c)
     taps = (3, s.rows + 2, s.cols, c)
-    one = video.shape[1:]
-    enc, last, lead = call(
+    enc, base = call(
         functools.partial(own_kernel, s),
-        [sd(video.shape, BF16), sd((s.frames - PREV,) + one, BF16), sd((PREV,) + frame, BF16)],
-        out_specs=[ANY, VMEM, VMEM],
+        [sd(video.shape, BF16), sd((PREV,) + frame, F32)],
+        out_specs=[ANY, VMEM],
         scratch=[
             pltpu.VMEM(taps, BF16),
             pltpu.VMEM((s.frames,) + frame, BF16),
+            pltpu.VMEM((s.frames,) + one, BF16),
+            pltpu.SemaphoreType.DMA((s.frames, QUARTERS)),
+        ],
+        flops=2 * s.rows * s.cols * c * c * (9 * s.frames + 3 * (s.frames - PREV)),
+        name="own",
+        in_specs=[VMEM] * (8 + s.ncol) + [ANY],
+    )(video, halo, aff, nbias, sw, sb, tw, tb, *cols, early)
+    grid, inner = call(
+        functools.partial(inner_kernel, s),
+        [sd((PREV,) + taps, BF16), sd((PREV,) + frame, BF16)],
+        name="inner",
+        in_specs=[VMEM] * 6,
+    )(early, late, moved, nbias, sw, sb)
+    (enc,) = call(
+        functools.partial(outer_kernel, s),
+        [sd(video.shape, BF16)],
+        out_specs=[ANY],
+        scratch=[
+            pltpu.VMEM((PREV,) + frame, BF16),
             pltpu.VMEM((PREV,) + one, BF16),
             pltpu.SemaphoreType.DMA((PREV, QUARTERS)),
         ],
-        name="own",
-        in_specs=[VMEM] * (8 + s.ncol),
-    )(video, halo, aff, nbias, sw, sb, tw, tb, *cols)
-    (enc,) = call(
-        functools.partial(prev_kernel, s),
-        [sd(video.shape, BF16)],
-        out_specs=[ANY],
-        scratch=[
-            pltpu.VMEM((PREV,) + taps, BF16),
-            pltpu.VMEM((PREV,) + frame, BF16),
-            pltpu.VMEM((PREV,) + one, BF16),
-            pltpu.SemaphoreType.DMA((s.frames, QUARTERS)),
-        ],
-        name="prev",
+        name="outer",
         in_specs=[VMEM] * 9 + [ANY],
         input_output_aliases={9: 0},
-    )(bulk, got, nbias, sw, sb, tw, tb, lead, last, enc)
+    )(got, moved, grid, inner, nbias, sw, sb, tw, base, enc)
     return enc
 
 

time: 27.6 us -> 26.5 us (0.960)
  the two profiles are of different devices: /device:TPU:0 before, /device:TPU:28 now
where the time goes in v3:
time: 26.5 us; the launch traced here: 26.4 us
  Pallas kernels  12 us (45%)
  starting transfers between devices  8.17 us (31%)
  waiting for transfers between devices  4.61 us (17%)
  local copies, waits for them, and re-layouts  1.45 us (5%)
    pallas_call x1, Pallas kernels, local(): call(functools.partial(own_kernel, s), [sd(video.shape, BF16), sd((PREV,)...  6.41 us
    pallas_call x1, Pallas kernels, local(): call(functools.partial(outer_kernel, s), [sd(video.shape, BF16)], out_spe...  2.27 us
    pallas_call x1, Pallas kernels, local(): call(functools.partial(inner_kernel, s), [sd((PREV,) + taps, BF16), sd((P...  2.14 us
    ppermute x1, starting transfers between devices, local(): moved = lax.ppermute(moved, 'ta', ring)  1.94 us
    ppermute x1, waiting for transfers between devices, local(): lax.ppermute(x, ('ha', 'wa'), p)  1.93 us
    ppermute x1, starting transfers between devices, local(): gotx = [lax.ppermute(x, 'wa', p) for x, p in zip(pays[:s.ncol], sides)]  1.68 us
    ppermute x1, starting transfers between devices, local(): got = lax.ppermute(hand, 'ta', ring)  1.61 us
    unnamed x16, local copies, waits for them, and re-layouts  1.45 us
  transfers between devices with their start and end apart: 8, of which 4 were waited for; matrix products, arithmetic and copies ran while one was open for 0% of the time, Pallas kernels for 37%

profile of v3, /device:TPU:28, one launch (start us, length us, event | category | flops | bytes accessed | tf_op | source)
XLA Modules:
  0.0 26.4 jit_solution(7747078614966107375)
XLA Ops:
  0.0 1.4 %copy-done = bf16[4,24,32,256]{3,2,1,0:T(8,128)(2,1)S(1)} copy-done((bf16[4,24,32,256]{3,2,1,0:T(8,128)(2,1)S(1)}, bf16[4,24,32,256]{3,2,1,0:T(8,128)(2,1)}, u32[]{:S(2)}) %copy-start) | copy-done | bytes 1572888
  1.4 0.1 head.1
  1.5 0.0 copy-start.6
  1.5 0.3 %collective-permute-start.6 = (bf16[26,32,256]{2,1,0:T(8,128)(2,1)S(1)}, bf16[26,32,256]{2,1,0:T(8,128)(2,1)S(1)}, u32[]{:S(2)}, u32[]{:S(2)}) collective-permute-start(bf16[26,32,256]{2,1,0:T(8,128)(2,1)S(1)} %get-tuple-element.24.early), channel_id=1, source_target_pairs={{0,1},{1,2},{2,3},{3,0},{4,5},{5,6},{6,7},{7,4},{8,9},{9,10},{10,1... | collective-permute-start | bytes 1277960 | tf_op jit(solution)/shard_map/ppermute | solution.py:505
  1.8 0.7 %local.1 = (bf16[160,256]{1,0:T(8,128)(2,1)S(1)}, f32[8,256]{1,0:T(8,128)S(1)}, bf16[128,256]{1,0:T(8,128)(2,1)S(1)}) custom-call(bf16[4,24,32,256]{3,2,1,0:T(8,128)(2,1)S(1)} %copy-done, bf16[26,32,256]{2,1,0:T(8,128)(2,1)S(1)} %get-tuple-element.24.early), custom_call_target="tpu_custom_call" | custom-call | flops 1024 | bytes 1024 | tf_op jit(solution)/shard_map/local/pallas_call | solution.py:499
  2.5 0.0 copy-start.3
  2.5 0.0 copy-start.4
  2.5 0.0 copy-start.5
  2.5 0.0 copy-start.7
  2.6 0.1 collective-permute-start
  2.6 1.3 %collective-permute-done.got = bf16[160,256]{1,0:T(8,128)(2,1)S(1)} collective-permute-done((bf16[160,256]{1,0:T(8,128)(2,1)S(1)}, bf16[160,256]{1,0:T(8,128)(2,1)S(1)}, u32[]{:S(2)}, u32[]{:S(2)}) %collective-permute-start) | collective-permute-done | bytes 81952 | tf_op jit(solution)/shard_map/ppermute | solution.py:506
  4.0 0.1 collective-permute-start.1
  4.1 1.7 %collective-permute-start.2 = (bf16[160,256]{1,0:T(8,128)(2,1)S(1)}, bf16[160,256]{1,0:T(8,128)(2,1)S(1)}, u32[]{:S(2)}, u32[]{:S(2)}) collective-permute-start(bf16[160,256]{1,0:T(8,128)(2,1)S(1)} %get-tuple-element.31), channel_id=1, source_target_pairs={{0,4},{4,0},{1,5},{5,1},{2,6},{6,2},{3,7},{7,3},{8,12},{12,8},{9,1... | collective-permute-start | bytes 245768 | tf_op jit(solution)/shard_map/ppermute | solution.py:520
  5.8 1.2 %collective-permute-start.3 = (bf16[48,256]{1,0:T(8,128)(2,1)S(1)}, bf16[48,256]{1,0:T(8,128)(2,1)S(1)}, u32[]{:S(2)}, u32[]{:S(2)}) collective-permute-start(bf16[48,256]{1,0:T(8,128)(2,1)S(1)} %get-tuple-element.32), channel_id=1, source_target_pairs={{0,28},{4,24},{8,20},{12,16},{16,12},{20,8},{24,4},{28,0},{1,29},{... | collective-permute-start | bytes 73736 | tf_op jit(solution)/shard_map/ppermute | solution.py:521
  6.9 1.3 %collective-permute-start.7 = (bf16[22,32,256]{2,1,0:T(8,128)(2,1)S(1)}, bf16[22,32,256]{2,1,0:T(8,128)(2,1)S(1)}, u32[]{:S(2)}, u32[]{:S(2)}) collective-permute-start(bf16[22,32,256]{2,1,0:T(8,128)(2,1)S(1)} %get-tuple-element.36), channel_id=1, source_target_pairs={{0,1},{1,2},{2,3},{4,5},{5,6},{6,7},{8,9},{9,10},{10,11},{12,13},{... | collective-permute-start | bytes 1081352 | tf_op jit(solution)/shard_map/ppermute | solution.py:522
  8.2 1.9 %collective-permute-done.3.refs_1_ = bf16[48,256]{1,0:T(8,128)(2,1)S(1)} collective-permute-done((bf16[48,256]{1,0:T(8,128)(2,1)S(1)}, bf16[48,256]{1,0:T(8,128)(2,1)S(1)}, u32[]{:S(2)}, u32[]{:S(2)}) %collective-permute-start.3) | collective-permute-done | bytes 24608 | tf_op jit(solution)/shard_map/ppermute | solution.py:521
  10.2 0.0 collective-permute-done.1.goty
  10.2 0.0 collective-permute-done.2.refs_0_
  10.2 0.3 %group.1 = (f32[8,256]{1,0:T(8,128)S(1)}, f32[4,256]{1,0:T(4,128)S(1)}) custom-call(f32[8,256]{1,0:T(8,128)S(1)} %get-tuple-element.29.part, f32[1,256]{1,0:T(1,128)S(1)} %bitcast.17, bf16[160,256]{1,0:T(8,128)(2,1)S(1)} %collective-permute-done.1.goty, bf16[160,256]{1,0:T(8,128)(2,1)S(1)} %collective-permute-done.2.refs_0_, ...), custom_call_target="tpu_custom_call" | custom-call | flops 1024 | bytes 1024 | tf_op jit(solution)/shard_map/group/pallas_call | solution.py:526
  10.5 1.9 %collective-permute-start.5 = (f32[4,256]{1,0:T(4,128)S(1)}, f32[4,256]{1,0:T(4,128)S(1)}, u32[]{:S(2)}, u32[]{:S(2)}) collective-permute-start(f32[4,256]{1,0:T(4,128)S(1)} %get-tuple-element.35), channel_id=1, source_target_pairs={{0,1},{1,2},{2,3},{3,0},{4,5},{5,6},{6,7},{7,4},{8,9},{9,10},{10,1... | collective-permute-start | bytes 12296 | tf_op jit(solution)/shard_map/ppermute | solution.py:532
  12.4 0.1 edge.1
  12.5 1.6 %collective-permute-start.4 = (bf16[192,256]{1,0:T(8,128)(2,1)S(1)}, bf16[192,256]{1,0:T(8,128)(2,1)S(1)}, u32[]{:S(2)}, u32[]{:S(2)}) collective-permute-start(bf16[192,256]{1,0:T(8,128)(2,1)S(1)} %get-tuple-element.34), channel_id=1, source_target_pairs={{0,1},{1,2},{2,3},{3,0},{4,5},{5,6},{6,7},{7,4},{8,9},{9,10},{10,1... | collective-permute-start | bytes 294920 | tf_op jit(solution)/shard_map/ppermute | solution.py:539
  14.1 0.1 collective-permute-done.6.early.refs_1_
  14.2 0.0 copy-done.3
  14.2 0.0 copy-done.4
  14.3 0.0 copy-done.5
  14.3 6.4 %own.1 = (bf16[4,24,32,256]{3,2,1,0:T(8,128)(2,1)}, f32[2,768,256]{2,1,0:T(8,128)S(1)}) custom-call(bf16[4,24,32,256]{3,2,1,0:T(8,128)(2,1)S(1)} %copy-done.1, bf16[4,2,32,256]{3,2,1,0:T(8,128)(2,1)S(1)} %get-tuple-element.39.halo, f32[8,256]{1,0:T(8,128)S(1)} %get-tuple-element.33.aff, f32[1,256]{1,0:T(1,128)S(1)} %bitcast.11, ...), custom_call_target="tpu_custom_call" | custom-call | flops 4227858432 | bytes 1024 | tf_op jit(solution)/shard_map/own/pallas_call | solution.py:542
  20.7 1.3 %collective-permute-done.5.moved = f32[4,256]{1,0:T(4,128)S(1)} collective-permute-done((f32[4,256]{1,0:T(4,128)S(1)}, f32[4,256]{1,0:T(4,128)S(1)}, u32[]{:S(2)}, u32[]{:S(2)}) %collective-permute-start.5) | collective-permute-done | bytes 4128 | tf_op jit(solution)/shard_map/ppermute | solution.py:532
  22.0 0.0 collective-permute-done.7.late
  22.0 2.1 %inner.1 = (bf16[2,3,26,32,256]{4,3,2,1,0:T(8,128)(2,1)S(1)}, bf16[2,768,256]{2,1,0:T(8,128)(2,1)S(1)}) custom-call(bf16[26,32,256]{2,1,0:T(8,128)(2,1)S(1)} %collective-permute-done.6.early.refs_1_, bf16[22,32,256]{2,1,0:T(8,128)(2,1)S(1)} %collective-permute-done.7.late, f32[4,256]{1,0:T(4,128)S(1)} %collective-permute-done.5.moved, ...), custom_call_target="tpu_custom_call" | custom-call | flops 1024 | bytes 1024 | tf_op jit(solution)/shard_map/inner/pallas_call | solution.py:556
  24.1 0.0 collective-permute-done.4.got
  24.1 2.3 %outer.1 = bf16[4,24,32,256]{3,2,1,0:T(8,128)(2,1)} custom-call(bf16[192,256]{1,0:T(8,128)(2,1)S(1)} %collective-permute-done.4.got, f32[4,256]{1,0:T(4,128)S(1)} %collective-permute-done.5.moved, bf16[2,3,26,32,256]{4,3,2,1,0:T(8,128)(2,1)S(1)} %get-tuple-element.37.taps, ...), custom_call_target="tpu_custom_call", output_to_operand_aliasing={{}: (9, {})} | custom-call | flops 1024 | bytes 1024 | tf_op jit(solution)/shard_map/outer/pallas_call | solution.py:562
  (8 shorter events, 0.1 us)
Async XLA Ops:
  0.0 1.4 %copy-start = (bf16[4,24,32,256]{3,2,1,0:T(8,128)(2,1)S(1)}, bf16[4,24,32,256]{3,2,1,0:T(8,128)(2,1)}, u32[]{:S(2)}) copy-start(bf16[4,24,32,256]{3,2,1,0:T(8,128)(2,1)} %video.7) | copy-start | bytes 4718596
  1.5 8.7 %copy-start.6 = (f32[256]{0:T(256)S(1)}, f32[256]{0:T(256)}, u32[]{:S(2)}) copy-start(f32[256]{0:T(256)} %param.8) | copy-start | bytes 3076
  1.5 12.8 %collective-permute-start.6 = (bf16[26,32,256]{2,1,0:T(8,128)(2,1)S(1)}, bf16[26,32,256]{2,1,0:T(8,128)(2,1)S(1)}, u32[]{:S(2)}, u32[]{:S(2)}) collective-permute-start(bf16[26,32,256]{2,1,0:T(8,128)(2,1)S(1)} %get-tuple-element.24.early), channel_id=1, source_target_pairs={{0,1},{1,2},{2,3},{3,0},{4,5},{5,6},{6,7},{7,4},{8,9},{9,10},{10,1... | collective-permute-start | bytes 1277960 | tf_op jit(solution)/shard_map/ppermute | solution.py:505
  1.8 12.5 %copy-start.2 = (bf16[3,3,256,256]{3,2,1,0:T(8,128)(2,1)S(1)}, bf16[3,3,256,256]{3,2,1,0:T(8,128)(2,1)}, u32[]{:S(2)}) copy-start(bf16[3,3,256,256]{3,2,1,0:T(8,128)(2,1)} %param.10) | copy-start | bytes 3538948
  2.5 11.7 %copy-start.1 = (bf16[4,24,32,256]{3,2,1,0:T(8,128)(2,1)S(1)}, bf16[4,24,32,256]{3,2,1,0:T(8,128)(2,1)}, u32[]{:S(2)}) copy-start(bf16[4,24,32,256]{3,2,1,0:T(8,128)(2,1)} %video.7) | copy-start | bytes 4718596
  2.5 11.7 %copy-start.3 = (bf16[3,256,256]{2,1,0:T(8,128)(2,1)S(1)}, bf16[3,256,256]{2,1,0:T(8,128)(2,1)}, u32[]{:S(2)}) copy-start(bf16[3,256,256]{2,1,0:T(8,128)(2,1)} %param.12) | copy-start | bytes 1179652
  2.5 11.7 %copy-start.4 = (f32[256]{0:T(256)S(1)}, f32[256]{0:T(256)}, u32[]{:S(2)}) copy-start(f32[256]{0:T(256)} %param.9) | copy-start | bytes 3076
  2.5 11.7 %copy-start.5 = (f32[256]{0:T(256)S(1)}, f32[256]{0:T(256)}, u32[]{:S(2)}) copy-start(f32[256]{0:T(256)} %param.11) | copy-start | bytes 3076
  2.5 11.7 %copy-start.7 = (f32[256]{0:T(256)S(1)}, f32[256]{0:T(256)}, u32[]{:S(2)}) copy-start(f32[256]{0:T(256)} %param.13) | copy-start | bytes 3076
  2.6 1.3 %collective-permute-start = (bf16[160,256]{1,0:T(8,128)(2,1)S(1)}, bf16[160,256]{1,0:T(8,128)(2,1)S(1)}, u32[]{:S(2)}, u32[]{:S(2)}) collective-permute-start(bf16[160,256]{1,0:T(8,128)(2,1)S(1)} %get-tuple-element.26), channel_id=1, source_target_pairs={{0,8},{8,0},{16,24},{24,16},{1,9},{9,1},{17,25},{25,17},{2,10},{10... | collective-permute-start | bytes 245768 | tf_op jit(solution)/shard_map/ppermute | solution.py:506
  4.0 6.2 %collective-permute-start.1 = (bf16[160,256]{1,0:T(8,128)(2,1)S(1)}, bf16[160,256]{1,0:T(8,128)(2,1)S(1)}, u32[]{:S(2)}, u32[]{:S(2)}) collective-permute-start(bf16[160,256]{1,0:T(8,128)(2,1)S(1)} %get-tuple-element.30), channel_id=1, source_target_pairs={{0,24},{8,16},{16,8},{24,0},{1,25},{9,17},{17,9},{25,1},{2,26},{10... | collective-permute-start | bytes 245768 | tf_op jit(solution)/shard_map/ppermute | solution.py:519
  4.1 6.1 %collective-permute-start.2 = (bf16[160,256]{1,0:T(8,128)(2,1)S(1)}, bf16[160,256]{1,0:T(8,128)(2,1)S(1)}, u32[]{:S(2)}, u32[]{:S(2)}) collective-permute-start(bf16[160,256]{1,0:T(8,128)(2,1)S(1)} %get-tuple-element.31), channel_id=1, source_target_pairs={{0,4},{4,0},{1,5},{5,1},{2,6},{6,2},{3,7},{7,3},{8,12},{12,8},{9,1... | collective-permute-start | bytes 245768 | tf_op jit(solution)/shard_map/ppermute | solution.py:520
  5.8 4.4 %collective-permute-start.3 = (bf16[48,256]{1,0:T(8,128)(2,1)S(1)}, bf16[48,256]{1,0:T(8,128)(2,1)S(1)}, u32[]{:S(2)}, u32[]{:S(2)}) collective-permute-start(bf16[48,256]{1,0:T(8,128)(2,1)S(1)} %get-tuple-element.32), channel_id=1, source_target_pairs={{0,28},{4,24},{8,20},{12,16},{16,12},{20,8},{24,4},{28,0},{1,29},{... | collective-permute-start | bytes 73736 | tf_op jit(solution)/shard_map/ppermute | solution.py:521
  6.9 15.0 %collective-permute-start.7 = (bf16[22,32,256]{2,1,0:T(8,128)(2,1)S(1)}, bf16[22,32,256]{2,1,0:T(8,128)(2,1)S(1)}, u32[]{:S(2)}, u32[]{:S(2)}) collective-permute-start(bf16[22,32,256]{2,1,0:T(8,128)(2,1)S(1)} %get-tuple-element.36), channel_id=1, source_target_pairs={{0,1},{1,2},{2,3},{4,5},{5,6},{6,7},{8,9},{9,10},{10,11},{12,13},{... | collective-permute-start | bytes 1081352 | tf_op jit(solution)/shard_map/ppermute | solution.py:522
  10.5 11.5 %collective-permute-start.5 = (f32[4,256]{1,0:T(4,128)S(1)}, f32[4,256]{1,0:T(4,128)S(1)}, u32[]{:S(2)}, u32[]{:S(2)}) collective-permute-start(f32[4,256]{1,0:T(4,128)S(1)} %get-tuple-element.35), channel_id=1, source_target_pairs={{0,1},{1,2},{2,3},{3,0},{4,5},{5,6},{6,7},{7,4},{8,9},{9,10},{10,1... | collective-permute-start | bytes 12296 | tf_op jit(solution)/shard_map/ppermute | solution.py:532
  12.5 11.6 %collective-permute-start.4 = (bf16[192,256]{1,0:T(8,128)(2,1)S(1)}, bf16[192,256]{1,0:T(8,128)(2,1)S(1)}, u32[]{:S(2)}, u32[]{:S(2)}) collective-permute-start(bf16[192,256]{1,0:T(8,128)(2,1)S(1)} %get-tuple-element.34), channel_id=1, source_target_pairs={{0,1},{1,2},{2,3},{3,0},{4,5},{5,6},{6,7},{7,4},{8,9},{9,10},{10,1... | collective-permute-start | bytes 294920 | tf_op jit(solution)/shard_map/ppermute | solution.py:539

commit v4 on v3

--- a/solution.py
+++ b/solution.py
@@ -66,6 +66,8 @@
         self.strip = 2 * self.cols + self.ncol * self.colrow
         self.stats = pad_to(3 * 2 * self.frames, 16)
         self.early = (PREV - 1) * self.rows + self.rows // 12
+        self.tail = self.rows // 4 + 1
+        self.late = PREV * self.rows - self.early - self.tail
         self.corner = pad_to(self.frames, 16)
 
 
@@ -73,7 +75,7 @@
     flat = (PREV * s.rows, s.cols, s.chans)
     sent = video[s.frames - PREV :].reshape(flat)
     early[...] = sent[: s.early]
-    late[...] = sent[s.early :]
+    late[...] = sent[s.early : s.early + s.late]
 
 
 def local_kernel(s, video, early, pay, stats, *cols):
@@ -187,11 +189,14 @@
     moved[PREV:] = scale[first:]
 
 
-def edge_kernel(s, aff, got, goty, *refs):
+def edge_kernel(s, aff, video, got, goty, *refs):
     gotx, gotd = refs[: s.ncol], refs[s.ncol : 2 * s.ncol]
     hand, halo, *cols = refs[2 * s.ncol :]
     even = lax.rem(lax.axis_index("ha"), 2) == 0
     first = s.frames - PREV
+    o = PREV * s.strip
+    rest = video[s.frames - 1, s.rows - s.tail :]
+    hand[o : o + s.tail * s.cols] = rest.reshape(s.tail * s.cols, s.chans)
     at = lax.broadcasted_iota(jnp.int32, (s.colrow, s.chans), 0)
     for f in range(s.frames):
         p = (f - first) * s.strip
@@ -249,10 +254,11 @@
         taps[2, i] = east.astype(BF16)
 
 
-def spatial_dot(s, taps, weight, bias):
-    step = s.rows // DOTS
+def spatial_dot(s, taps, weight, bias, rows):
+    size = s.rows // DOTS
     done = []
-    for r in range(0, s.rows, step):
+    for r in range(0, rows, size):
+        step = min(size, rows - r)
         lhs = jnp.concatenate(
             [
                 taps[dx, r + dy : r + dy + step].reshape(step * s.cols, s.chans)
@@ -307,7 +313,7 @@
 
         edges = [c[pl.ds(f * s.colrow, s.colrow)] for c in cols]
         fill_taps(s, taps, raw_row, edges, aff[pl.ds(f, 1)], aff[pl.ds(s.frames + f, 1)], shift)
-        spatial[f] = spatial_dot(s, taps, sw, sb)
+        spatial[f] = spatial_dot(s, taps, sw, sb, s.rows)
         return _
 
     lax.fori_loop(0, s.frames, frame, 0)
@@ -337,7 +343,7 @@
         wait(put(s, out, enc, sem, f))
 
 
-def inner_kernel(s, early, late, moved, nbias, sw, sb, taps, spatial):
+def inner_kernel(s, early, late, moved, nbias, sw, sb, base, taps, spatial):
     shift = nbias[...] * 0.5
 
     @pl.when(lax.axis_index("ta") > 0)
@@ -348,13 +354,16 @@
                 if i == 0 or i == s.rows + 1:
                     return None
                 r = p * s.rows + i - 1
+                if r >= s.early + s.late:
+                    return None
                 return early[r] if r < s.early else late[r - s.early]
 
             fill_taps(s, taps.at[p], raw_row, None, moved[p : p + 1], moved[PREV + p : PREV + p + 1], shift)
-            spatial[p] = spatial_dot(s, taps.at[p], sw, sb)
-
-
-def outer_kernel(s, got, moved, taps, spatial, nbias, sw, sb, tw, base, _, enc, grid, out, sem):
+            rows = s.rows if p < PREV - 1 else s.rows - s.tail - 1
+            spatial[p, : rows * s.cols] = spatial_dot(s, taps.at[p], sw, sb, rows)
+
+
+def outer_kernel(s, got, moved, taps, spatial, nbias, sw, sb, tw, base, _, enc, more, grid, out, sem):
     ha, wa = lax.axis_index("ha"), lax.axis_index("wa")
     shift = nbias[...] * 0.5
     inside = [jnp.where(ha > 0, 1.0, 0.0).astype(F32), jnp.where(ha < s.ha - 1, 1.0, 0.0).astype(F32)]
@@ -370,6 +379,25 @@
     @pl.when(lax.axis_index("ta") > 0)
     def _():
         lhs = []
+        start_row = s.rows - s.tail - 1
+        end = PREV - 1
+
+        def tap(p, dx, i):
+            return more[dx, i - start_row] if p == end and i >= start_row else taps[p, dx, i]
+
+        def shifted(act):
+            west = jnp.where(at == 0, 0.0, pltpu.roll(act, 1, 0))
+            east = jnp.where(at == s.cols - 1, 0.0, pltpu.roll(act, s.cols - 1, 0))
+            return [x.astype(BF16) for x in (west, act, east)]
+
+        for dx in range(3):
+            more[dx, :2] = taps[end, dx, start_row : start_row + 2]
+        for i in range(s.tail):
+            o = PREV * s.strip + i * s.cols
+            raw = got[o : o + s.cols].astype(F32)
+            act = activation(raw, moved[end : end + 1], moved[PREV + end : PREV + end + 1], shift)
+            for dx, x in enumerate(shifted(act)):
+                more[dx, 2 + i] = x
         for p in range(PREV):
             mean, scale = moved[p : p + 1], moved[PREV + p : PREV + p + 1]
             o = p * s.strip
@@ -377,17 +405,14 @@
             for k in range(2):
                 raw = got[o + k * s.cols : o + (k + 1) * s.cols].astype(F32)
                 act = activation(raw, mean, scale, shift) * inside[k]
-                west = jnp.where(at == 0, 0.0, pltpu.roll(act, 1, 0))
-                east = jnp.where(at == s.cols - 1, 0.0, pltpu.roll(act, s.cols - 1, 0))
-                acts.append((west, act, east))
-            top = [a.astype(BF16) for a in acts[0]]
-            bottom = [a.astype(BF16) for a in acts[1]]
+                acts.append(act)
+            top, bottom = shifted(acts[0]), shifted(acts[1])
             lhs.append(
-                jnp.concatenate(top + [taps[p, dx, i] for i in (1, 2) for dx in range(3)], axis=1)
+                jnp.concatenate(top + [tap(p, dx, i) for i in (1, 2) for dx in range(3)], axis=1)
             )
             n = s.rows
             lhs.append(
-                jnp.concatenate([taps[p, dx, i] for i in (n - 1, n) for dx in range(3)] + bottom, axis=1)
+                jnp.concatenate([tap(p, dx, i) for i in (n - 1, n) for dx in range(3)] + bottom, axis=1)
             )
             for k in range(s.ncol):
                 o2 = o + 2 * s.cols + k * s.colrow
@@ -396,13 +421,10 @@
                 lower = cell[n + 1 : n + 2] * inside[1]
                 right = sides[k]
 
-                def end(x):
-                    return jnp.where(right, x[-1:], x[:1])
-
                 def column(d):
                     rows = []
                     for i in range(1, n + 1):
-                        tile = taps[p, 1, i].astype(F32)
+                        tile = tap(p, 1, i).astype(F32)
                         if d == 0:
                             rows.append(jnp.where(right, tile[s.cols - 1 :], tile[:1]))
                         else:
@@ -413,11 +435,8 @@
                 here, inner = column(0), column(1)
                 far = jnp.where(down < n, cell, 0.0)
                 ends = [
-                    (end(acts[0][1]), end(acts[1][1])),
-                    (
-                        jnp.where(right, acts[0][1][s.cols - 2 : s.cols - 1], acts[0][1][1:2]),
-                        jnp.where(right, acts[1][1][s.cols - 2 : s.cols - 1], acts[1][1][1:2]),
-                    ),
+                    tuple(jnp.where(right, a[s.cols - 1 :], a[:1]) for a in acts),
+                    tuple(jnp.where(right, a[s.cols - 2 : s.cols - 1], a[1:2]) for a in acts),
                     (upper, lower),
                 ]
                 steps = []
@@ -432,6 +451,17 @@
                     mid, inn, out_ = group
                     steps += [jnp.where(right, inn, out_), mid, jnp.where(right, out_, inn)]
                 lhs.append(jnp.concatenate([x.astype(BF16) for x in steps], axis=1))
+        fresh = s.tail * s.cols
+        lhs.append(
+            jnp.concatenate(
+                [
+                    more[dx, dy : dy + s.tail].reshape(fresh, s.chans)
+                    for dy in range(3)
+                    for dx in range(3)
+                ],
+                axis=1,
+            )
+        )
         border = jnp.dot(jnp.concatenate(lhs, axis=0), sw[...], preferred_element_type=F32) + sb[...]
         size = 2 * s.cols + s.ncol * s.colrow
         tile = 16
@@ -440,7 +470,10 @@
             o = p * size
             n = (s.rows - 1) * s.cols
             grid[p, : s.cols] = border[o : o + s.cols].astype(BF16)
-            grid[p, s.cols : n] = spatial[p, s.cols : n]
+            m = n if p < end else start_row * s.cols
+            grid[p, s.cols : m] = spatial[p, s.cols : m]
+            if p == end:
+                grid[p, m : m + fresh] = border[PREV * size : PREV * size + fresh].astype(BF16)
             grid[p, n:] = border[o + s.cols : o + 2 * s.cols].astype(BF16)
             for k in range(s.ncol):
                 place = jnp.where(sides[k], tile - 1, 0)
@@ -485,7 +518,7 @@
     gain, nbias, sb, tb = (v.reshape(1, c) for v in (norm_gain, norm_bias, spatial_bias, temporal_bias))
 
     one = video.shape[1:]
-    late_shape = sd((PREV * s.rows - s.early,) + one[1:], BF16)
+    late_shape = sd((s.late,) + one[1:], BF16)
     early, late = call(
         functools.partial(head_kernel, s),
         [sd((s.early,) + one[1:], BF16), late_shape],
@@ -532,10 +565,10 @@
     moved = lax.ppermute(moved, "ta", ring)
     hand, halo, *cols = call(
         functools.partial(edge_kernel, s),
-        [sd((PREV * s.strip, c), BF16), sd((s.frames, 2, s.cols, c), BF16)] + colout,
+        [sd((PREV * s.strip + s.tail * s.cols, c), BF16), sd((s.frames, 2, s.cols, c), BF16)] + colout,
         name="edge",
-        in_specs=[VMEM] * (3 + 2 * s.ncol),
-    )(aff, got1, goty, *gotx, *gotd)
+        in_specs=[VMEM] * (4 + 2 * s.ncol),
+    )(aff, video, got1, goty, *gotx, *gotd)
     got = lax.ppermute(hand, "ta", ring)
     frame = (s.rows * s.cols, c)
     taps = (3, s.rows + 2, s.cols, c)
@@ -557,13 +590,14 @@
         functools.partial(inner_kernel, s),
         [sd((PREV,) + taps, BF16), sd((PREV,) + frame, BF16)],
         name="inner",
-        in_specs=[VMEM] * 6,
-    )(early, late, moved, nbias, sw, sb)
+        in_specs=[VMEM] * 6 + [ANY],
+    )(early, late, moved, nbias, sw, sb, base)
     (enc,) = call(
         functools.partial(outer_kernel, s),
         [sd(video.shape, BF16)],
         out_specs=[ANY],
         scratch=[
+            pltpu.VMEM((3, s.tail + 2) + one[1:], BF16),
             pltpu.VMEM((PREV,) + frame, BF16),
             pltpu.VMEM((PREV,) + one, BF16),
             pltpu.SemaphoreType.DMA((PREV, QUARTERS)),

time: 26.5 us -> 25.9 us (0.977)
  the two profiles are of different devices: /device:TPU:28 before, /device:TPU:16 now
where the time goes in v4:
time: 25.9 us; the launch traced here: 25.8 us
  Pallas kernels  12.1 us (47%)
  starting transfers between devices  8.62 us (33%)
  waiting for transfers between devices  3.47 us (13%)
  local copies, waits for them, and re-layouts  1.44 us (6%)
    pallas_call x1, Pallas kernels, local(): call(functools.partial(own_kernel, s), [sd(video.shape, BF16), sd((PREV,)...  6.41 us
    pallas_call x1, Pallas kernels, local(): call(functools.partial(outer_kernel, s), [sd(video.shape, BF16)], out_spe...  2.67 us
    ppermute x1, starting transfers between devices, local(): late = lax.ppermute(late, 'ta', ring[:-1])  2 us
    ppermute x1, waiting for transfers between devices, local(): lax.ppermute(x, ('ha', 'wa'), p)  2 us
    pallas_call x1, Pallas kernels, local(): call(functools.partial(inner_kernel, s), [sd((PREV,) + taps, BF16), sd((P...  1.84 us
    ppermute x1, starting transfers between devices, local(): got = lax.ppermute(hand, 'ta', ring)  1.64 us
    ppermute x1, starting transfers between devices, local(): early = lax.ppermute(early, 'ta', ring)  1.63 us
    ppermute x1, starting transfers between devices, local(): gotx = [lax.ppermute(x, 'wa', p) for x, p in zip(pays[:s.ncol], sides)]  1.51 us
  transfers between devices with their start and end apart: 8, of which 3 were waited for; matrix products, arithmetic and copies ran while one was open for 0% of the time, Pallas kernels for 36%

profile of v4, /device:TPU:16, one launch (start us, length us, event | category | flops | bytes accessed | tf_op | source)
XLA Modules:
  0.0 25.8 jit_solution(2477147169423040353)
XLA Ops:
  0.0 1.4 %copy-done = bf16[4,24,32,256]{3,2,1,0:T(8,128)(2,1)S(1)} copy-done((bf16[4,24,32,256]{3,2,1,0:T(8,128)(2,1)S(1)}, bf16[4,24,32,256]{3,2,1,0:T(8,128)(2,1)}, u32[]{:S(2)}) %copy-start) | copy-done | bytes 1572888
  1.5 0.0 copy-start.6
  1.5 1.6 %collective-permute-start.6 = (bf16[26,32,256]{2,1,0:T(8,128)(2,1)S(1)}, bf16[26,32,256]{2,1,0:T(8,128)(2,1)S(1)}, u32[]{:S(2)}, u32[]{:S(2)}) collective-permute-start(bf16[26,32,256]{2,1,0:T(8,128)(2,1)S(1)} %get-tuple-element.24.early), channel_id=1, source_target_pairs={{0,1},{1,2},{2,3},{3,0},{4,5},{5,6},{6,7},{7,4},{8,9},{9,10},{10,1... | collective-permute-start | bytes 1277960 | tf_op jit(solution)/shard_map/ppermute | solution.py:538
  3.1 0.7 %local.1 = (bf16[160,256]{1,0:T(8,128)(2,1)S(1)}, f32[8,256]{1,0:T(8,128)S(1)}, bf16[128,256]{1,0:T(8,128)(2,1)S(1)}) custom-call(bf16[4,24,32,256]{3,2,1,0:T(8,128)(2,1)S(1)} %copy-done, bf16[26,32,256]{2,1,0:T(8,128)(2,1)S(1)} %get-tuple-element.24.early), custom_call_target="tpu_custom_call" | custom-call | flops 1024 | bytes 1024 | tf_op jit(solution)/shard_map/local/pallas_call | solution.py:532
  3.9 0.1 collective-permute-start
  3.9 1.3 %collective-permute-done.got = bf16[160,256]{1,0:T(8,128)(2,1)S(1)} collective-permute-done((bf16[160,256]{1,0:T(8,128)(2,1)S(1)}, bf16[160,256]{1,0:T(8,128)(2,1)S(1)}, u32[]{:S(2)}, u32[]{:S(2)}) %collective-permute-start) | collective-permute-done | bytes 81952 | tf_op jit(solution)/shard_map/ppermute | solution.py:539
  5.2 0.0 copy-start.7
  5.3 1.3 %collective-permute-start.1 = (bf16[160,256]{1,0:T(8,128)(2,1)S(1)}, bf16[160,256]{1,0:T(8,128)(2,1)S(1)}, u32[]{:S(2)}, u32[]{:S(2)}) collective-permute-start(bf16[160,256]{1,0:T(8,128)(2,1)S(1)} %get-tuple-element.30), channel_id=1, source_target_pairs={{0,24},{8,16},{16,8},{24,0},{1,25},{9,17},{17,9},{25,1},{2,26},{10... | collective-permute-start | bytes 245768 | tf_op jit(solution)/shard_map/ppermute | solution.py:552
  6.6 1.5 %collective-permute-start.2 = (bf16[160,256]{1,0:T(8,128)(2,1)S(1)}, bf16[160,256]{1,0:T(8,128)(2,1)S(1)}, u32[]{:S(2)}, u32[]{:S(2)}) collective-permute-start(bf16[160,256]{1,0:T(8,128)(2,1)S(1)} %get-tuple-element.31), channel_id=1, source_target_pairs={{0,4},{4,0},{1,5},{5,1},{2,6},{6,2},{3,7},{7,3},{8,12},{12,8},{9,1... | collective-permute-start | bytes 245768 | tf_op jit(solution)/shard_map/ppermute | solution.py:553
  8.1 0.1 collective-permute-start.3
  8.3 2.0 %collective-permute-start.7 = (bf16[15,32,256]{2,1,0:T(8,128)(2,1)S(1)}, bf16[15,32,256]{2,1,0:T(8,128)(2,1)S(1)}, u32[]{:S(2)}, u32[]{:S(2)}) collective-permute-start(bf16[15,32,256]{2,1,0:T(8,128)(2,1)S(1)} %get-tuple-element.36), channel_id=1, source_target_pairs={{0,1},{1,2},{2,3},{4,5},{5,6},{6,7},{8,9},{9,10},{10,11},{12,13},{... | collective-permute-start | bytes 737288 | tf_op jit(solution)/shard_map/ppermute | solution.py:555
  10.3 2.0 %collective-permute-done.3.refs_1_ = bf16[48,256]{1,0:T(8,128)(2,1)S(1)} collective-permute-done((bf16[48,256]{1,0:T(8,128)(2,1)S(1)}, bf16[48,256]{1,0:T(8,128)(2,1)S(1)}, u32[]{:S(2)}, u32[]{:S(2)}) %collective-permute-start.3) | collective-permute-done | bytes 24608 | tf_op jit(solution)/shard_map/ppermute | solution.py:554
  12.3 0.0 collective-permute-done.1.goty
  12.3 0.0 collective-permute-done.2.refs_0_
  12.3 0.0 copy-done.6
  12.3 0.3 %group.1 = (f32[8,256]{1,0:T(8,128)S(1)}, f32[4,256]{1,0:T(4,128)S(1)}) custom-call(f32[8,256]{1,0:T(8,128)S(1)} %get-tuple-element.29.part, f32[1,256]{1,0:T(1,128)S(1)} %bitcast.17, bf16[160,256]{1,0:T(8,128)(2,1)S(1)} %collective-permute-done.1.goty, bf16[160,256]{1,0:T(8,128)(2,1)S(1)} %collective-permute-done.2.refs_0_, ...), custom_call_target="tpu_custom_call" | custom-call | flops 1024 | bytes 1024 | tf_op jit(solution)/shard_map/group/pallas_call | solution.py:559
  12.6 0.3 %collective-permute-start.5 = (f32[4,256]{1,0:T(4,128)S(1)}, f32[4,256]{1,0:T(4,128)S(1)}, u32[]{:S(2)}, u32[]{:S(2)}) collective-permute-start(f32[4,256]{1,0:T(4,128)S(1)} %get-tuple-element.35), channel_id=1, source_target_pairs={{0,1},{1,2},{2,3},{3,0},{4,5},{5,6},{6,7},{7,4},{8,9},{9,10},{10,1... | collective-permute-start | bytes 12296 | tf_op jit(solution)/shard_map/ppermute | solution.py:565
  12.9 0.0 copy-done.1
  12.9 0.1 edge.1
  12.9 1.6 %collective-permute-start.4 = (bf16[416,256]{1,0:T(8,128)(2,1)S(1)}, bf16[416,256]{1,0:T(8,128)(2,1)S(1)}, u32[]{:S(2)}, u32[]{:S(2)}) collective-permute-start(bf16[416,256]{1,0:T(8,128)(2,1)S(1)} %get-tuple-element.34), channel_id=1, source_target_pairs={{0,1},{1,2},{2,3},{3,0},{4,5},{5,6},{6,7},{7,4},{8,9},{9,10},{10,1... | collective-permute-start | bytes 638984 | tf_op jit(solution)/shard_map/ppermute | solution.py:572
  14.6 0.0 collective-permute-done.6.refs_1_.early
  14.6 0.0 copy-done.2
  14.6 0.0 copy-done.3
  14.6 0.0 copy-done.4
  14.6 0.0 copy-done.5
  14.6 0.0 copy-done.7
  14.6 6.4 %own.1 = (bf16[4,24,32,256]{3,2,1,0:T(8,128)(2,1)}, f32[2,768,256]{2,1,0:T(8,128)S(1)}) custom-call(bf16[4,24,32,256]{3,2,1,0:T(8,128)(2,1)S(1)} %copy-done.1, bf16[4,2,32,256]{3,2,1,0:T(8,128)(2,1)S(1)} %get-tuple-element.37.halo, f32[8,256]{1,0:T(8,128)S(1)} %get-tuple-element.33.aff, f32[1,256]{1,0:T(1,128)S(1)} %bitcast.11, ...), custom_call_target="tpu_custom_call" | custom-call | flops 4227858432 | bytes 1024 | tf_op jit(solution)/shard_map/own/pallas_call | solution.py:575
  21.0 0.0 collective-permute-done.5.moved
  21.1 0.0 collective-permute-done.7.late
  21.1 1.8 %inner.1 = (bf16[2,3,26,32,256]{4,3,2,1,0:T(8,128)(2,1)S(1)}, bf16[2,768,256]{2,1,0:T(8,128)(2,1)S(1)}) custom-call(bf16[26,32,256]{2,1,0:T(8,128)(2,1)S(1)} %collective-permute-done.6.refs_1_.early, bf16[15,32,256]{2,1,0:T(8,128)(2,1)S(1)} %collective-permute-done.7.late, f32[4,256]{1,0:T(4,128)S(1)} %collective-permute-done.5.moved, ...), custom_call_target="tpu_custom_call" | custom-call | flops 1024 | bytes 1024 | tf_op jit(solution)/shard_map/inner/pallas_call | solution.py:589
  22.9 0.2 collective-permute-done.4.got
  23.1 2.7 %outer.1 = bf16[4,24,32,256]{3,2,1,0:T(8,128)(2,1)} custom-call(bf16[416,256]{1,0:T(8,128)(2,1)S(1)} %collective-permute-done.4.got, f32[4,256]{1,0:T(4,128)S(1)} %collective-permute-done.5.moved, bf16[2,3,26,32,256]{4,3,2,1,0:T(8,128)(2,1)S(1)} %get-tuple-element.40.taps, ...), custom_call_target="tpu_custom_call", output_to_operand_aliasing={{}: (9, {})} | custom-call | flops 1024 | bytes 1024 | tf_op jit(solution)/shard_map/outer/pallas_call | solution.py:595
  (8 shorter events, 0.1 us)
Async XLA Ops:
  0.0 1.4 %copy-start = (bf16[4,24,32,256]{3,2,1,0:T(8,128)(2,1)S(1)}, bf16[4,24,32,256]{3,2,1,0:T(8,128)(2,1)}, u32[]{:S(2)}) copy-start(bf16[4,24,32,256]{3,2,1,0:T(8,128)(2,1)} %video.9) | copy-start | bytes 4718596
  1.5 10.8 %copy-start.6 = (f32[256]{0:T(256)S(1)}, f32[256]{0:T(256)}, u32[]{:S(2)}) copy-start(f32[256]{0:T(256)} %param.8) | copy-start | bytes 3076
  1.5 13.1 %collective-permute-start.6 = (bf16[26,32,256]{2,1,0:T(8,128)(2,1)S(1)}, bf16[26,32,256]{2,1,0:T(8,128)(2,1)S(1)}, u32[]{:S(2)}, u32[]{:S(2)}) collective-permute-start(bf16[26,32,256]{2,1,0:T(8,128)(2,1)S(1)} %get-tuple-element.24.early), channel_id=1, source_target_pairs={{0,1},{1,2},{2,3},{3,0},{4,5},{5,6},{6,7},{7,4},{8,9},{9,10},{10,1... | collective-permute-start | bytes 1277960 | tf_op jit(solution)/shard_map/ppermute | solution.py:538
  3.8 9.0 %copy-start.1 = (bf16[4,24,32,256]{3,2,1,0:T(8,128)(2,1)S(1)}, bf16[4,24,32,256]{3,2,1,0:T(8,128)(2,1)}, u32[]{:S(2)}) copy-start(bf16[4,24,32,256]{3,2,1,0:T(8,128)(2,1)} %video.9) | copy-start | bytes 4718596
  3.9 1.3 %collective-permute-start = (bf16[160,256]{1,0:T(8,128)(2,1)S(1)}, bf16[160,256]{1,0:T(8,128)(2,1)S(1)}, u32[]{:S(2)}, u32[]{:S(2)}) collective-permute-start(bf16[160,256]{1,0:T(8,128)(2,1)S(1)} %get-tuple-element.26), channel_id=1, source_target_pairs={{0,8},{8,0},{16,24},{24,16},{1,9},{9,1},{17,25},{25,17},{2,10},{10... | collective-permute-start | bytes 245768 | tf_op jit(solution)/shard_map/ppermute | solution.py:539
  5.2 9.4 %copy-start.2 = (bf16[3,3,256,256]{3,2,1,0:T(8,128)(2,1)S(1)}, bf16[3,3,256,256]{3,2,1,0:T(8,128)(2,1)}, u32[]{:S(2)}) copy-start(bf16[3,3,256,256]{3,2,1,0:T(8,128)(2,1)} %param.10) | copy-start | bytes 3538948
  5.2 9.4 %copy-start.3 = (bf16[3,256,256]{2,1,0:T(8,128)(2,1)S(1)}, bf16[3,256,256]{2,1,0:T(8,128)(2,1)}, u32[]{:S(2)}) copy-start(bf16[3,256,256]{2,1,0:T(8,128)(2,1)} %param.12) | copy-start | bytes 1179652
  5.2 9.4 %copy-start.4 = (f32[256]{0:T(256)S(1)}, f32[256]{0:T(256)}, u32[]{:S(2)}) copy-start(f32[256]{0:T(256)} %param.9) | copy-start | bytes 3076
  5.2 9.4 %copy-start.5 = (f32[256]{0:T(256)S(1)}, f32[256]{0:T(256)}, u32[]{:S(2)}) copy-start(f32[256]{0:T(256)} %param.11) | copy-start | bytes 3076
  5.2 9.4 %copy-start.7 = (f32[256]{0:T(256)S(1)}, f32[256]{0:T(256)}, u32[]{:S(2)}) copy-start(f32[256]{0:T(256)} %param.13) | copy-start | bytes 3076
  5.3 7.0 %collective-permute-start.1 = (bf16[160,256]{1,0:T(8,128)(2,1)S(1)}, bf16[160,256]{1,0:T(8,128)(2,1)S(1)}, u32[]{:S(2)}, u32[]{:S(2)}) collective-permute-start(bf16[160,256]{1,0:T(8,128)(2,1)S(1)} %get-tuple-element.30), channel_id=1, source_target_pairs={{0,24},{8,16},{16,8},{24,0},{1,25},{9,17},{17,9},{25,1},{2,26},{10... | collective-permute-start | bytes 245768 | tf_op jit(solution)/shard_map/ppermute | solution.py:552
  6.6 5.7 %collective-permute-start.2 = (bf16[160,256]{1,0:T(8,128)(2,1)S(1)}, bf16[160,256]{1,0:T(8,128)(2,1)S(1)}, u32[]{:S(2)}, u32[]{:S(2)}) collective-permute-start(bf16[160,256]{1,0:T(8,128)(2,1)S(1)} %get-tuple-element.31), channel_id=1, source_target_pairs={{0,4},{4,0},{1,5},{5,1},{2,6},{6,2},{3,7},{7,3},{8,12},{12,8},{9,1... | collective-permute-start | bytes 245768 | tf_op jit(solution)/shard_map/ppermute | solution.py:553
  8.1 4.2 %collective-permute-start.3 = (bf16[48,256]{1,0:T(8,128)(2,1)S(1)}, bf16[48,256]{1,0:T(8,128)(2,1)S(1)}, u32[]{:S(2)}, u32[]{:S(2)}) collective-permute-start(bf16[48,256]{1,0:T(8,128)(2,1)S(1)} %get-tuple-element.32), channel_id=1, source_target_pairs={{0,28},{4,24},{8,20},{12,16},{16,12},{20,8},{24,4},{28,0},{1,29},{... | collective-permute-start | bytes 73736 | tf_op jit(solution)/shard_map/ppermute | solution.py:554
  8.3 12.8 %collective-permute-start.7 = (bf16[15,32,256]{2,1,0:T(8,128)(2,1)S(1)}, bf16[15,32,256]{2,1,0:T(8,128)(2,1)S(1)}, u32[]{:S(2)}, u32[]{:S(2)}) collective-permute-start(bf16[15,32,256]{2,1,0:T(8,128)(2,1)S(1)} %get-tuple-element.36), channel_id=1, source_target_pairs={{0,1},{1,2},{2,3},{4,5},{5,6},{6,7},{8,9},{9,10},{10,11},{12,13},{... | collective-permute-start | bytes 737288 | tf_op jit(solution)/shard_map/ppermute | solution.py:555
  12.6 8.4 %collective-permute-start.5 = (f32[4,256]{1,0:T(4,128)S(1)}, f32[4,256]{1,0:T(4,128)S(1)}, u32[]{:S(2)}, u32[]{:S(2)}) collective-permute-start(f32[4,256]{1,0:T(4,128)S(1)} %get-tuple-element.35), channel_id=1, source_target_pairs={{0,1},{1,2},{2,3},{3,0},{4,5},{5,6},{6,7},{7,4},{8,9},{9,10},{10,1... | collective-permute-start | bytes 12296 | tf_op jit(solution)/shard_map/ppermute | solution.py:565
  12.9 10.2 %collective-permute-start.4 = (bf16[416,256]{1,0:T(8,128)(2,1)S(1)}, bf16[416,256]{1,0:T(8,128)(2,1)S(1)}, u32[]{:S(2)}, u32[]{:S(2)}) collective-permute-start(bf16[416,256]{1,0:T(8,128)(2,1)S(1)} %get-tuple-element.34), channel_id=1, source_target_pairs={{0,1},{1,2},{2,3},{3,0},{4,5},{5,6},{6,7},{7,4},{8,9},{9,10},{10,1... | collective-permute-start | bytes 638984 | tf_op jit(solution)/shard_map/ppermute | solution.py:572

commit v5 on v4

--- a/solution.py
+++ b/solution.py
@@ -343,7 +343,12 @@
         wait(put(s, out, enc, sem, f))
 
 
-def inner_kernel(s, early, late, moved, nbias, sw, sb, base, taps, spatial):
+def taps_back(s, grids, f, tw):
+    lhs = jnp.concatenate([grids[q] for q in range(PREV - 1, f - 1, -1)], axis=1)
+    return jnp.dot(lhs, tw[(f + 1) * s.chans :], preferred_element_type=F32)
+
+
+def inner_kernel(s, early, late, moved, nbias, sw, sb, tw, base, taps, spatial, pre, rim):
     shift = nbias[...] * 0.5
 
     @pl.when(lax.axis_index("ta") > 0)
@@ -361,9 +366,22 @@
             fill_taps(s, taps.at[p], raw_row, None, moved[p : p + 1], moved[PREV + p : PREV + p + 1], shift)
             rows = s.rows if p < PREV - 1 else s.rows - s.tail - 1
             spatial[p, : rows * s.cols] = spatial_dot(s, taps.at[p], sw, sb, rows)
-
-
-def outer_kernel(s, got, moved, taps, spatial, nbias, sw, sb, tw, base, _, enc, more, grid, out, sem):
+        part = slice(s.cols, (s.rows - s.tail - 1) * s.cols)
+        for f in range(PREV):
+            y = taps_back(s, [spatial[q, part] for q in range(PREV)], f, tw) + base[f, part]
+            pre[f, 1 : s.rows - s.tail - 1] = y.astype(BF16).reshape(-1, s.cols, s.chans)
+            for k in range(s.ncol):
+                right = lax.axis_index("wa") == 0 if s.ncol == 1 else k == 1
+                cells = []
+                for h in range(s.rows):
+                    o = h * s.cols
+                    last = base[f, o + s.cols - 8 : o + s.cols]
+                    cells.append(jnp.where(right, last[7:], base[f, o : o + 8][:1]))
+                cells.append(jnp.zeros((s.colrow - s.rows, s.chans), F32))
+                rim[f, k] = jnp.concatenate(cells, axis=0)
+
+
+def outer_kernel(s, got, moved, taps, spatial, nbias, sw, sb, tw, base, pre, rim, _, enc, more, grid, out, sem):
     ha, wa = lax.axis_index("ha"), lax.axis_index("wa")
     shift = nbias[...] * 0.5
     inside = [jnp.where(ha > 0, 1.0, 0.0).astype(F32), jnp.where(ha < s.ha - 1, 1.0, 0.0).astype(F32)]
@@ -466,33 +484,40 @@
         size = 2 * s.cols + s.ncol * s.colrow
         tile = 16
         cells = lax.broadcasted_iota(jnp.int32, (tile, s.chans), 0)
+        masks = [cells == jnp.where(right, tile - 1, 0) for right in sides]
+        starts = [jnp.where(right, s.cols - tile, 0) for right in sides]
+        first, body = s.cols, (s.tail + 1) * s.cols
         for p in range(PREV):
             o = p * size
-            n = (s.rows - 1) * s.cols
-            grid[p, : s.cols] = border[o : o + s.cols].astype(BF16)
-            m = n if p < end else start_row * s.cols
-            grid[p, s.cols : m] = spatial[p, s.cols : m]
-            if p == end:
-                grid[p, m : m + fresh] = border[PREV * size : PREV * size + fresh].astype(BF16)
-            grid[p, n:] = border[o + s.cols : o + 2 * s.cols].astype(BF16)
+            grid[p, :first] = border[o : o + first].astype(BF16)
+            if p < end:
+                rest = spatial[p, start_row * s.cols : (s.rows - 1) * s.cols]
+            else:
+                rest = border[PREV * size : PREV * size + fresh].astype(BF16)
+            grid[p, first : body] = rest
+            grid[p, body : body + s.cols] = border[o + s.cols : o + 2 * s.cols].astype(BF16)
             for k in range(s.ncol):
-                place = jnp.where(sides[k], tile - 1, 0)
-                mask = cells == place
-                for h in range(s.rows):
-                    o2 = o + 2 * s.cols + k * s.colrow + h
-                    at0 = h * s.cols + jnp.where(sides[k], s.cols - tile, 0)
-                    part = pl.ds(pl.multiple_of(at0, tile), tile)
-                    row = jnp.where(mask, border[o2 : o2 + 1], grid[p, part].astype(F32))
-                    grid[p, part] = row.astype(BF16)
-        half = s.rows * s.cols // 2
+                o2 = o + 2 * s.cols + k * s.colrow
+                for g in range(s.tail + 2):
+                    h = 0 if g == 0 else start_row + g - 1
+                    at0 = pl.ds(pl.multiple_of(g * s.cols + starts[k], tile), tile)
+                    row = jnp.where(masks[k], border[o2 + h : o2 + h + 1], grid[p, at0].astype(F32))
+                    grid[p, at0] = row.astype(BF16)
+                o3 = body + s.cols + k * s.colrow
+                grid[p, o3 : o3 + s.colrow] = border[o2 : o2 + s.colrow].astype(BF16)
         for f in range(PREV):
-            for k in range(2):
-                part = slice(k * half, (k + 1) * half)
-                lhs = jnp.concatenate([grid[q, part] for q in range(PREV - 1, f - 1, -1)], axis=1)
-                y = jnp.dot(lhs, tw[(f + 1) * s.chans :], preferred_element_type=F32) + base[f, part]
-                block = (s.rows // 2, s.cols, s.chans)
-                out[f, k * block[0] : (k + 1) * block[0]] = y.astype(BF16).reshape(block)
-                start(put(s, out, enc, sem, f, range(k * QUARTERS // 2, (k + 1) * QUARTERS // 2)))
+            own = [base[f, :first], base[f, start_row * s.cols :]] + [rim[f, k] for k in range(s.ncol)]
+            y = taps_back(s, [grid[q] for q in range(PREV)], f, tw) + jnp.concatenate(own, axis=0)
+            out[f, 0] = y[:first].astype(BF16)
+            out[f, start_row:] = y[first : body + s.cols].astype(BF16).reshape(-1, s.cols, s.chans)
+            out[f, 1:start_row] = pre[f, 1:start_row]
+            for k in range(s.ncol):
+                o3 = body + s.cols + k * s.colrow
+                at0 = pl.ds(pl.multiple_of(starts[k], tile), tile)
+                for h in range(1, start_row):
+                    row = jnp.where(masks[k], y[o3 + h : o3 + h + 1], out[f, h, at0].astype(F32))
+                    out[f, h, at0] = row.astype(BF16)
+            start(put(s, out, enc, sem, f))
         for f in range(PREV):
             wait(put(s, out, enc, sem, f))
 
@@ -586,26 +611,31 @@
         name="own",
         in_specs=[VMEM] * (8 + s.ncol) + [ANY],
     )(video, halo, aff, nbias, sw, sb, tw, tb, *cols, early)
-    grid, inner = call(
+    grid, inner, pre, rim = call(
         functools.partial(inner_kernel, s),
-        [sd((PREV,) + taps, BF16), sd((PREV,) + frame, BF16)],
+        [
+            sd((PREV,) + taps, BF16),
+            sd((PREV,) + frame, BF16),
+            sd((PREV,) + one, BF16),
+            sd((PREV, s.ncol, s.colrow, c), F32),
+        ],
         name="inner",
-        in_specs=[VMEM] * 6 + [ANY],
-    )(early, late, moved, nbias, sw, sb, base)
+        in_specs=[VMEM] * 8,
+    )(early, late, moved, nbias, sw, sb, tw, base)
     (enc,) = call(
         functools.partial(outer_kernel, s),
         [sd(video.shape, BF16)],
         out_specs=[ANY],
         scratch=[
             pltpu.VMEM((3, s.tail + 2) + one[1:], BF16),
-            pltpu.VMEM((PREV,) + frame, BF16),
+            pltpu.VMEM((PREV, (s.tail + 2) * s.cols + s.ncol * s.colrow, c), BF16),
             pltpu.VMEM((PREV,) + one, BF16),
             pltpu.SemaphoreType.DMA((PREV, QUARTERS)),
         ],
         name="outer",
-        in_specs=[VMEM] * 9 + [ANY],
-        input_output_aliases={9: 0},
-    )(got, moved, grid, inner, nbias, sw, sb, tw, base, enc)
+        in_specs=[VMEM] * 11 + [ANY],
+        input_output_aliases={11: 0},
+    )(got, moved, grid, inner, nbias, sw, sb, tw, base, pre, rim, enc)
     return enc
 
 

time: 25.9 us -> 25.7 us (level)
    pallas_call x1, Pallas kernels: 2.67 us -> 2.26 us  [local(): call(functools.partial(outer_kernel, s), [sd(video.shape, BF16)], out_spe...]
    pallas_call x1, Pallas kernels: 1.84 us -> 2.15 us  [local(): call(functools.partial(inner_kernel, s), [sd((PREV,) + taps, BF16), sd((P...]
  transfers between devices with their start and end apart: 8 -> 8, of which waited for: 3 -> 2; matrix products, arithmetic and copies ran while one was open for 0% -> 0% of each run, Pallas kernels for 36% -> 38%
where the time goes in v5:
time: 25.7 us; the launch traced here: 25.6 us
  Pallas kernels  12.1 us (47%)
  starting transfers between devices  8.62 us (34%)
  waiting for transfers between devices  3.28 us (13%)
  local copies, waits for them, and re-layouts  1.44 us (6%)
    pallas_call x1, Pallas kernels, local(): call(functools.partial(own_kernel, s), [sd(video.shape, BF16), sd((PREV,)...  6.49 us
    pallas_call x1, Pallas kernels, local(): call(functools.partial(outer_kernel, s), [sd(video.shape, BF16)], out_spe...  2.26 us
    pallas_call x1, Pallas kernels, local(): call(functools.partial(inner_kernel, s), [sd((PREV,) + taps, BF16), sd((P...  2.15 us
    ppermute x1, starting transfers between devices, local(): late = lax.ppermute(late, 'ta', ring[:-1])  2 us
    ppermute x1, waiting for transfers between devices, local(): lax.ppermute(x, ('ha', 'wa'), p)  2 us
    ppermute x1, starting transfers between devices, local(): got = lax.ppermute(hand, 'ta', ring)  1.64 us
    ppermute x1, starting transfers between devices, local(): early = lax.ppermute(early, 'ta', ring)  1.63 us
    ppermute x1, starting transfers between devices, local(): gotx = [lax.ppermute(x, 'wa', p) for x, p in zip(pays[:s.ncol], sides)]  1.51 us
  transfers between devices with their start and end apart: 8, of which 2 were waited for; matrix products, arithmetic and copies ran while one was open for 0% of the time, Pallas kernels for 38%

profile of v5, /device:TPU:16, one launch (start us, length us, event | category | flops | bytes accessed | tf_op | source)
XLA Modules:
  0.0 25.6 jit_solution(4967996459321637623)
XLA Ops:
  0.0 1.4 %copy-done = bf16[4,24,32,256]{3,2,1,0:T(8,128)(2,1)S(1)} copy-done((bf16[4,24,32,256]{3,2,1,0:T(8,128)(2,1)S(1)}, bf16[4,24,32,256]{3,2,1,0:T(8,128)(2,1)}, u32[]{:S(2)}) %copy-start) | copy-done | bytes 1572888
  1.5 0.0 copy-start.6
  1.5 1.6 %collective-permute-start.6 = (bf16[26,32,256]{2,1,0:T(8,128)(2,1)S(1)}, bf16[26,32,256]{2,1,0:T(8,128)(2,1)S(1)}, u32[]{:S(2)}, u32[]{:S(2)}) collective-permute-start(bf16[26,32,256]{2,1,0:T(8,128)(2,1)S(1)} %get-tuple-element.26.early), channel_id=1, source_target_pairs={{0,1},{1,2},{2,3},{3,0},{4,5},{5,6},{6,7},{7,4},{8,9},{9,10},{10,1... | collective-permute-start | bytes 1277960 | tf_op jit(solution)/shard_map/ppermute | solution.py:563
  3.1 0.7 %local.1 = (bf16[160,256]{1,0:T(8,128)(2,1)S(1)}, f32[8,256]{1,0:T(8,128)S(1)}, bf16[128,256]{1,0:T(8,128)(2,1)S(1)}) custom-call(bf16[4,24,32,256]{3,2,1,0:T(8,128)(2,1)S(1)} %copy-done, bf16[26,32,256]{2,1,0:T(8,128)(2,1)S(1)} %get-tuple-element.26.early), custom_call_target="tpu_custom_call" | custom-call | flops 1024 | bytes 1024 | tf_op jit(solution)/shard_map/local/pallas_call | solution.py:557
  3.9 0.1 collective-permute-start
  3.9 1.3 %collective-permute-done.got = bf16[160,256]{1,0:T(8,128)(2,1)S(1)} collective-permute-done((bf16[160,256]{1,0:T(8,128)(2,1)S(1)}, bf16[160,256]{1,0:T(8,128)(2,1)S(1)}, u32[]{:S(2)}, u32[]{:S(2)}) %collective-permute-start) | collective-permute-done | bytes 81952 | tf_op jit(solution)/shard_map/ppermute | solution.py:564
  5.2 0.0 copy-start.7
  5.3 1.3 %collective-permute-start.1 = (bf16[160,256]{1,0:T(8,128)(2,1)S(1)}, bf16[160,256]{1,0:T(8,128)(2,1)S(1)}, u32[]{:S(2)}, u32[]{:S(2)}) collective-permute-start(bf16[160,256]{1,0:T(8,128)(2,1)S(1)} %get-tuple-element.32), channel_id=1, source_target_pairs={{0,24},{8,16},{16,8},{24,0},{1,25},{9,17},{17,9},{25,1},{2,26},{10... | collective-permute-start | bytes 245768 | tf_op jit(solution)/shard_map/ppermute | solution.py:577
  6.6 1.5 %collective-permute-start.2 = (bf16[160,256]{1,0:T(8,128)(2,1)S(1)}, bf16[160,256]{1,0:T(8,128)(2,1)S(1)}, u32[]{:S(2)}, u32[]{:S(2)}) collective-permute-start(bf16[160,256]{1,0:T(8,128)(2,1)S(1)} %get-tuple-element.33), channel_id=1, source_target_pairs={{0,4},{4,0},{1,5},{5,1},{2,6},{6,2},{3,7},{7,3},{8,12},{12,8},{9,1... | collective-permute-start | bytes 245768 | tf_op jit(solution)/shard_map/ppermute | solution.py:578
  8.1 0.1 collective-permute-start.3
  8.3 2.0 %collective-permute-start.7 = (bf16[15,32,256]{2,1,0:T(8,128)(2,1)S(1)}, bf16[15,32,256]{2,1,0:T(8,128)(2,1)S(1)}, u32[]{:S(2)}, u32[]{:S(2)}) collective-permute-start(bf16[15,32,256]{2,1,0:T(8,128)(2,1)S(1)} %get-tuple-element.38), channel_id=1, source_target_pairs={{0,1},{1,2},{2,3},{4,5},{5,6},{6,7},{8,9},{9,10},{10,11},{12,13},{... | collective-permute-start | bytes 737288 | tf_op jit(solution)/shard_map/ppermute | solution.py:580
  10.3 2.0 %collective-permute-done.3.refs_1_ = bf16[48,256]{1,0:T(8,128)(2,1)S(1)} collective-permute-done((bf16[48,256]{1,0:T(8,128)(2,1)S(1)}, bf16[48,256]{1,0:T(8,128)(2,1)S(1)}, u32[]{:S(2)}, u32[]{:S(2)}) %collective-permute-start.3) | collective-permute-done | bytes 24608 | tf_op jit(solution)/shard_map/ppermute | solution.py:579
  12.3 0.0 collective-permute-done.1.goty
  12.3 0.0 collective-permute-done.2.refs_0_
  12.3 0.0 copy-done.6
  12.3 0.3 %group.1 = (f32[8,256]{1,0:T(8,128)S(1)}, f32[4,256]{1,0:T(4,128)S(1)}) custom-call(f32[8,256]{1,0:T(8,128)S(1)} %get-tuple-element.31.part, f32[1,256]{1,0:T(1,128)S(1)} %bitcast.18, bf16[160,256]{1,0:T(8,128)(2,1)S(1)} %collective-permute-done.1.goty, bf16[160,256]{1,0:T(8,128)(2,1)S(1)} %collective-permute-done.2.refs_0_, ...), custom_call_target="tpu_custom_call" | custom-call | flops 1024 | bytes 1024 | tf_op jit(solution)/shard_map/group/pallas_call | solution.py:584
  12.6 0.3 %collective-permute-start.5 = (f32[4,256]{1,0:T(4,128)S(1)}, f32[4,256]{1,0:T(4,128)S(1)}, u32[]{:S(2)}, u32[]{:S(2)}) collective-permute-start(f32[4,256]{1,0:T(4,128)S(1)} %get-tuple-element.37), channel_id=1, source_target_pairs={{0,1},{1,2},{2,3},{3,0},{4,5},{5,6},{6,7},{7,4},{8,9},{9,10},{10,1... | collective-permute-start | bytes 12296 | tf_op jit(solution)/shard_map/ppermute | solution.py:590
  12.9 0.0 copy-done.1
  12.9 0.1 edge.1
  12.9 1.6 %collective-permute-start.4 = (bf16[416,256]{1,0:T(8,128)(2,1)S(1)}, bf16[416,256]{1,0:T(8,128)(2,1)S(1)}, u32[]{:S(2)}, u32[]{:S(2)}) collective-permute-start(bf16[416,256]{1,0:T(8,128)(2,1)S(1)} %get-tuple-element.36), channel_id=1, source_target_pairs={{0,1},{1,2},{2,3},{3,0},{4,5},{5,6},{6,7},{7,4},{8,9},{9,10},{10,1... | collective-permute-start | bytes 638984 | tf_op jit(solution)/shard_map/ppermute | solution.py:597
  14.6 0.0 collective-permute-done.6.refs_1_.early
  14.6 0.0 copy-done.2
  14.6 0.0 copy-done.3
  14.6 0.0 copy-done.4
  14.6 0.0 copy-done.5
  14.6 0.0 copy-done.7
  14.6 6.5 %own.1 = (bf16[4,24,32,256]{3,2,1,0:T(8,128)(2,1)}, f32[2,768,256]{2,1,0:T(8,128)S(1)}) custom-call(bf16[4,24,32,256]{3,2,1,0:T(8,128)(2,1)S(1)} %copy-done.1, bf16[4,2,32,256]{3,2,1,0:T(8,128)(2,1)S(1)} %get-tuple-element.39.halo, f32[8,256]{1,0:T(8,128)S(1)} %get-tuple-element.35.aff, f32[1,256]{1,0:T(1,128)S(1)} %bitcast.12, ...), custom_call_target="tpu_custom_call" | custom-call | flops 4227858432 | bytes 1024 | tf_op jit(solution)/shard_map/own/pallas_call | solution.py:600
  21.1 0.0 collective-permute-done.5.moved
  21.1 0.0 collective-permute-done.7.late
  21.1 2.2 %inner.1 = (bf16[2,3,26,32,256]{4,3,2,1,0:T(8,128)(2,1)S(1)}, bf16[2,768,256]{2,1,0:T(8,128)(2,1)S(1)}, bf16[2,24,32,256]{3,2,1,0:T(8,128)(2,1)S(1)}, f32[2,1,32,256]{3,2,1,0:T(8,128)S(1)}) custom-call(bf16[26,32,256]{2,1,0:T(8,128)(2,1)S(1)} %collective-permute-done.6.refs_1_.early, bf16[15,32,256]{2,1,0:T(8,128)(2,1)S(1)} %collective-permute-done.7.late, ...), custom_call_target="tpu_custom_call" | custom-call | flops 1024 | bytes 1024 | tf_op jit(solution)/shard_map/inner/pallas_call | solution.py:614
  23.3 0.0 collective-permute-done.4.got
  23.3 2.3 %outer.1 = bf16[4,24,32,256]{3,2,1,0:T(8,128)(2,1)} custom-call(bf16[416,256]{1,0:T(8,128)(2,1)S(1)} %collective-permute-done.4.got, f32[4,256]{1,0:T(4,128)S(1)} %collective-permute-done.5.moved, bf16[2,3,26,32,256]{4,3,2,1,0:T(8,128)(2,1)S(1)} %get-tuple-element.42.taps, ...), custom_call_target="tpu_custom_call", output_to_operand_aliasing={{}: (11, {})} | custom-call | flops 1024 | bytes 1024 | tf_op jit(solution)/shard_map/outer/pallas_call | solution.py:625
  (8 shorter events, 0.1 us)
Async XLA Ops:
  0.0 1.4 %copy-start = (bf16[4,24,32,256]{3,2,1,0:T(8,128)(2,1)S(1)}, bf16[4,24,32,256]{3,2,1,0:T(8,128)(2,1)}, u32[]{:S(2)}) copy-start(bf16[4,24,32,256]{3,2,1,0:T(8,128)(2,1)} %video.9) | copy-start | bytes 4718596
  1.5 10.8 %copy-start.6 = (f32[256]{0:T(256)S(1)}, f32[256]{0:T(256)}, u32[]{:S(2)}) copy-start(f32[256]{0:T(256)} %param.8) | copy-start | bytes 3076
  1.5 13.1 %collective-permute-start.6 = (bf16[26,32,256]{2,1,0:T(8,128)(2,1)S(1)}, bf16[26,32,256]{2,1,0:T(8,128)(2,1)S(1)}, u32[]{:S(2)}, u32[]{:S(2)}) collective-permute-start(bf16[26,32,256]{2,1,0:T(8,128)(2,1)S(1)} %get-tuple-element.26.early), channel_id=1, source_target_pairs={{0,1},{1,2},{2,3},{3,0},{4,5},{5,6},{6,7},{7,4},{8,9},{9,10},{10,1... | collective-permute-start | bytes 1277960 | tf_op jit(solution)/shard_map/ppermute | solution.py:563
  3.8 9.0 %copy-start.1 = (bf16[4,24,32,256]{3,2,1,0:T(8,128)(2,1)S(1)}, bf16[4,24,32,256]{3,2,1,0:T(8,128)(2,1)}, u32[]{:S(2)}) copy-start(bf16[4,24,32,256]{3,2,1,0:T(8,128)(2,1)} %video.9) | copy-start | bytes 4718596
  3.9 1.3 %collective-permute-start = (bf16[160,256]{1,0:T(8,128)(2,1)S(1)}, bf16[160,256]{1,0:T(8,128)(2,1)S(1)}, u32[]{:S(2)}, u32[]{:S(2)}) collective-permute-start(bf16[160,256]{1,0:T(8,128)(2,1)S(1)} %get-tuple-element.28), channel_id=1, source_target_pairs={{0,8},{8,0},{16,24},{24,16},{1,9},{9,1},{17,25},{25,17},{2,10},{10... | collective-permute-start | bytes 245768 | tf_op jit(solution)/shard_map/ppermute | solution.py:564
  5.2 9.4 %copy-start.2 = (bf16[3,3,256,256]{3,2,1,0:T(8,128)(2,1)S(1)}, bf16[3,3,256,256]{3,2,1,0:T(8,128)(2,1)}, u32[]{:S(2)}) copy-start(bf16[3,3,256,256]{3,2,1,0:T(8,128)(2,1)} %param.10) | copy-start | bytes 3538948
  5.2 9.4 %copy-start.3 = (bf16[3,256,256]{2,1,0:T(8,128)(2,1)S(1)}, bf16[3,256,256]{2,1,0:T(8,128)(2,1)}, u32[]{:S(2)}) copy-start(bf16[3,256,256]{2,1,0:T(8,128)(2,1)} %param.12) | copy-start | bytes 1179652
  5.2 9.4 %copy-start.4 = (f32[256]{0:T(256)S(1)}, f32[256]{0:T(256)}, u32[]{:S(2)}) copy-start(f32[256]{0:T(256)} %param.9) | copy-start | bytes 3076
  5.2 9.4 %copy-start.5 = (f32[256]{0:T(256)S(1)}, f32[256]{0:T(256)}, u32[]{:S(2)}) copy-start(f32[256]{0:T(256)} %param.11) | copy-start | bytes 3076
  5.2 9.4 %copy-start.7 = (f32[256]{0:T(256)S(1)}, f32[256]{0:T(256)}, u32[]{:S(2)}) copy-start(f32[256]{0:T(256)} %param.13) | copy-start | bytes 3076
  5.3 7.0 %collective-permute-start.1 = (bf16[160,256]{1,0:T(8,128)(2,1)S(1)}, bf16[160,256]{1,0:T(8,128)(2,1)S(1)}, u32[]{:S(2)}, u32[]{:S(2)}) collective-permute-start(bf16[160,256]{1,0:T(8,128)(2,1)S(1)} %get-tuple-element.32), channel_id=1, source_target_pairs={{0,24},{8,16},{16,8},{24,0},{1,25},{9,17},{17,9},{25,1},{2,26},{10... | collective-permute-start | bytes 245768 | tf_op jit(solution)/shard_map/ppermute | solution.py:577
  6.6 5.7 %collective-permute-start.2 = (bf16[160,256]{1,0:T(8,128)(2,1)S(1)}, bf16[160,256]{1,0:T(8,128)(2,1)S(1)}, u32[]{:S(2)}, u32[]{:S(2)}) collective-permute-start(bf16[160,256]{1,0:T(8,128)(2,1)S(1)} %get-tuple-element.33), channel_id=1, source_target_pairs={{0,4},{4,0},{1,5},{5,1},{2,6},{6,2},{3,7},{7,3},{8,12},{12,8},{9,1... | collective-permute-start | bytes 245768 | tf_op jit(solution)/shard_map/ppermute | solution.py:578
  8.1 4.2 %collective-permute-start.3 = (bf16[48,256]{1,0:T(8,128)(2,1)S(1)}, bf16[48,256]{1,0:T(8,128)(2,1)S(1)}, u32[]{:S(2)}, u32[]{:S(2)}) collective-permute-start(bf16[48,256]{1,0:T(8,128)(2,1)S(1)} %get-tuple-element.34), channel_id=1, source_target_pairs={{0,28},{4,24},{8,20},{12,16},{16,12},{20,8},{24,4},{28,0},{1,29},{... | collective-permute-start | bytes 73736 | tf_op jit(solution)/shard_map/ppermute | solution.py:579
  8.3 12.9 %collective-permute-start.7 = (bf16[15,32,256]{2,1,0:T(8,128)(2,1)S(1)}, bf16[15,32,256]{2,1,0:T(8,128)(2,1)S(1)}, u32[]{:S(2)}, u32[]{:S(2)}) collective-permute-start(bf16[15,32,256]{2,1,0:T(8,128)(2,1)S(1)} %get-tuple-element.38), channel_id=1, source_target_pairs={{0,1},{1,2},{2,3},{4,5},{5,6},{6,7},{8,9},{9,10},{10,11},{12,13},{... | collective-permute-start | bytes 737288 | tf_op jit(solution)/shard_map/ppermute | solution.py:580
  12.6 8.5 %collective-permute-start.5 = (f32[4,256]{1,0:T(4,128)S(1)}, f32[4,256]{1,0:T(4,128)S(1)}, u32[]{:S(2)}, u32[]{:S(2)}) collective-permute-start(f32[4,256]{1,0:T(4,128)S(1)} %get-tuple-element.37), channel_id=1, source_target_pairs={{0,1},{1,2},{2,3},{3,0},{4,5},{5,6},{6,7},{7,4},{8,9},{9,10},{10,1... | collective-permute-start | bytes 12296 | tf_op jit(solution)/shard_map/ppermute | solution.py:590
  12.9 10.4 %collective-permute-start.4 = (bf16[416,256]{1,0:T(8,128)(2,1)S(1)}, bf16[416,256]{1,0:T(8,128)(2,1)S(1)}, u32[]{:S(2)}, u32[]{:S(2)}) collective-permute-start(bf16[416,256]{1,0:T(8,128)(2,1)S(1)} %get-tuple-element.36), channel_id=1, source_target_pairs={{0,1},{1,2},{2,3},{3,0},{4,5},{5,6},{6,7},{7,4},{8,9},{9,10},{10,1... | collective-permute-start | bytes 638984 | tf_op jit(solution)/shard_map/ppermute | solution.py:597

commit v6 on v5

--- a/solution.py
+++ b/solution.py
@@ -10,6 +10,7 @@
 G = 32
 EPS = 1e-06
 QUARTERS = 4
+EDGE = 8
 DOTS = 6
 PREV = 2
 F32 = jnp.float32
@@ -396,6 +397,13 @@
 
     @pl.when(lax.axis_index("ta") > 0)
     def _():
+        copies = []
+        width = s.cols - EDGE * s.ncol
+        safe = EDGE if s.ncol > 1 else pl.multiple_of(jnp.where(wa == 0, 0, EDGE), EDGE)
+        for f in range(PREV):
+            place = (f, pl.ds(1, s.rows - s.tail - 2), pl.ds(safe, width))
+            copies.append(pltpu.make_async_copy(pre.at[place], enc.at[place], sem.at[f, 4]))
+        start(copies)
         lhs = []
         start_row = s.rows - s.tail - 1
         end = PREV - 1
@@ -510,16 +518,23 @@
             y = taps_back(s, [grid[q] for q in range(PREV)], f, tw) + jnp.concatenate(own, axis=0)
             out[f, 0] = y[:first].astype(BF16)
             out[f, start_row:] = y[first : body + s.cols].astype(BF16).reshape(-1, s.cols, s.chans)
-            out[f, 1:start_row] = pre[f, 1:start_row]
+            rows = pl.ds(start_row, s.tail + 1)
+            copies += [
+                pltpu.make_async_copy(out.at[f, 0], enc.at[f, 0], sem.at[f, 0]),
+                pltpu.make_async_copy(out.at[f, rows], enc.at[f, rows], sem.at[f, 1]),
+            ]
+            start(copies[-2:])
             for k in range(s.ncol):
                 o3 = body + s.cols + k * s.colrow
                 at0 = pl.ds(pl.multiple_of(starts[k], tile), tile)
                 for h in range(1, start_row):
-                    row = jnp.where(masks[k], y[o3 + h : o3 + h + 1], out[f, h, at0].astype(F32))
+                    row = jnp.where(masks[k], y[o3 + h : o3 + h + 1], pre[f, h, at0].astype(F32))
                     out[f, h, at0] = row.astype(BF16)
-            start(put(s, out, enc, sem, f))
-        for f in range(PREV):
-            wait(put(s, out, enc, sem, f))
+                edge = pl.multiple_of(jnp.where(sides[k], s.cols - EDGE, 0), EDGE)
+                place = (f, pl.ds(1, start_row - 1), pl.ds(edge, EDGE))
+                copies.append(pltpu.make_async_copy(out.at[place], enc.at[place], sem.at[f, 2 + k]))
+                copies[-1].start()
+        wait(copies)
 
 
 def mates(n, phase):
@@ -630,7 +645,7 @@
             pltpu.VMEM((3, s.tail + 2) + one[1:], BF16),
             pltpu.VMEM((PREV, (s.tail + 2) * s.cols + s.ncol * s.colrow, c), BF16),
             pltpu.VMEM((PREV,) + one, BF16),
-            pltpu.SemaphoreType.DMA((PREV, QUARTERS)),
+            pltpu.SemaphoreType.DMA((PREV, 5)),
         ],
         name="outer",
         in_specs=[VMEM] * 11 + [ANY],

time: 25.7 us -> 25.6 us (level)
  transfers between devices with their start and end apart: 8 -> 8, of which waited for: 2 -> 2; matrix products, arithmetic and copies ran while one was open for 0% -> 0% of each run, Pallas kernels for 38% -> 39%
where the time goes in v6:
time: 25.6 us; the launch traced here: 25.4 us
  Pallas kernels  12 us (47%)
  starting transfers between devices  8.62 us (34%)
  waiting for transfers between devices  3.28 us (13%)
  local copies, waits for them, and re-layouts  1.44 us (6%)
    pallas_call x1, Pallas kernels, local(): call(functools.partial(own_kernel, s), [sd(video.shape, BF16), sd((PREV,)...  6.49 us
    pallas_call x1, Pallas kernels, local(): call(functools.partial(inner_kernel, s), [sd((PREV,) + taps, BF16), sd((P...  2.15 us
    pallas_call x1, Pallas kernels, local(): call(functools.partial(outer_kernel, s), [sd(video.shape, BF16)], out_spe...  2.13 us
    ppermute x1, starting transfers between devices, local(): late = lax.ppermute(late, 'ta', ring[:-1])  2 us
    ppermute x1, waiting for transfers between devices, local(): lax.ppermute(x, ('ha', 'wa'), p)  2 us
    ppermute x1, starting transfers between devices, local(): got = lax.ppermute(hand, 'ta', ring)  1.64 us
    ppermute x1, starting transfers between devices, local(): early = lax.ppermute(early, 'ta', ring)  1.63 us
    ppermute x1, starting transfers between devices, local(): gotx = [lax.ppermute(x, 'wa', p) for x, p in zip(pays[:s.ncol], sides)]  1.51 us
  transfers between devices with their start and end apart: 8, of which 2 were waited for; matrix products, arithmetic and copies ran while one was open for 0% of the time, Pallas kernels for 39%

profile of v6, /device:TPU:16, one launch (start us, length us, event | category | flops | bytes accessed | tf_op | source)
XLA Modules:
  0.0 25.4 jit_solution(16352986894034676906)
XLA Ops:
  0.0 1.4 %copy-done = bf16[4,24,32,256]{3,2,1,0:T(8,128)(2,1)S(1)} copy-done((bf16[4,24,32,256]{3,2,1,0:T(8,128)(2,1)S(1)}, bf16[4,24,32,256]{3,2,1,0:T(8,128)(2,1)}, u32[]{:S(2)}) %copy-start) | copy-done | bytes 1572888
  1.5 0.0 copy-start.6
  1.5 1.6 %collective-permute-start.6 = (bf16[26,32,256]{2,1,0:T(8,128)(2,1)S(1)}, bf16[26,32,256]{2,1,0:T(8,128)(2,1)S(1)}, u32[]{:S(2)}, u32[]{:S(2)}) collective-permute-start(bf16[26,32,256]{2,1,0:T(8,128)(2,1)S(1)} %get-tuple-element.26.early), channel_id=1, source_target_pairs={{0,1},{1,2},{2,3},{3,0},{4,5},{5,6},{6,7},{7,4},{8,9},{9,10},{10,1... | collective-permute-start | bytes 1277960 | tf_op jit(solution)/shard_map/ppermute | solution.py:578
  3.1 0.7 %local.1 = (bf16[160,256]{1,0:T(8,128)(2,1)S(1)}, f32[8,256]{1,0:T(8,128)S(1)}, bf16[128,256]{1,0:T(8,128)(2,1)S(1)}) custom-call(bf16[4,24,32,256]{3,2,1,0:T(8,128)(2,1)S(1)} %copy-done, bf16[26,32,256]{2,1,0:T(8,128)(2,1)S(1)} %get-tuple-element.26.early), custom_call_target="tpu_custom_call" | custom-call | flops 1024 | bytes 1024 | tf_op jit(solution)/shard_map/local/pallas_call | solution.py:572
  3.9 0.1 collective-permute-start
  3.9 1.3 %collective-permute-done.got = bf16[160,256]{1,0:T(8,128)(2,1)S(1)} collective-permute-done((bf16[160,256]{1,0:T(8,128)(2,1)S(1)}, bf16[160,256]{1,0:T(8,128)(2,1)S(1)}, u32[]{:S(2)}, u32[]{:S(2)}) %collective-permute-start) | collective-permute-done | bytes 81952 | tf_op jit(solution)/shard_map/ppermute | solution.py:579
  5.2 0.0 copy-start.7
  5.3 1.3 %collective-permute-start.1 = (bf16[160,256]{1,0:T(8,128)(2,1)S(1)}, bf16[160,256]{1,0:T(8,128)(2,1)S(1)}, u32[]{:S(2)}, u32[]{:S(2)}) collective-permute-start(bf16[160,256]{1,0:T(8,128)(2,1)S(1)} %get-tuple-element.32), channel_id=1, source_target_pairs={{0,24},{8,16},{16,8},{24,0},{1,25},{9,17},{17,9},{25,1},{2,26},{10... | collective-permute-start | bytes 245768 | tf_op jit(solution)/shard_map/ppermute | solution.py:592
  6.6 1.5 %collective-permute-start.2 = (bf16[160,256]{1,0:T(8,128)(2,1)S(1)}, bf16[160,256]{1,0:T(8,128)(2,1)S(1)}, u32[]{:S(2)}, u32[]{:S(2)}) collective-permute-start(bf16[160,256]{1,0:T(8,128)(2,1)S(1)} %get-tuple-element.33), channel_id=1, source_target_pairs={{0,4},{4,0},{1,5},{5,1},{2,6},{6,2},{3,7},{7,3},{8,12},{12,8},{9,1... | collective-permute-start | bytes 245768 | tf_op jit(solution)/shard_map/ppermute | solution.py:593
  8.1 0.1 collective-permute-start.3
  8.3 2.0 %collective-permute-start.7 = (bf16[15,32,256]{2,1,0:T(8,128)(2,1)S(1)}, bf16[15,32,256]{2,1,0:T(8,128)(2,1)S(1)}, u32[]{:S(2)}, u32[]{:S(2)}) collective-permute-start(bf16[15,32,256]{2,1,0:T(8,128)(2,1)S(1)} %get-tuple-element.38), channel_id=1, source_target_pairs={{0,1},{1,2},{2,3},{4,5},{5,6},{6,7},{8,9},{9,10},{10,11},{12,13},{... | collective-permute-start | bytes 737288 | tf_op jit(solution)/shard_map/ppermute | solution.py:595
  10.3 2.0 %collective-permute-done.3.refs_1_ = bf16[48,256]{1,0:T(8,128)(2,1)S(1)} collective-permute-done((bf16[48,256]{1,0:T(8,128)(2,1)S(1)}, bf16[48,256]{1,0:T(8,128)(2,1)S(1)}, u32[]{:S(2)}, u32[]{:S(2)}) %collective-permute-start.3) | collective-permute-done | bytes 24608 | tf_op jit(solution)/shard_map/ppermute | solution.py:594
  12.3 0.0 collective-permute-done.1.goty
  12.3 0.0 collective-permute-done.2.refs_0_
  12.3 0.0 copy-done.6
  12.3 0.3 %group.1 = (f32[8,256]{1,0:T(8,128)S(1)}, f32[4,256]{1,0:T(4,128)S(1)}) custom-call(f32[8,256]{1,0:T(8,128)S(1)} %get-tuple-element.31.part, f32[1,256]{1,0:T(1,128)S(1)} %bitcast.18, bf16[160,256]{1,0:T(8,128)(2,1)S(1)} %collective-permute-done.1.goty, bf16[160,256]{1,0:T(8,128)(2,1)S(1)} %collective-permute-done.2.refs_0_, ...), custom_call_target="tpu_custom_call" | custom-call | flops 1024 | bytes 1024 | tf_op jit(solution)/shard_map/group/pallas_call | solution.py:599
  12.6 0.3 %collective-permute-start.5 = (f32[4,256]{1,0:T(4,128)S(1)}, f32[4,256]{1,0:T(4,128)S(1)}, u32[]{:S(2)}, u32[]{:S(2)}) collective-permute-start(f32[4,256]{1,0:T(4,128)S(1)} %get-tuple-element.37), channel_id=1, source_target_pairs={{0,1},{1,2},{2,3},{3,0},{4,5},{5,6},{6,7},{7,4},{8,9},{9,10},{10,1... | collective-permute-start | bytes 12296 | tf_op jit(solution)/shard_map/ppermute | solution.py:605
  12.9 0.0 copy-done.1
  12.9 0.1 edge.1
  12.9 1.6 %collective-permute-start.4 = (bf16[416,256]{1,0:T(8,128)(2,1)S(1)}, bf16[416,256]{1,0:T(8,128)(2,1)S(1)}, u32[]{:S(2)}, u32[]{:S(2)}) collective-permute-start(bf16[416,256]{1,0:T(8,128)(2,1)S(1)} %get-tuple-element.36), channel_id=1, source_target_pairs={{0,1},{1,2},{2,3},{3,0},{4,5},{5,6},{6,7},{7,4},{8,9},{9,10},{10,1... | collective-permute-start | bytes 638984 | tf_op jit(solution)/shard_map/ppermute | solution.py:612
  14.6 0.0 collective-permute-done.6.refs_1_.early
  14.6 0.0 copy-done.2
  14.6 0.0 copy-done.3
  14.6 0.0 copy-done.4
  14.6 0.0 copy-done.5
  14.6 0.0 copy-done.7
  14.6 6.5 %own.1 = (bf16[4,24,32,256]{3,2,1,0:T(8,128)(2,1)}, f32[2,768,256]{2,1,0:T(8,128)S(1)}) custom-call(bf16[4,24,32,256]{3,2,1,0:T(8,128)(2,1)S(1)} %copy-done.1, bf16[4,2,32,256]{3,2,1,0:T(8,128)(2,1)S(1)} %get-tuple-element.39.halo, f32[8,256]{1,0:T(8,128)S(1)} %get-tuple-element.35.aff, f32[1,256]{1,0:T(1,128)S(1)} %bitcast.12, ...), custom_call_target="tpu_custom_call" | custom-call | flops 4227858432 | bytes 1024 | tf_op jit(solution)/shard_map/own/pallas_call | solution.py:615
  21.1 0.0 collective-permute-done.5.moved
  21.1 0.0 collective-permute-done.7.late
  21.1 2.2 %inner.1 = (bf16[2,3,26,32,256]{4,3,2,1,0:T(8,128)(2,1)S(1)}, bf16[2,768,256]{2,1,0:T(8,128)(2,1)S(1)}, bf16[2,24,32,256]{3,2,1,0:T(8,128)(2,1)S(1)}, f32[2,1,32,256]{3,2,1,0:T(8,128)S(1)}) custom-call(bf16[26,32,256]{2,1,0:T(8,128)(2,1)S(1)} %collective-permute-done.6.refs_1_.early, bf16[15,32,256]{2,1,0:T(8,128)(2,1)S(1)} %collective-permute-done.7.late, ...), custom_call_target="tpu_custom_call" | custom-call | flops 1024 | bytes 1024 | tf_op jit(solution)/shard_map/inner/pallas_call | solution.py:629
  23.3 0.0 collective-permute-done.4.got
  23.3 2.1 %outer.1 = bf16[4,24,32,256]{3,2,1,0:T(8,128)(2,1)} custom-call(bf16[416,256]{1,0:T(8,128)(2,1)S(1)} %collective-permute-done.4.got, f32[4,256]{1,0:T(4,128)S(1)} %collective-permute-done.5.moved, bf16[2,3,26,32,256]{4,3,2,1,0:T(8,128)(2,1)S(1)} %get-tuple-element.42.taps, ...), custom_call_target="tpu_custom_call", output_to_operand_aliasing={{}: (11, {})} | custom-call | flops 1024 | bytes 1024 | tf_op jit(solution)/shard_map/outer/pallas_call | solution.py:640
  (8 shorter events, 0.1 us)
Async XLA Ops:
  0.0 1.4 %copy-start = (bf16[4,24,32,256]{3,2,1,0:T(8,128)(2,1)S(1)}, bf16[4,24,32,256]{3,2,1,0:T(8,128)(2,1)}, u32[]{:S(2)}) copy-start(bf16[4,24,32,256]{3,2,1,0:T(8,128)(2,1)} %video.9) | copy-start | bytes 4718596
  1.5 10.8 %copy-start.6 = (f32[256]{0:T(256)S(1)}, f32[256]{0:T(256)}, u32[]{:S(2)}) copy-start(f32[256]{0:T(256)} %param.8) | copy-start | bytes 3076
  1.5 13.1 %collective-permute-start.6 = (bf16[26,32,256]{2,1,0:T(8,128)(2,1)S(1)}, bf16[26,32,256]{2,1,0:T(8,128)(2,1)S(1)}, u32[]{:S(2)}, u32[]{:S(2)}) collective-permute-start(bf16[26,32,256]{2,1,0:T(8,128)(2,1)S(1)} %get-tuple-element.26.early), channel_id=1, source_target_pairs={{0,1},{1,2},{2,3},{3,0},{4,5},{5,6},{6,7},{7,4},{8,9},{9,10},{10,1... | collective-permute-start | bytes 1277960 | tf_op jit(solution)/shard_map/ppermute | solution.py:578
  3.8 9.0 %copy-start.1 = (bf16[4,24,32,256]{3,2,1,0:T(8,128)(2,1)S(1)}, bf16[4,24,32,256]{3,2,1,0:T(8,128)(2,1)}, u32[]{:S(2)}) copy-start(bf16[4,24,32,256]{3,2,1,0:T(8,128)(2,1)} %video.9) | copy-start | bytes 4718596
  3.9 1.3 %collective-permute-start = (bf16[160,256]{1,0:T(8,128)(2,1)S(1)}, bf16[160,256]{1,0:T(8,128)(2,1)S(1)}, u32[]{:S(2)}, u32[]{:S(2)}) collective-permute-start(bf16[160,256]{1,0:T(8,128)(2,1)S(1)} %get-tuple-element.28), channel_id=1, source_target_pairs={{0,8},{8,0},{16,24},{24,16},{1,9},{9,1},{17,25},{25,17},{2,10},{10... | collective-permute-start | bytes 245768 | tf_op jit(solution)/shard_map/ppermute | solution.py:579
  5.2 9.4 %copy-start.2 = (bf16[3,3,256,256]{3,2,1,0:T(8,128)(2,1)S(1)}, bf16[3,3,256,256]{3,2,1,0:T(8,128)(2,1)}, u32[]{:S(2)}) copy-start(bf16[3,3,256,256]{3,2,1,0:T(8,128)(2,1)} %param.10) | copy-start | bytes 3538948
  5.2 9.4 %copy-start.3 = (bf16[3,256,256]{2,1,0:T(8,128)(2,1)S(1)}, bf16[3,256,256]{2,1,0:T(8,128)(2,1)}, u32[]{:S(2)}) copy-start(bf16[3,256,256]{2,1,0:T(8,128)(2,1)} %param.12) | copy-start | bytes 1179652
  5.2 9.4 %copy-start.4 = (f32[256]{0:T(256)S(1)}, f32[256]{0:T(256)}, u32[]{:S(2)}) copy-start(f32[256]{0:T(256)} %param.9) | copy-start | bytes 3076
  5.2 9.4 %copy-start.5 = (f32[256]{0:T(256)S(1)}, f32[256]{0:T(256)}, u32[]{:S(2)}) copy-start(f32[256]{0:T(256)} %param.11) | copy-start | bytes 3076
  5.2 9.4 %copy-start.7 = (f32[256]{0:T(256)S(1)}, f32[256]{0:T(256)}, u32[]{:S(2)}) copy-start(f32[256]{0:T(256)} %param.13) | copy-start | bytes 3076
  5.3 7.0 %collective-permute-start.1 = (bf16[160,256]{1,0:T(8,128)(2,1)S(1)}, bf16[160,256]{1,0:T(8,128)(2,1)S(1)}, u32[]{:S(2)}, u32[]{:S(2)}) collective-permute-start(bf16[160,256]{1,0:T(8,128)(2,1)S(1)} %get-tuple-element.32), channel_id=1, source_target_pairs={{0,24},{8,16},{16,8},{24,0},{1,25},{9,17},{17,9},{25,1},{2,26},{10... | collective-permute-start | bytes 245768 | tf_op jit(solution)/shard_map/ppermute | solution.py:592
  6.6 5.7 %collective-permute-start.2 = (bf16[160,256]{1,0:T(8,128)(2,1)S(1)}, bf16[160,256]{1,0:T(8,128)(2,1)S(1)}, u32[]{:S(2)}, u32[]{:S(2)}) collective-permute-start(bf16[160,256]{1,0:T(8,128)(2,1)S(1)} %get-tuple-element.33), channel_id=1, source_target_pairs={{0,4},{4,0},{1,5},{5,1},{2,6},{6,2},{3,7},{7,3},{8,12},{12,8},{9,1... | collective-permute-start | bytes 245768 | tf_op jit(solution)/shard_map/ppermute | solution.py:593
  8.1 4.2 %collective-permute-start.3 = (bf16[48,256]{1,0:T(8,128)(2,1)S(1)}, bf16[48,256]{1,0:T(8,128)(2,1)S(1)}, u32[]{:S(2)}, u32[]{:S(2)}) collective-permute-start(bf16[48,256]{1,0:T(8,128)(2,1)S(1)} %get-tuple-element.34), channel_id=1, source_target_pairs={{0,28},{4,24},{8,20},{12,16},{16,12},{20,8},{24,4},{28,0},{1,29},{... | collective-permute-start | bytes 73736 | tf_op jit(solution)/shard_map/ppermute | solution.py:594
  8.3 12.9 %collective-permute-start.7 = (bf16[15,32,256]{2,1,0:T(8,128)(2,1)S(1)}, bf16[15,32,256]{2,1,0:T(8,128)(2,1)S(1)}, u32[]{:S(2)}, u32[]{:S(2)}) collective-permute-start(bf16[15,32,256]{2,1,0:T(8,128)(2,1)S(1)} %get-tuple-element.38), channel_id=1, source_target_pairs={{0,1},{1,2},{2,3},{4,5},{5,6},{6,7},{8,9},{9,10},{10,11},{12,13},{... | collective-permute-start | bytes 737288 | tf_op jit(solution)/shard_map/ppermute | solution.py:595
  12.6 8.5 %collective-permute-start.5 = (f32[4,256]{1,0:T(4,128)S(1)}, f32[4,256]{1,0:T(4,128)S(1)}, u32[]{:S(2)}, u32[]{:S(2)}) collective-permute-start(f32[4,256]{1,0:T(4,128)S(1)} %get-tuple-element.37), channel_id=1, source_target_pairs={{0,1},{1,2},{2,3},{3,0},{4,5},{5,6},{6,7},{7,4},{8,9},{9,10},{10,1... | collective-permute-start | bytes 12296 | tf_op jit(solution)/shard_map/ppermute | solution.py:605
  12.9 10.4 %collective-permute-start.4 = (bf16[416,256]{1,0:T(8,128)(2,1)S(1)}, bf16[416,256]{1,0:T(8,128)(2,1)S(1)}, u32[]{:S(2)}, u32[]{:S(2)}) collective-permute-start(bf16[416,256]{1,0:T(8,128)(2,1)S(1)} %get-tuple-element.36), channel_id=1, source_target_pairs={{0,1},{1,2},{2,3},{3,0},{4,5},{5,6},{6,7},{7,4},{8,9},{9,10},{10,1... | collective-permute-start | bytes 638984 | tf_op jit(solution)/shard_map/ppermute | solution.py:612

commit v7 on v6

--- a/solution.py
+++ b/solution.py
@@ -349,7 +349,7 @@
     return jnp.dot(lhs, tw[(f + 1) * s.chans :], preferred_element_type=F32)
 
 
-def inner_kernel(s, early, late, moved, nbias, sw, sb, tw, base, taps, spatial, pre, rim):
+def inner_kernel(s, early, late, moved, nbias, sw, sb, tw, base, taps, spatial, pre, rim, cut):
     shift = nbias[...] * 0.5
 
     @pl.when(lax.axis_index("ta") > 0)
@@ -366,6 +366,16 @@
 
             fill_taps(s, taps.at[p], raw_row, None, moved[p : p + 1], moved[PREV + p : PREV + p + 1], shift)
             rows = s.rows if p < PREV - 1 else s.rows - s.tail - 1
+            for k in range(s.ncol):
+                right = lax.axis_index("wa") == 0 if s.ncol == 1 else k == 1
+                for d in range(2):
+                    cells = []
+                    for i in range(1, rows + 1):
+                        tile = taps[p, 1, i].astype(F32)
+                        far = tile[s.cols - 1 - d : s.cols - d]
+                        cells.append(jnp.where(right, far, tile[d : d + 1]))
+                    cells.append(jnp.zeros((s.colrow - rows, s.chans), F32))
+                    cut[p, 2 * k + d] = jnp.concatenate(cells, axis=0)
             spatial[p, : rows * s.cols] = spatial_dot(s, taps.at[p], sw, sb, rows)
         part = slice(s.cols, (s.rows - s.tail - 1) * s.cols)
         for f in range(PREV):
@@ -382,7 +392,7 @@
                 rim[f, k] = jnp.concatenate(cells, axis=0)
 
 
-def outer_kernel(s, got, moved, taps, spatial, nbias, sw, sb, tw, base, pre, rim, _, enc, more, grid, out, sem):
+def outer_kernel(s, got, moved, taps, spatial, nbias, sw, sb, tw, base, pre, rim, cut, _, enc, more, grid, out, sem):
     ha, wa = lax.axis_index("ha"), lax.axis_index("wa")
     shift = nbias[...] * 0.5
     inside = [jnp.where(ha > 0, 1.0, 0.0).astype(F32), jnp.where(ha < s.ha - 1, 1.0, 0.0).astype(F32)]
@@ -448,15 +458,17 @@
                 right = sides[k]
 
                 def column(d):
-                    rows = []
-                    for i in range(1, n + 1):
+                    known = n if p < end else start_row
+                    x = cut[p, 2 * k + d]
+                    if known == n:
+                        return x
+                    rows = [jnp.zeros((known, s.chans), F32)]
+                    for i in range(known + 1, n + 1):
                         tile = tap(p, 1, i).astype(F32)
-                        if d == 0:
-                            rows.append(jnp.where(right, tile[s.cols - 1 :], tile[:1]))
-                        else:
-                            rows.append(jnp.where(right, tile[s.cols - 2 : s.cols - 1], tile[1:2]))
-                    fill = jnp.zeros((s.colrow - n, s.chans), F32)
-                    return jnp.concatenate(rows + [fill], axis=0)
+                        far = tile[s.cols - 1 - d : s.cols - d]
+                        rows.append(jnp.where(right, far, tile[d : d + 1]))
+                    rows.append(jnp.zeros((s.colrow - n, s.chans), F32))
+                    return x + jnp.concatenate(rows, axis=0)
 
                 here, inner = column(0), column(1)
                 far = jnp.where(down < n, cell, 0.0)
@@ -626,13 +638,14 @@
         name="own",
         in_specs=[VMEM] * (8 + s.ncol) + [ANY],
     )(video, halo, aff, nbias, sw, sb, tw, tb, *cols, early)
-    grid, inner, pre, rim = call(
+    grid, inner, pre, rim, cut = call(
         functools.partial(inner_kernel, s),
         [
             sd((PREV,) + taps, BF16),
             sd((PREV,) + frame, BF16),
             sd((PREV,) + one, BF16),
             sd((PREV, s.ncol, s.colrow, c), F32),
+            sd((PREV, 2 * s.ncol, s.colrow, c), F32),
         ],
         name="inner",
         in_specs=[VMEM] * 8,
@@ -648,9 +661,9 @@
             pltpu.SemaphoreType.DMA((PREV, 5)),
         ],
         name="outer",
-        in_specs=[VMEM] * 11 + [ANY],
-        input_output_aliases={11: 0},
-    )(got, moved, grid, inner, nbias, sw, sb, tw, base, pre, rim, enc)
+        in_specs=[VMEM] * 12 + [ANY],
+        input_output_aliases={12: 0},
+    )(got, moved, grid, inner, nbias, sw, sb, tw, base, pre, rim, cut, enc)
     return enc
 
 

time: 25.6 us -> 25.6 us (level)
  no operation moved by 1% of the time
where the time goes in v7:
time: 25.6 us; the launch traced here: 25.4 us
  Pallas kernels  11.9 us (46%)
  starting transfers between devices  8.62 us (34%)
  waiting for transfers between devices  3.28 us (13%)
  local copies, waits for them, and re-layouts  1.44 us (6%)
    pallas_call x1, Pallas kernels, local(): call(functools.partial(own_kernel, s), [sd(video.shape, BF16), sd((PREV,)...  6.48 us
    pallas_call x1, Pallas kernels, local(): call(functools.partial(inner_kernel, s), [sd((PREV,) + taps, BF16), sd((P...  2.21 us
    pallas_call x1, Pallas kernels, local(): call(functools.partial(outer_kernel, s), [sd(video.shape, BF16)], out_spe...  2.03 us
    ppermute x1, starting transfers between devices, local(): late = lax.ppermute(late, 'ta', ring[:-1])  2 us
    ppermute x1, waiting for transfers between devices, local(): lax.ppermute(x, ('ha', 'wa'), p)  2 us
    ppermute x1, starting transfers between devices, local(): got = lax.ppermute(hand, 'ta', ring)  1.64 us
    ppermute x1, starting transfers between devices, local(): early = lax.ppermute(early, 'ta', ring)  1.63 us
    ppermute x1, starting transfers between devices, local(): gotx = [lax.ppermute(x, 'wa', p) for x, p in zip(pays[:s.ncol], sides)]  1.51 us
  transfers between devices with their start and end apart: 8, of which 2 were waited for; matrix products, arithmetic and copies ran while one was open for 0% of the time, Pallas kernels for 39%

profile of v7, /device:TPU:16, one launch (start us, length us, event | category | flops | bytes accessed | tf_op | source)
XLA Modules:
  0.0 25.4 jit_solution(11893088456871710674)
XLA Ops:
  0.0 1.4 %copy-done = bf16[4,24,32,256]{3,2,1,0:T(8,128)(2,1)S(1)} copy-done((bf16[4,24,32,256]{3,2,1,0:T(8,128)(2,1)S(1)}, bf16[4,24,32,256]{3,2,1,0:T(8,128)(2,1)}, u32[]{:S(2)}) %copy-start) | copy-done | bytes 1572888
  1.5 0.0 copy-start.6
  1.5 1.6 %collective-permute-start.6 = (bf16[26,32,256]{2,1,0:T(8,128)(2,1)S(1)}, bf16[26,32,256]{2,1,0:T(8,128)(2,1)S(1)}, u32[]{:S(2)}, u32[]{:S(2)}) collective-permute-start(bf16[26,32,256]{2,1,0:T(8,128)(2,1)S(1)} %get-tuple-element.27.early), channel_id=1, source_target_pairs={{0,1},{1,2},{2,3},{3,0},{4,5},{5,6},{6,7},{7,4},{8,9},{9,10},{10,1... | collective-permute-start | bytes 1277960 | tf_op jit(solution)/shard_map/ppermute | solution.py:590
  3.1 0.7 %local.1 = (bf16[160,256]{1,0:T(8,128)(2,1)S(1)}, f32[8,256]{1,0:T(8,128)S(1)}, bf16[128,256]{1,0:T(8,128)(2,1)S(1)}) custom-call(bf16[4,24,32,256]{3,2,1,0:T(8,128)(2,1)S(1)} %copy-done, bf16[26,32,256]{2,1,0:T(8,128)(2,1)S(1)} %get-tuple-element.27.early), custom_call_target="tpu_custom_call" | custom-call | flops 1024 | bytes 1024 | tf_op jit(solution)/shard_map/local/pallas_call | solution.py:584
  3.9 0.1 collective-permute-start
  3.9 1.3 %collective-permute-done.got = bf16[160,256]{1,0:T(8,128)(2,1)S(1)} collective-permute-done((bf16[160,256]{1,0:T(8,128)(2,1)S(1)}, bf16[160,256]{1,0:T(8,128)(2,1)S(1)}, u32[]{:S(2)}, u32[]{:S(2)}) %collective-permute-start) | collective-permute-done | bytes 81952 | tf_op jit(solution)/shard_map/ppermute | solution.py:591
  5.2 0.0 copy-start.7
  5.3 1.3 %collective-permute-start.1 = (bf16[160,256]{1,0:T(8,128)(2,1)S(1)}, bf16[160,256]{1,0:T(8,128)(2,1)S(1)}, u32[]{:S(2)}, u32[]{:S(2)}) collective-permute-start(bf16[160,256]{1,0:T(8,128)(2,1)S(1)} %get-tuple-element.33), channel_id=1, source_target_pairs={{0,24},{8,16},{16,8},{24,0},{1,25},{9,17},{17,9},{25,1},{2,26},{10... | collective-permute-start | bytes 245768 | tf_op jit(solution)/shard_map/ppermute | solution.py:604
  6.6 1.5 %collective-permute-start.2 = (bf16[160,256]{1,0:T(8,128)(2,1)S(1)}, bf16[160,256]{1,0:T(8,128)(2,1)S(1)}, u32[]{:S(2)}, u32[]{:S(2)}) collective-permute-start(bf16[160,256]{1,0:T(8,128)(2,1)S(1)} %get-tuple-element.34), channel_id=1, source_target_pairs={{0,4},{4,0},{1,5},{5,1},{2,6},{6,2},{3,7},{7,3},{8,12},{12,8},{9,1... | collective-permute-start | bytes 245768 | tf_op jit(solution)/shard_map/ppermute | solution.py:605
  8.1 0.1 collective-permute-start.3
  8.3 2.0 %collective-permute-start.7 = (bf16[15,32,256]{2,1,0:T(8,128)(2,1)S(1)}, bf16[15,32,256]{2,1,0:T(8,128)(2,1)S(1)}, u32[]{:S(2)}, u32[]{:S(2)}) collective-permute-start(bf16[15,32,256]{2,1,0:T(8,128)(2,1)S(1)} %get-tuple-element.39), channel_id=1, source_target_pairs={{0,1},{1,2},{2,3},{4,5},{5,6},{6,7},{8,9},{9,10},{10,11},{12,13},{... | collective-permute-start | bytes 737288 | tf_op jit(solution)/shard_map/ppermute | solution.py:607
  10.3 2.0 %collective-permute-done.3.refs_1_ = bf16[48,256]{1,0:T(8,128)(2,1)S(1)} collective-permute-done((bf16[48,256]{1,0:T(8,128)(2,1)S(1)}, bf16[48,256]{1,0:T(8,128)(2,1)S(1)}, u32[]{:S(2)}, u32[]{:S(2)}) %collective-permute-start.3) | collective-permute-done | bytes 24608 | tf_op jit(solution)/shard_map/ppermute | solution.py:606
  12.3 0.0 collective-permute-done.1.goty
  12.3 0.0 collective-permute-done.2.refs_0_
  12.3 0.0 copy-done.6
  12.3 0.3 %group.1 = (f32[8,256]{1,0:T(8,128)S(1)}, f32[4,256]{1,0:T(4,128)S(1)}) custom-call(f32[8,256]{1,0:T(8,128)S(1)} %get-tuple-element.32.part, f32[1,256]{1,0:T(1,128)S(1)} %bitcast.18, bf16[160,256]{1,0:T(8,128)(2,1)S(1)} %collective-permute-done.1.goty, bf16[160,256]{1,0:T(8,128)(2,1)S(1)} %collective-permute-done.2.refs_0_, ...), custom_call_target="tpu_custom_call" | custom-call | flops 1024 | bytes 1024 | tf_op jit(solution)/shard_map/group/pallas_call | solution.py:611
  12.6 0.3 %collective-permute-start.5 = (f32[4,256]{1,0:T(4,128)S(1)}, f32[4,256]{1,0:T(4,128)S(1)}, u32[]{:S(2)}, u32[]{:S(2)}) collective-permute-start(f32[4,256]{1,0:T(4,128)S(1)} %get-tuple-element.38), channel_id=1, source_target_pairs={{0,1},{1,2},{2,3},{3,0},{4,5},{5,6},{6,7},{7,4},{8,9},{9,10},{10,1... | collective-permute-start | bytes 12296 | tf_op jit(solution)/shard_map/ppermute | solution.py:617
  12.9 0.0 copy-done.1
  12.9 0.1 edge.1
  12.9 1.6 %collective-permute-start.4 = (bf16[416,256]{1,0:T(8,128)(2,1)S(1)}, bf16[416,256]{1,0:T(8,128)(2,1)S(1)}, u32[]{:S(2)}, u32[]{:S(2)}) collective-permute-start(bf16[416,256]{1,0:T(8,128)(2,1)S(1)} %get-tuple-element.37), channel_id=1, source_target_pairs={{0,1},{1,2},{2,3},{3,0},{4,5},{5,6},{6,7},{7,4},{8,9},{9,10},{10,1... | collective-permute-start | bytes 638984 | tf_op jit(solution)/shard_map/ppermute | solution.py:624
  14.6 0.0 collective-permute-done.6.refs_1_.early
  14.6 0.0 copy-done.2
  14.6 0.0 copy-done.3
  14.6 0.0 copy-done.4
  14.6 0.0 copy-done.5
  14.6 0.0 copy-done.7
  14.6 6.5 %own.1 = (bf16[4,24,32,256]{3,2,1,0:T(8,128)(2,1)}, f32[2,768,256]{2,1,0:T(8,128)S(1)}) custom-call(bf16[4,24,32,256]{3,2,1,0:T(8,128)(2,1)S(1)} %copy-done.1, bf16[4,2,32,256]{3,2,1,0:T(8,128)(2,1)S(1)} %get-tuple-element.40.halo, f32[8,256]{1,0:T(8,128)S(1)} %get-tuple-element.36.aff, f32[1,256]{1,0:T(1,128)S(1)} %bitcast.12, ...), custom_call_target="tpu_custom_call" | custom-call | flops 4227858432 | bytes 1024 | tf_op jit(solution)/shard_map/own/pallas_call | solution.py:627
  21.1 0.0 collective-permute-done.5.moved
  21.1 0.0 collective-permute-done.7.late
  21.1 2.2 %inner.1 = (bf16[2,3,26,32,256]{4,3,2,1,0:T(8,128)(2,1)S(1)}, bf16[2,768,256]{2,1,0:T(8,128)(2,1)S(1)}, bf16[2,24,32,256]{3,2,1,0:T(8,128)(2,1)S(1)}, f32[2,1,32,256]{3,2,1,0:T(8,128)S(1)}, f32[2,2,32,256]{3,2,1,0:T(8,128)S(1)}) custom-call(bf16[26,32,256]{2,1,0:T(8,128)(2,1)S(1)} %collective-permute-done.6.refs_1_.early, ...), custom_call_target="tpu_custom_call" | custom-call | flops 1024 | bytes 1024 | tf_op jit(solution)/shard_map/inner/pallas_call | solution.py:641
  23.4 0.0 collective-permute-done.4.got
  23.4 2.0 %outer.1 = bf16[4,24,32,256]{3,2,1,0:T(8,128)(2,1)} custom-call(bf16[416,256]{1,0:T(8,128)(2,1)S(1)} %collective-permute-done.4.got, f32[4,256]{1,0:T(4,128)S(1)} %collective-permute-done.5.moved, bf16[2,3,26,32,256]{4,3,2,1,0:T(8,128)(2,1)S(1)} %get-tuple-element.43.taps, ...), custom_call_target="tpu_custom_call", output_to_operand_aliasing={{}: (12, {})} | custom-call | flops 1024 | bytes 1024 | tf_op jit(solution)/shard_map/outer/pallas_call | solution.py:653
  (8 shorter events, 0.1 us)
Async XLA Ops:
  0.0 1.4 %copy-start = (bf16[4,24,32,256]{3,2,1,0:T(8,128)(2,1)S(1)}, bf16[4,24,32,256]{3,2,1,0:T(8,128)(2,1)}, u32[]{:S(2)}) copy-start(bf16[4,24,32,256]{3,2,1,0:T(8,128)(2,1)} %video.9) | copy-start | bytes 4718596
  1.5 10.8 %copy-start.6 = (f32[256]{0:T(256)S(1)}, f32[256]{0:T(256)}, u32[]{:S(2)}) copy-start(f32[256]{0:T(256)} %param.8) | copy-start | bytes 3076
  1.5 13.1 %collective-permute-start.6 = (bf16[26,32,256]{2,1,0:T(8,128)(2,1)S(1)}, bf16[26,32,256]{2,1,0:T(8,128)(2,1)S(1)}, u32[]{:S(2)}, u32[]{:S(2)}) collective-permute-start(bf16[26,32,256]{2,1,0:T(8,128)(2,1)S(1)} %get-tuple-element.27.early), channel_id=1, source_target_pairs={{0,1},{1,2},{2,3},{3,0},{4,5},{5,6},{6,7},{7,4},{8,9},{9,10},{10,1... | collective-permute-start | bytes 1277960 | tf_op jit(solution)/shard_map/ppermute | solution.py:590
  3.8 9.0 %copy-start.1 = (bf16[4,24,32,256]{3,2,1,0:T(8,128)(2,1)S(1)}, bf16[4,24,32,256]{3,2,1,0:T(8,128)(2,1)}, u32[]{:S(2)}) copy-start(bf16[4,24,32,256]{3,2,1,0:T(8,128)(2,1)} %video.9) | copy-start | bytes 4718596
  3.9 1.3 %collective-permute-start = (bf16[160,256]{1,0:T(8,128)(2,1)S(1)}, bf16[160,256]{1,0:T(8,128)(2,1)S(1)}, u32[]{:S(2)}, u32[]{:S(2)}) collective-permute-start(bf16[160,256]{1,0:T(8,128)(2,1)S(1)} %get-tuple-element.29), channel_id=1, source_target_pairs={{0,8},{8,0},{16,24},{24,16},{1,9},{9,1},{17,25},{25,17},{2,10},{10... | collective-permute-start | bytes 245768 | tf_op jit(solution)/shard_map/ppermute | solution.py:591
  5.2 9.4 %copy-start.2 = (bf16[3,3,256,256]{3,2,1,0:T(8,128)(2,1)S(1)}, bf16[3,3,256,256]{3,2,1,0:T(8,128)(2,1)}, u32[]{:S(2)}) copy-start(bf16[3,3,256,256]{3,2,1,0:T(8,128)(2,1)} %param.10) | copy-start | bytes 3538948
  5.2 9.4 %copy-start.3 = (bf16[3,256,256]{2,1,0:T(8,128)(2,1)S(1)}, bf16[3,256,256]{2,1,0:T(8,128)(2,1)}, u32[]{:S(2)}) copy-start(bf16[3,256,256]{2,1,0:T(8,128)(2,1)} %param.12) | copy-start | bytes 1179652
  5.2 9.4 %copy-start.4 = (f32[256]{0:T(256)S(1)}, f32[256]{0:T(256)}, u32[]{:S(2)}) copy-start(f32[256]{0:T(256)} %param.9) | copy-start | bytes 3076
  5.2 9.4 %copy-start.5 = (f32[256]{0:T(256)S(1)}, f32[256]{0:T(256)}, u32[]{:S(2)}) copy-start(f32[256]{0:T(256)} %param.11) | copy-start | bytes 3076
  5.2 9.4 %copy-start.7 = (f32[256]{0:T(256)S(1)}, f32[256]{0:T(256)}, u32[]{:S(2)}) copy-start(f32[256]{0:T(256)} %param.13) | copy-start | bytes 3076
  5.3 7.0 %collective-permute-start.1 = (bf16[160,256]{1,0:T(8,128)(2,1)S(1)}, bf16[160,256]{1,0:T(8,128)(2,1)S(1)}, u32[]{:S(2)}, u32[]{:S(2)}) collective-permute-start(bf16[160,256]{1,0:T(8,128)(2,1)S(1)} %get-tuple-element.33), channel_id=1, source_target_pairs={{0,24},{8,16},{16,8},{24,0},{1,25},{9,17},{17,9},{25,1},{2,26},{10... | collective-permute-start | bytes 245768 | tf_op jit(solution)/shard_map/ppermute | solution.py:604
  6.6 5.7 %collective-permute-start.2 = (bf16[160,256]{1,0:T(8,128)(2,1)S(1)}, bf16[160,256]{1,0:T(8,128)(2,1)S(1)}, u32[]{:S(2)}, u32[]{:S(2)}) collective-permute-start(bf16[160,256]{1,0:T(8,128)(2,1)S(1)} %get-tuple-element.34), channel_id=1, source_target_pairs={{0,4},{4,0},{1,5},{5,1},{2,6},{6,2},{3,7},{7,3},{8,12},{12,8},{9,1... | collective-permute-start | bytes 245768 | tf_op jit(solution)/shard_map/ppermute | solution.py:605
  8.1 4.2 %collective-permute-start.3 = (bf16[48,256]{1,0:T(8,128)(2,1)S(1)}, bf16[48,256]{1,0:T(8,128)(2,1)S(1)}, u32[]{:S(2)}, u32[]{:S(2)}) collective-permute-start(bf16[48,256]{1,0:T(8,128)(2,1)S(1)} %get-tuple-element.35), channel_id=1, source_target_pairs={{0,28},{4,24},{8,20},{12,16},{16,12},{20,8},{24,4},{28,0},{1,29},{... | collective-permute-start | bytes 73736 | tf_op jit(solution)/shard_map/ppermute | solution.py:606
  8.3 12.9 %collective-permute-start.7 = (bf16[15,32,256]{2,1,0:T(8,128)(2,1)S(1)}, bf16[15,32,256]{2,1,0:T(8,128)(2,1)S(1)}, u32[]{:S(2)}, u32[]{:S(2)}) collective-permute-start(bf16[15,32,256]{2,1,0:T(8,128)(2,1)S(1)} %get-tuple-element.39), channel_id=1, source_target_pairs={{0,1},{1,2},{2,3},{4,5},{5,6},{6,7},{8,9},{9,10},{10,11},{12,13},{... | collective-permute-start | bytes 737288 | tf_op jit(solution)/shard_map/ppermute | solution.py:607
  12.6 8.5 %collective-permute-start.5 = (f32[4,256]{1,0:T(4,128)S(1)}, f32[4,256]{1,0:T(4,128)S(1)}, u32[]{:S(2)}, u32[]{:S(2)}) collective-permute-start(f32[4,256]{1,0:T(4,128)S(1)} %get-tuple-element.38), channel_id=1, source_target_pairs={{0,1},{1,2},{2,3},{3,0},{4,5},{5,6},{6,7},{7,4},{8,9},{9,10},{10,1... | collective-permute-start | bytes 12296 | tf_op jit(solution)/shard_map/ppermute | solution.py:617
  12.9 10.4 %collective-permute-start.4 = (bf16[416,256]{1,0:T(8,128)(2,1)S(1)}, bf16[416,256]{1,0:T(8,128)(2,1)S(1)}, u32[]{:S(2)}, u32[]{:S(2)}) collective-permute-start(bf16[416,256]{1,0:T(8,128)(2,1)S(1)} %get-tuple-element.37), channel_id=1, source_target_pairs={{0,1},{1,2},{2,3},{3,0},{4,5},{5,6},{6,7},{7,4},{8,9},{9,10},{10,1... | collective-permute-start | bytes 638984 | tf_op jit(solution)/shard_map/ppermute | solution.py:624

commit v8 on v7

--- a/solution.py
+++ b/solution.py
@@ -304,7 +304,7 @@
     shift = nbias[...] * 0.5
     first = lax.axis_index("ta") == 0
 
-    def frame(f, _):
+    def frame(f):
         def raw_row(i):
             if i == 0:
                 return halo[f, 0]
@@ -313,11 +313,11 @@
             return video[f, i - 1]
 
         edges = [c[pl.ds(f * s.colrow, s.colrow)] for c in cols]
-        fill_taps(s, taps, raw_row, edges, aff[pl.ds(f, 1)], aff[pl.ds(s.frames + f, 1)], shift)
-        spatial[f] = spatial_dot(s, taps, sw, sb, s.rows)
-        return _
-
-    lax.fori_loop(0, s.frames, frame, 0)
+        fill_taps(s, taps.at[f % 2], raw_row, edges, aff[pl.ds(f, 1)], aff[pl.ds(s.frames + f, 1)], shift)
+        spatial[f] = spatial_dot(s, taps.at[f % 2], sw, sb, s.rows)
+
+    for f in range(s.frames):
+        frame(f)
 
     def encode(f):
         out[f] = temporal_dot(s, [spatial[max(f - k, 0)] for k in range(3)], tw, tb)
@@ -629,7 +629,7 @@
         [sd(video.shape, BF16), sd((PREV,) + frame, F32)],
         out_specs=[ANY, VMEM],
         scratch=[
-            pltpu.VMEM(taps, BF16),
+            pltpu.VMEM((2,) + taps, BF16),
             pltpu.VMEM((s.frames,) + frame, BF16),
             pltpu.VMEM((s.frames,) + one, BF16),
             pltpu.SemaphoreType.DMA((s.frames, QUARTERS)),

time: 25.6 us -> 25.3 us (0.988)
  Pallas kernels: 11.9 us -> 11.1 us
  waiting for transfers between devices: 3.28 us -> 3.83 us
    pallas_call x1, Pallas kernels: 6.48 us -> 5.68 us  [local(): call(functools.partial(own_kernel, s), [sd(video.shape, BF16), sd((PREV,)...]
    ppermute x1, waiting for transfers between devices: 0.01 us -> 0.55 us  [local(): got = lax.ppermute(hand, 'ta', ring)]
  transfers between devices with their start and end apart: 8 -> 8, of which waited for: 2 -> 3; matrix products, arithmetic and copies ran while one was open for 0% -> 0% of each run, Pallas kernels for 39% -> 36%
where the time goes in v8:
time: 25.3 us; the launch traced here: 25.1 us
  Pallas kernels  11.1 us (44%)
  starting transfers between devices  8.62 us (34%)
  waiting for transfers between devices  3.83 us (15%)
  local copies, waits for them, and re-layouts  1.44 us (6%)
    pallas_call x1, Pallas kernels, local(): call(functools.partial(own_kernel, s), [sd(video.shape, BF16), sd((PREV,)...  5.68 us
    pallas_call x1, Pallas kernels, local(): call(functools.partial(inner_kernel, s), [sd((PREV,) + taps, BF16), sd((P...  2.21 us
    pallas_call x1, Pallas kernels, local(): call(functools.partial(outer_kernel, s), [sd(video.shape, BF16)], out_spe...  2.01 us
    ppermute x1, starting transfers between devices, local(): late = lax.ppermute(late, 'ta', ring[:-1])  2 us
    ppermute x1, waiting for transfers between devices, local(): lax.ppermute(x, ('ha', 'wa'), p)  2 us
    ppermute x1, starting transfers between devices, local(): got = lax.ppermute(hand, 'ta', ring)  1.64 us
    ppermute x1, starting transfers between devices, local(): early = lax.ppermute(early, 'ta', ring)  1.63 us
    ppermute x1, starting transfers between devices, local(): gotx = [lax.ppermute(x, 'wa', p) for x, p in zip(pays[:s.ncol], sides)]  1.51 us
  transfers between devices with their start and end apart: 8, of which 3 were waited for; matrix products, arithmetic and copies ran while one was open for 0% of the time, Pallas kernels for 36%

profile of v8, /device:TPU:16, one launch (start us, length us, event | category | flops | bytes accessed | tf_op | source)
XLA Modules:
  0.0 25.1 jit_solution(3634135834406814657)
XLA Ops:
  0.0 1.4 %copy-done = bf16[4,24,32,256]{3,2,1,0:T(8,128)(2,1)S(1)} copy-done((bf16[4,24,32,256]{3,2,1,0:T(8,128)(2,1)S(1)}, bf16[4,24,32,256]{3,2,1,0:T(8,128)(2,1)}, u32[]{:S(2)}) %copy-start) | copy-done | bytes 1572888
  1.5 0.0 copy-start.6
  1.5 1.6 %collective-permute-start.6 = (bf16[26,32,256]{2,1,0:T(8,128)(2,1)S(1)}, bf16[26,32,256]{2,1,0:T(8,128)(2,1)S(1)}, u32[]{:S(2)}, u32[]{:S(2)}) collective-permute-start(bf16[26,32,256]{2,1,0:T(8,128)(2,1)S(1)} %get-tuple-element.27.early), channel_id=1, source_target_pairs={{0,1},{1,2},{2,3},{3,0},{4,5},{5,6},{6,7},{7,4},{8,9},{9,10},{10,1... | collective-permute-start | bytes 1277960 | tf_op jit(solution)/shard_map/ppermute | solution.py:590
  3.1 0.7 %local.1 = (bf16[160,256]{1,0:T(8,128)(2,1)S(1)}, f32[8,256]{1,0:T(8,128)S(1)}, bf16[128,256]{1,0:T(8,128)(2,1)S(1)}) custom-call(bf16[4,24,32,256]{3,2,1,0:T(8,128)(2,1)S(1)} %copy-done, bf16[26,32,256]{2,1,0:T(8,128)(2,1)S(1)} %get-tuple-element.27.early), custom_call_target="tpu_custom_call" | custom-call | flops 1024 | bytes 1024 | tf_op jit(solution)/shard_map/local/pallas_call | solution.py:584
  3.9 0.1 collective-permute-start
  3.9 1.3 %collective-permute-done.got = bf16[160,256]{1,0:T(8,128)(2,1)S(1)} collective-permute-done((bf16[160,256]{1,0:T(8,128)(2,1)S(1)}, bf16[160,256]{1,0:T(8,128)(2,1)S(1)}, u32[]{:S(2)}, u32[]{:S(2)}) %collective-permute-start) | collective-permute-done | bytes 81952 | tf_op jit(solution)/shard_map/ppermute | solution.py:591
  5.2 0.0 copy-start.7
  5.3 1.3 %collective-permute-start.1 = (bf16[160,256]{1,0:T(8,128)(2,1)S(1)}, bf16[160,256]{1,0:T(8,128)(2,1)S(1)}, u32[]{:S(2)}, u32[]{:S(2)}) collective-permute-start(bf16[160,256]{1,0:T(8,128)(2,1)S(1)} %get-tuple-element.33), channel_id=1, source_target_pairs={{0,24},{8,16},{16,8},{24,0},{1,25},{9,17},{17,9},{25,1},{2,26},{10... | collective-permute-start | bytes 245768 | tf_op jit(solution)/shard_map/ppermute | solution.py:604
  6.6 1.5 %collective-permute-start.2 = (bf16[160,256]{1,0:T(8,128)(2,1)S(1)}, bf16[160,256]{1,0:T(8,128)(2,1)S(1)}, u32[]{:S(2)}, u32[]{:S(2)}) collective-permute-start(bf16[160,256]{1,0:T(8,128)(2,1)S(1)} %get-tuple-element.34), channel_id=1, source_target_pairs={{0,4},{4,0},{1,5},{5,1},{2,6},{6,2},{3,7},{7,3},{8,12},{12,8},{9,1... | collective-permute-start | bytes 245768 | tf_op jit(solution)/shard_map/ppermute | solution.py:605
  8.1 0.1 collective-permute-start.3
  8.3 2.0 %collective-permute-start.7 = (bf16[15,32,256]{2,1,0:T(8,128)(2,1)S(1)}, bf16[15,32,256]{2,1,0:T(8,128)(2,1)S(1)}, u32[]{:S(2)}, u32[]{:S(2)}) collective-permute-start(bf16[15,32,256]{2,1,0:T(8,128)(2,1)S(1)} %get-tuple-element.39), channel_id=1, source_target_pairs={{0,1},{1,2},{2,3},{4,5},{5,6},{6,7},{8,9},{9,10},{10,11},{12,13},{... | collective-permute-start | bytes 737288 | tf_op jit(solution)/shard_map/ppermute | solution.py:607
  10.3 2.0 %collective-permute-done.3.refs_1_ = bf16[48,256]{1,0:T(8,128)(2,1)S(1)} collective-permute-done((bf16[48,256]{1,0:T(8,128)(2,1)S(1)}, bf16[48,256]{1,0:T(8,128)(2,1)S(1)}, u32[]{:S(2)}, u32[]{:S(2)}) %collective-permute-start.3) | collective-permute-done | bytes 24608 | tf_op jit(solution)/shard_map/ppermute | solution.py:606
  12.3 0.0 collective-permute-done.1.goty
  12.3 0.0 collective-permute-done.2.refs_0_
  12.3 0.0 copy-done.6
  12.3 0.3 %group.1 = (f32[8,256]{1,0:T(8,128)S(1)}, f32[4,256]{1,0:T(4,128)S(1)}) custom-call(f32[8,256]{1,0:T(8,128)S(1)} %get-tuple-element.32.part, f32[1,256]{1,0:T(1,128)S(1)} %bitcast.18, bf16[160,256]{1,0:T(8,128)(2,1)S(1)} %collective-permute-done.1.goty, bf16[160,256]{1,0:T(8,128)(2,1)S(1)} %collective-permute-done.2.refs_0_, ...), custom_call_target="tpu_custom_call" | custom-call | flops 1024 | bytes 1024 | tf_op jit(solution)/shard_map/group/pallas_call | solution.py:611
  12.6 0.3 %collective-permute-start.5 = (f32[4,256]{1,0:T(4,128)S(1)}, f32[4,256]{1,0:T(4,128)S(1)}, u32[]{:S(2)}, u32[]{:S(2)}) collective-permute-start(f32[4,256]{1,0:T(4,128)S(1)} %get-tuple-element.38), channel_id=1, source_target_pairs={{0,1},{1,2},{2,3},{3,0},{4,5},{5,6},{6,7},{7,4},{8,9},{9,10},{10,1... | collective-permute-start | bytes 12296 | tf_op jit(solution)/shard_map/ppermute | solution.py:617
  12.9 0.0 copy-done.1
  12.9 0.1 edge.1
  12.9 1.6 %collective-permute-start.4 = (bf16[416,256]{1,0:T(8,128)(2,1)S(1)}, bf16[416,256]{1,0:T(8,128)(2,1)S(1)}, u32[]{:S(2)}, u32[]{:S(2)}) collective-permute-start(bf16[416,256]{1,0:T(8,128)(2,1)S(1)} %get-tuple-element.37), channel_id=1, source_target_pairs={{0,1},{1,2},{2,3},{3,0},{4,5},{5,6},{6,7},{7,4},{8,9},{9,10},{10,1... | collective-permute-start | bytes 638984 | tf_op jit(solution)/shard_map/ppermute | solution.py:624
  14.6 0.0 collective-permute-done.6.refs_1_.early
  14.6 0.0 copy-done.2
  14.6 0.0 copy-done.3
  14.6 0.0 copy-done.4
  14.6 0.0 copy-done.5
  14.6 0.0 copy-done.7
  14.6 5.7 %own.1 = (bf16[4,24,32,256]{3,2,1,0:T(8,128)(2,1)}, f32[2,768,256]{2,1,0:T(8,128)S(1)}) custom-call(bf16[4,24,32,256]{3,2,1,0:T(8,128)(2,1)S(1)} %copy-done.1, bf16[4,2,32,256]{3,2,1,0:T(8,128)(2,1)S(1)} %get-tuple-element.40.halo, f32[8,256]{1,0:T(8,128)S(1)} %get-tuple-element.36.aff, f32[1,256]{1,0:T(1,128)S(1)} %bitcast.12, ...), custom_call_target="tpu_custom_call" | custom-call | flops 4227858432 | bytes 1024 | tf_op jit(solution)/shard_map/own/pallas_call | solution.py:627
  20.3 0.0 collective-permute-done.5.moved
  20.3 0.0 collective-permute-done.7.late
  20.3 2.2 %inner.1 = (bf16[2,3,26,32,256]{4,3,2,1,0:T(8,128)(2,1)S(1)}, bf16[2,768,256]{2,1,0:T(8,128)(2,1)S(1)}, bf16[2,24,32,256]{3,2,1,0:T(8,128)(2,1)S(1)}, f32[2,1,32,256]{3,2,1,0:T(8,128)S(1)}, f32[2,2,32,256]{3,2,1,0:T(8,128)S(1)}) custom-call(bf16[26,32,256]{2,1,0:T(8,128)(2,1)S(1)} %collective-permute-done.6.refs_1_.early, ...), custom_call_target="tpu_custom_call" | custom-call | flops 1024 | bytes 1024 | tf_op jit(solution)/shard_map/inner/pallas_call | solution.py:641
  22.6 0.6 %collective-permute-done.4.got = bf16[416,256]{1,0:T(8,128)(2,1)S(1)} collective-permute-done((bf16[416,256]{1,0:T(8,128)(2,1)S(1)}, bf16[416,256]{1,0:T(8,128)(2,1)S(1)}, u32[]{:S(2)}, u32[]{:S(2)}) %collective-permute-start.4) | collective-permute-done | bytes 213024 | tf_op jit(solution)/shard_map/ppermute | solution.py:624
  23.1 2.0 %outer.1 = bf16[4,24,32,256]{3,2,1,0:T(8,128)(2,1)} custom-call(bf16[416,256]{1,0:T(8,128)(2,1)S(1)} %collective-permute-done.4.got, f32[4,256]{1,0:T(4,128)S(1)} %collective-permute-done.5.moved, bf16[2,3,26,32,256]{4,3,2,1,0:T(8,128)(2,1)S(1)} %get-tuple-element.43.taps, ...), custom_call_target="tpu_custom_call", output_to_operand_aliasing={{}: (12, {})} | custom-call | flops 1024 | bytes 1024 | tf_op jit(solution)/shard_map/outer/pallas_call | solution.py:653
  (8 shorter events, 0.1 us)
Async XLA Ops:
  0.0 1.4 %copy-start = (bf16[4,24,32,256]{3,2,1,0:T(8,128)(2,1)S(1)}, bf16[4,24,32,256]{3,2,1,0:T(8,128)(2,1)}, u32[]{:S(2)}) copy-start(bf16[4,24,32,256]{3,2,1,0:T(8,128)(2,1)} %video.9) | copy-start | bytes 4718596
  1.5 10.8 %copy-start.6 = (f32[256]{0:T(256)S(1)}, f32[256]{0:T(256)}, u32[]{:S(2)}) copy-start(f32[256]{0:T(256)} %param.8) | copy-start | bytes 3076
  1.5 13.1 %collective-permute-start.6 = (bf16[26,32,256]{2,1,0:T(8,128)(2,1)S(1)}, bf16[26,32,256]{2,1,0:T(8,128)(2,1)S(1)}, u32[]{:S(2)}, u32[]{:S(2)}) collective-permute-start(bf16[26,32,256]{2,1,0:T(8,128)(2,1)S(1)} %get-tuple-element.27.early), channel_id=1, source_target_pairs={{0,1},{1,2},{2,3},{3,0},{4,5},{5,6},{6,7},{7,4},{8,9},{9,10},{10,1... | collective-permute-start | bytes 1277960 | tf_op jit(solution)/shard_map/ppermute | solution.py:590
  3.8 9.0 %copy-start.1 = (bf16[4,24,32,256]{3,2,1,0:T(8,128)(2,1)S(1)}, bf16[4,24,32,256]{3,2,1,0:T(8,128)(2,1)}, u32[]{:S(2)}) copy-start(bf16[4,24,32,256]{3,2,1,0:T(8,128)(2,1)} %video.9) | copy-start | bytes 4718596
  3.9 1.3 %collective-permute-start = (bf16[160,256]{1,0:T(8,128)(2,1)S(1)}, bf16[160,256]{1,0:T(8,128)(2,1)S(1)}, u32[]{:S(2)}, u32[]{:S(2)}) collective-permute-start(bf16[160,256]{1,0:T(8,128)(2,1)S(1)} %get-tuple-element.29), channel_id=1, source_target_pairs={{0,8},{8,0},{16,24},{24,16},{1,9},{9,1},{17,25},{25,17},{2,10},{10... | collective-permute-start | bytes 245768 | tf_op jit(solution)/shard_map/ppermute | solution.py:591
  5.2 9.4 %copy-start.2 = (bf16[3,3,256,256]{3,2,1,0:T(8,128)(2,1)S(1)}, bf16[3,3,256,256]{3,2,1,0:T(8,128)(2,1)}, u32[]{:S(2)}) copy-start(bf16[3,3,256,256]{3,2,1,0:T(8,128)(2,1)} %param.10) | copy-start | bytes 3538948
  5.2 9.4 %copy-start.3 = (bf16[3,256,256]{2,1,0:T(8,128)(2,1)S(1)}, bf16[3,256,256]{2,1,0:T(8,128)(2,1)}, u32[]{:S(2)}) copy-start(bf16[3,256,256]{2,1,0:T(8,128)(2,1)} %param.12) | copy-start | bytes 1179652
  5.2 9.4 %copy-start.4 = (f32[256]{0:T(256)S(1)}, f32[256]{0:T(256)}, u32[]{:S(2)}) copy-start(f32[256]{0:T(256)} %param.9) | copy-start | bytes 3076
  5.2 9.4 %copy-start.5 = (f32[256]{0:T(256)S(1)}, f32[256]{0:T(256)}, u32[]{:S(2)}) copy-start(f32[256]{0:T(256)} %param.11) | copy-start | bytes 3076
  5.2 9.4 %copy-start.7 = (f32[256]{0:T(256)S(1)}, f32[256]{0:T(256)}, u32[]{:S(2)}) copy-start(f32[256]{0:T(256)} %param.13) | copy-start | bytes 3076
  5.3 7.0 %collective-permute-start.1 = (bf16[160,256]{1,0:T(8,128)(2,1)S(1)}, bf16[160,256]{1,0:T(8,128)(2,1)S(1)}, u32[]{:S(2)}, u32[]{:S(2)}) collective-permute-start(bf16[160,256]{1,0:T(8,128)(2,1)S(1)} %get-tuple-element.33), channel_id=1, source_target_pairs={{0,24},{8,16},{16,8},{24,0},{1,25},{9,17},{17,9},{25,1},{2,26},{10... | collective-permute-start | bytes 245768 | tf_op jit(solution)/shard_map/ppermute | solution.py:604
  6.6 5.7 %collective-permute-start.2 = (bf16[160,256]{1,0:T(8,128)(2,1)S(1)}, bf16[160,256]{1,0:T(8,128)(2,1)S(1)}, u32[]{:S(2)}, u32[]{:S(2)}) collective-permute-start(bf16[160,256]{1,0:T(8,128)(2,1)S(1)} %get-tuple-element.34), channel_id=1, source_target_pairs={{0,4},{4,0},{1,5},{5,1},{2,6},{6,2},{3,7},{7,3},{8,12},{12,8},{9,1... | collective-permute-start | bytes 245768 | tf_op jit(solution)/shard_map/ppermute | solution.py:605
  8.1 4.2 %collective-permute-start.3 = (bf16[48,256]{1,0:T(8,128)(2,1)S(1)}, bf16[48,256]{1,0:T(8,128)(2,1)S(1)}, u32[]{:S(2)}, u32[]{:S(2)}) collective-permute-start(bf16[48,256]{1,0:T(8,128)(2,1)S(1)} %get-tuple-element.35), channel_id=1, source_target_pairs={{0,28},{4,24},{8,20},{12,16},{16,12},{20,8},{24,4},{28,0},{1,29},{... | collective-permute-start | bytes 73736 | tf_op jit(solution)/shard_map/ppermute | solution.py:606
  8.3 12.1 %collective-permute-start.7 = (bf16[15,32,256]{2,1,0:T(8,128)(2,1)S(1)}, bf16[15,32,256]{2,1,0:T(8,128)(2,1)S(1)}, u32[]{:S(2)}, u32[]{:S(2)}) collective-permute-start(bf16[15,32,256]{2,1,0:T(8,128)(2,1)S(1)} %get-tuple-element.39), channel_id=1, source_target_pairs={{0,1},{1,2},{2,3},{4,5},{5,6},{6,7},{8,9},{9,10},{10,11},{12,13},{... | collective-permute-start | bytes 737288 | tf_op jit(solution)/shard_map/ppermute | solution.py:607
  12.6 7.7 %collective-permute-start.5 = (f32[4,256]{1,0:T(4,128)S(1)}, f32[4,256]{1,0:T(4,128)S(1)}, u32[]{:S(2)}, u32[]{:S(2)}) collective-permute-start(f32[4,256]{1,0:T(4,128)S(1)} %get-tuple-element.38), channel_id=1, source_target_pairs={{0,1},{1,2},{2,3},{3,0},{4,5},{5,6},{6,7},{7,4},{8,9},{9,10},{10,1... | collective-permute-start | bytes 12296 | tf_op jit(solution)/shard_map/ppermute | solution.py:617
  12.9 10.2 %collective-permute-start.4 = (bf16[416,256]{1,0:T(8,128)(2,1)S(1)}, bf16[416,256]{1,0:T(8,128)(2,1)S(1)}, u32[]{:S(2)}, u32[]{:S(2)}) collective-permute-start(bf16[416,256]{1,0:T(8,128)(2,1)S(1)} %get-tuple-element.37), channel_id=1, source_target_pairs={{0,1},{1,2},{2,3},{3,0},{4,5},{5,6},{6,7},{7,4},{8,9},{9,10},{10,1... | collective-permute-start | bytes 638984 | tf_op jit(solution)/shard_map/ppermute | solution.py:624
